TPU v7x, 128 devices: a whole 4x4x4 slice. The times are simulated.
128 devices in a mesh: lat: 8 (over z, core), lonr: 16 (over x, y).
Axes of the slice: x: 4, y: 4, z: 4, core: 2. Of those that a mesh axis runs over, the one named last changes fastest.
Arguments:
- entropy: float32 [40, 1024, 2048], P(None, 'lat', 'lonr'), may hold values from 5 to 6
- zonal_flux: float32 [40, 1024, 2048], P(None, 'lat', 'lonr'), may hold values from 1.5 to 3.5
- meridional_flux: float32 [40, 1024, 2048], P(None, 'lat', 'lonr'), may hold values from -0.6 to 0.6
- start_entropy: float32 [40, 1024, 2048], P(None, 'lat', 'lonr'), may hold values from -6 to 6
- start_pressure: float32 [40, 1024, 2048], P(None, 'lat', 'lonr'), may hold values from -6 to 6
- order_slot: int32 [768], replicated, may hold values from 0 to 767, as said below
Outputs:
- new_entropy: float32 [40, 1024, 2048], P(None, 'lat', 'lonr')
- new_pressure: float32 [40, 1024, 2048], P(None, 'lat', 'lonr')
- spectrum: float32 [768, 64, 2, 768], P(('lat', 'lonr'))
Inputs may be any that keep to these rules, and one draw needn't show every extreme that they name: order_slot is a permutation of the orders; slots 2k and 2k + 1 hold two orders whose sum is 767.
All inputs are finite; a program needn't handle non-finite values.
Results may differ from a plain program's by a relative error of at most 0.0058.
Values may be sent and summed in bfloat16 or wider, within the bound.
No kernel may reach another device: no remote copies, remote signals or barrier semaphores. Data moves between devices by JAX's collectives and lax.ppermute only.
A program may use at most 192 MiB of HBM per device.

v0:
```python
import math

import jax
import jax.numpy as jnp
from jax import lax
from jax.sharding import PartitionSpec as P

FLEV = 32


section_weight = 0.5
sound_factor = 0.3
gamma_three_halves = 0.5 * math.log(math.pi) - math.log(2.0)


def with_halo(cells, sides, width, closed):
    for axis, dim in sides:
        count = lax.axis_size(axis)
        ends = count if closed else count - 1
        head = lax.slice_in_dim(cells, 0, width, axis=dim)
        tail = lax.slice_in_dim(cells, cells.shape[dim] - width, cells.shape[dim], axis=dim)
        cells = jnp.concatenate(
            [
                lax.ppermute(tail, axis, [(i, (i + 1) % count) for i in range(ends)]),
                cells,
                lax.ppermute(head, axis, [((i + 1) % count, i) for i in range(ends)]),
            ],
            axis=dim,
        )
    return cells


def interp_faces(extended, axis_index, cell_count):

    def shifted(offset):
        return lax.slice_in_dim(extended, offset, offset + cell_count + 1, axis=axis_index)

    return (
        37.0 * (shifted(2) + shifted(3))
        - 8.0 * (shifted(1) + shifted(4))
        + (shifted(0) + shifted(5))
    ) / 60.0


def face_sines(first_row, cell_count, total_lat):
    global_row = first_row - 1 + jnp.arange(cell_count + 1, dtype=jnp.int32)
    inside = (global_row >= 0) & (global_row < total_lat - 1)
    return jnp.where(
        inside, jnp.sin(math.pi * (global_row + 1).astype(jnp.float32) / total_lat), 0.0
    )


def cell_sines(first_row, cell_count, total_lat):
    global_row = first_row + jnp.arange(cell_count, dtype=jnp.int32)
    return jnp.sin(math.pi * (global_row.astype(jnp.float32) + 0.5) / total_lat)


def tendencies(lat_ent, lat_mer, lon_ent, lon_zon, first_row, total_lat):
    row_count = lat_ent.shape[1] - 6
    col_count = lon_ent.shape[2] - 6
    face_sine = face_sines(first_row, row_count, total_lat)[None, :, None]
    cell_sine = cell_sines(first_row, row_count, total_lat)[None, :, None]
    mer_faces = lat_mer[:, 2 : row_count + 3, :] * face_sine
    merid_term = mer_faces * interp_faces(lat_ent, 1, row_count)
    zon_faces = lon_zon[:, :, 2 : col_count + 3]
    zonal_term = zon_faces * interp_faces(lon_ent, 2, col_count)
    ent_tend = -(
        zonal_term[:, :, 1:]
        - zonal_term[:, :, :-1]
        + (merid_term[:, 1:] - merid_term[:, :-1]) / cell_sine
    )
    pres_tend = -sound_factor * (
        zon_faces[:, :, 1:]
        - zon_faces[:, :, :-1]
        + (mer_faces[:, 1:] - mer_faces[:, :-1]) / cell_sine
    )
    return (ent_tend, pres_tend)


def fourier_tables(order_slot, lon_count):
    longitude = jnp.arange(lon_count, dtype=jnp.int32)
    product = order_slot[None, :] * longitude[:, None] % lon_count
    angles = 2.0 * math.pi / lon_count * product.astype(jnp.float32)
    stacked = jnp.stack((jnp.cos(angles), jnp.sin(angles)), axis=2)
    scales = jnp.where(order_slot == 0, 1.0, 2.0) / lon_count
    forward_table = stacked.reshape(lon_count, -1).astype(jnp.bfloat16)
    inverse_table = (stacked * scales[None, :, None]).reshape(lon_count, -1).T.astype(jnp.bfloat16)
    return (forward_table, inverse_table)


def legendre_tables(orders, total_lat, degree_count):
    colatitude = math.pi * (jnp.arange(total_lat, dtype=jnp.float32) + 0.5) / total_lat
    cosine = jnp.cos(colatitude)[None, :]
    sine_row = jnp.sin(colatitude)
    weights = (sine_row * (math.pi / total_lat))[None, :]
    order_f = orders.astype(jnp.float32)[:, None]
    log_start = (
        -0.5 * math.log(2.0)
        + 0.5 * (lax.lgamma(order_f + 1.5) - gamma_three_halves - lax.lgamma(order_f + 1.0))
        + order_f * jnp.log(sine_row)[None, :]
    )

    def block_step(state_in, block_index):
        prev_vals, curr_vals, log_scale = state_in
        analysis_rows = []
        synthesis_rows = []
        for inner_step in range(16):
            degree = block_index * 16 + inner_step
            deg_f = degree.astype(jnp.float32)
            started = orders[:, None] == degree
            running = orders[:, None] < degree
            denom_a = jnp.maximum(deg_f * deg_f - order_f * order_f, 1.0)
            coef_a = jnp.where(
                running, jnp.sqrt(jnp.maximum(4.0 * deg_f * deg_f - 1.0, 0.0) / denom_a), 0.0
            )
            numer_b = jnp.maximum((deg_f - 1.0) * (deg_f - 1.0) - order_f * order_f, 0.0)
            denom_b = jnp.maximum(4.0 * (deg_f - 1.0) * (deg_f - 1.0) - 1.0, 1.0)
            coef_b = coef_a * jnp.sqrt(numer_b / denom_b)
            new_vals = jnp.where(started, 1.0, coef_a * cosine * curr_vals - coef_b * prev_vals)
            log_scale = jnp.where(started, log_start, log_scale)
            values = new_vals * jnp.exp(log_scale)
            analysis_rows.append((values * weights).astype(jnp.bfloat16))
            synthesis_rows.append(values.astype(jnp.bfloat16))
            biggest = jnp.maximum(jnp.abs(curr_vals), jnp.abs(new_vals))
            factor = jnp.where(biggest > 1.0, biggest, 1.0)
            prev_vals = curr_vals / factor
            curr_vals = new_vals / factor
            log_scale = log_scale + jnp.log(factor)
        return (
            (prev_vals, curr_vals, log_scale),
            (jnp.stack(analysis_rows, axis=1), jnp.stack(synthesis_rows, axis=1)),
        )

    initial = jnp.zeros((orders.shape[0], total_lat), jnp.float32)
    block_ids = jnp.arange(degree_count // 16, dtype=jnp.int32)
    ignored, tables = lax.scan(block_step, (initial, initial, initial), block_ids)
    return (tables[0], tables[1])


def legendre_filter(spectral, order_slot):
    item_count = spectral.shape[0]
    slot_count = spectral.shape[1] // 2
    total_lat = spectral.shape[2]
    degree_count = order_slot.shape[0]
    degree_blocks = degree_count // 16
    block_id = lax.axis_index("lat") * lax.axis_size("lonr") + lax.axis_index("lonr")
    my_orders = lax.dynamic_slice_in_dim(order_slot, block_id * slot_count, slot_count)
    analysis, synthesis = legendre_tables(my_orders, total_lat, degree_count)
    grouped = spectral.reshape(item_count, slot_count, 2, total_lat)
    spectrum = jnp.einsum("bolj,iorj->oirbl", analysis, grouped, preferred_element_type=jnp.float32)
    rounded = spectrum.astype(jnp.bfloat16)
    returned = jnp.einsum(
        "oirbl,bolj->iorj", rounded, synthesis, preferred_element_type=jnp.float32
    )
    returned = returned.astype(jnp.bfloat16).reshape(item_count, 2 * slot_count, total_lat)
    spectrum = spectrum.reshape(slot_count, item_count, 2, degree_blocks * 16)
    return (spectrum, returned)


def per_device(entropy, zonal_flux, meridional_flux, start_entropy, start_pressure, order_slot):
    row_count = entropy.shape[1]
    col_count = entropy.shape[2]
    first_row = lax.axis_index("lat") * row_count
    total_lat = row_count * lax.axis_size("lat")
    lat_ext = with_halo(jnp.stack((entropy, meridional_flux)), (("lat", 2),), 3, False)
    lon_ext = with_halo(jnp.stack((entropy, zonal_flux)), (("lonr", 3),), 3, True)
    ent_tend, pres_tend = tendencies(
        lat_ext[0], lat_ext[1], lon_ext[0], lon_ext[1], first_row, total_lat
    )
    item_grid = jnp.concatenate((ent_tend[:FLEV], pres_tend[:FLEV])).astype(jnp.bfloat16)
    forward_table, inverse_table = fourier_tables(order_slot, col_count * lax.axis_size("lonr"))
    spectral = jnp.einsum(
        "ajk,kc->acj",
        lax.all_to_all(item_grid, "lonr", split_axis=0, concat_axis=2, tiled=True),
        forward_table,
        preferred_element_type=jnp.float32,
    ).astype(jnp.bfloat16)
    spectral = lax.all_to_all(spectral, "lat", split_axis=1, concat_axis=2, tiled=True)
    spectral = lax.all_to_all(spectral, "lonr", split_axis=1, concat_axis=0, tiled=True)
    spectrum, returned = legendre_filter(spectral, order_slot)
    returned = lax.all_to_all(returned, "lonr", split_axis=0, concat_axis=1, tiled=True)
    returned = lax.all_to_all(returned, "lat", split_axis=2, concat_axis=1, tiled=True)
    filt_grid = lax.all_to_all(
        jnp.einsum(
            "acj,ck->ajk", returned, inverse_table, preferred_element_type=jnp.float32
        ).astype(jnp.bfloat16),
        "lonr",
        split_axis=2,
        concat_axis=0,
        tiled=True,
    )
    filt_grid = filt_grid.astype(jnp.float32)
    ent_total = jnp.concatenate((filt_grid[:FLEV], ent_tend[FLEV:]))
    pres_total = jnp.concatenate((filt_grid[FLEV:], pres_tend[FLEV:]))
    new_entropy = start_entropy + section_weight * ent_total
    new_pressure = start_pressure + section_weight * pres_total
    return (new_entropy, new_pressure, spectrum)


def solution(mesh):
    return jax.shard_map(
        per_device,
        mesh=mesh,
        in_specs=(
            P(None, "lat", "lonr"),
            P(None, "lat", "lonr"),
            P(None, "lat", "lonr"),
            P(None, "lat", "lonr"),
            P(None, "lat", "lonr"),
            P(),
        ),
        out_specs=(
            P(None, "lat", "lonr"),
            P(None, "lat", "lonr"),
            P(("lat", "lonr"), None, None, None),
        ),
        check_vma=False,
    )
```

profile of v0, /device:TPU:0, one launch (start us, length us, event | category | flops | bytes accessed | tf_op | source)
XLA Modules:
  0.0 640.6 jit_solution(14375845920319192787)
XLA Ops:
  0.6 2.6 copy.131
  3.2 3.4 copy.133
  6.6 7.6 %fusion.56 = (f32[2,40,3,128]{2,1,3,0:T(8,128)}, f32[2,40,3,128]{2,1,3,0:T(8,128)}) fusion(f32[1,40,128,128]{2,1,3,0:T(8,128)S(1)} %bitcast.307, f32[1,40,128,128]{2,1,3,0:T(8,128)} %bitcast.345), kind=kLoop, calls=%fused_computation.213 | loop fusion | flops 61440 | bytes 5488640 | tf_op jit(solution)/shard_map/stack | solution.py:165
  14.2 3.3 copy.135
  17.5 1.3 collective-permute-start.3
  18.8 3.3 copy.134
  22.1 3.7 collective-permute-start.2
  25.8 3.4 copy.132
  30.0 5.4 collective-permute-start.1
  35.7 3.1 copy.137
  38.8 3.9 copy.136
  42.8 12.6 %pad_maximum_fusion.1 = f32[2,40,134,128]{2,1,3,0:T(8,128)} fusion(f32[2,40,3,128]{2,1,3,0:T(8,128)} %copy.137, f32[1,40,128,128]{2,1,3,0:T(8,128)} %bitcast.346, f32[1,40,128,128]{2,1,3,0:T(8,128)S(1)} %bitcast.309, f32[2,40,3,128]{2,1,3,0:T(8,128)} %copy.136), kind=kLoop, calls=%fused_computation.193 | loop fusion | flops 4116480 | bytes 10977280 | tf_op jit(solution)/shard_map/concatenate | solution.py:22
  55.4 7.1 %slice_bitcast_fusion.1 = (f32[40,134,128]{1,0,2:T(8,128)}, f32[40,134,128]{1,0,2:T(8,128)S(1)}) fusion(f32[2,40,134,128]{2,1,3,0:T(8,128)} %pad_maximum_fusion.1), kind=kLoop, calls=%fused_computation.225 | loop fusion | bytes 10977280 | tf_op jit(solution)/shard_map/squeeze | solution.py:168
  62.6 1.1 pad_maximum_fusion.2
  64.0 2.7 fusion.71
  66.7 12.5 %fusion.59 = (f32[40,129,128]{1,0,2:T(8,128)}, f32[40,129,128]{1,0,2:T(8,128)}) fusion(f32[40,134,128]{1,0,2:T(8,128)S(1)} %get-tuple-element.651, f32[129]{0:T(256)S(1)} %and_select_fusion, f32[40,134,128]{1,0,2:T(8,128)} %get-tuple-element.650), kind=kLoop, calls=%fused_computation.217 | loop fusion | flops 6604800 | bytes 23777796 | tf_op jit(solution)/shard_map/mul | solution.py:64
  79.2 8.1 %fusion.77 = (f32[40,128,128]{1,0,2:T(8,128)S(1)}, f32[40,128,128]{1,0,2:T(8,128)S(1)}) fusion(f32[40,129,128]{1,0,2:T(8,128)} %get-tuple-element.593, f32[40,128,134]{1,0,2:T(8,128)S(1)} %get-tuple-element.652, f32[128]{0:T(128)S(1)} %multiply_sine_fusion, f32[40,129,128]{1,0,2:T(8,128)} %get-tuple-element.592, f32[40,128,129]{1,0,2:T(8,128)} %fusion.71), kind=kLoop, calls=%fused_computation.249 | loop fusion | flops 6553600 | bytes 26214912 | tf_op jit(solution)/shard_map/mul | solution.py:72
  89.6 2.7 copy.138
  92.3 7.2 %all-to-all-start = ((bf16[64,128,128]{1,2,0:T(8,128)(2,1)}), bf16[64,128,128]{1,2,0:T(8,128)(2,1)}, u32[]{:S(2)}, u32[]{:S(2)}) async-start(bf16[64,128,128]{1,2,0:T(8,128)(2,1)} %copy.138), calls=%async_computation | async-start | bytes 4194304 | tf_op jit(solution)/shard_map/all_to_all | solution.py:174
  99.5 25.7 %fusion.64 = (f32[2048,768,1]{1,0,2:T(8,128)S(1)}, f32[2048,768,1]{1,0,2:T(8,128)}) fusion(s32[768]{0:T(1024)S(1)} %copy-done.5), kind=kLoop, calls=%fused_computation.231 | loop fusion | flops 22020096 | bytes 12585984 | tf_op jit(solution)/shard_map/cos | solution.py:84
  125.2 2.8 copy-done
  127.9 6.4 %fusion.96 = bf16[2048,768,2]{1,0,2:T(8,128)(2,1)} fusion(f32[2048,768,1]{1,0,2:T(8,128)} %get-tuple-element.661, f32[2048,768,1]{1,0,2:T(8,128)S(1)} %get-tuple-element.660), kind=kLoop, calls=%fused_computation.308 | loop fusion | flops 3145728 | bytes 18874368 | tf_op jit(solution)/shard_map/convert_element_type | solution.py:86
  134.4 16.4 %copy.130 = bf16[2048,768,2]{0,2,1:T(2,128)(2,1)} copy(bf16[2048,768,2]{1,0,2:T(8,128)(2,1)} %fusion.96) | data formatting | bytes 12582912 | tf_op jit(solution)/shard_map/convert_element_type | solution.py:86
  150.7 10.2 %reshape.1275 = bf16[2048,1536,1]{0,1,2:T(8,128)(2,1)} reshape(bf16[2048,768,2]{0,2,1:T(2,128)(2,1)} %copy.130) | data formatting | bytes 12582912 | tf_op jit(solution)/shard_map/convert_element_type | solution.py:86
  161.0 3.5 copy.139
  164.4 2.3 all_to_all.73
  166.7 6.2 fusion.68
  172.9 8.2 %copy.140 = bf16[4,1536,128]{2,0,1:T(4,128)(2,1)} copy(bf16[4,1536,128]{2,1,0:T(8,128)(2,1)S(1)} %fusion.68) | data formatting | bytes 3145728 | tf_op jit(solution)/shard_map/convert_element_type | solution.py:177
  181.1 4.9 all-to-all-start.1
  186.3 21.2 %all-to-all-done.1 = bf16[4,1536,128]{2,0,1:T(4,128)(2,1)S(1)} async-done(((bf16[4,1536,128]{2,0,1:T(4,128)(2,1)}), bf16[4,1536,128]{2,0,1:T(4,128)(2,1)S(1)}, u32[]{:S(2)}, u32[]{:S(2)}) %all-to-all-start.1) | async-done | bytes 1572896 | tf_op jit(solution)/shard_map/all_to_all | solution.py:178
  207.5 2.2 copy.184
  209.7 2.5 all_to_all.77
  212.2 2.4 copy.142
  214.6 7.3 %all-to-all-start.2 = ((bf16[4,192,1024]{2,0,1:T(4,128)(2,1)}), bf16[4,192,1024]{2,0,1:T(4,128)(2,1)S(1)}, u32[]{:S(2)}, u32[]{:S(2)}) async-start(bf16[4,192,1024]{2,0,1:T(4,128)(2,1)} %copy.142), calls=%async_computation.2 | async-start | bytes 3145728 | tf_op jit(solution)/shard_map/all_to_all | solution.py:179
  221.9 227.8 %while.23 = (s32[]{:T(128)}, f32[6,1024]{1,0:T(8,128)S(1)}, f32[6,1024]{1,0:T(8,128)S(1)}, f32[6,1024]{1,0:T(8,128)S(1)}, bf16[48,6,16,1024]{3,1,2,0:T(8,128)(2,...) while((s32[]{:T(128)}, f32[6,1024]{1,0:T(8,128)S(1)}, ...), condition=%wide.region_1.2_spmd.clone.clone, body=%wide.region_0.1_spmd.clone.clone.sunk | while | flops 2758801 | bytes 5348160 | solution.py:136
  363.2 0.9 bitcast_dynamic-update-slice_fusion.3
  377.6 0.9 bitcast_dynamic-update-slice_fusion.3
  434.6 0.9 bitcast_dynamic-update-slice_fusion.3
  449.7 1.9 copy.143
  451.6 2.4 reshape.1276
  453.9 12.9 %fusion.42 = f32[6,64,2,48,16]{1,3,4,2,0:T(8,128)} fusion(bf16[48,6,16,1024,1]{3,1,2,0,4:T(8,128)(2,1)} %bitcast.361, bf16[64,6,2,1024,1]{3,0,2,1,4:T(8,128)(2,1)S(1)} %reshape.1276), kind=kOutput, calls=%fused_computation.197 | convolution fusion | flops 1207959552 | bytes 13369344 | tf_op jit(solution)/shard_map/bolj,iorj->oirbl/dot_general | solution.py:150
  466.8 16.8 %bitcast_convert_fusion = bf16[6,1024,64,2]{1,2,3,0:T(8,128)(2,1)S(1)} fusion(f32[6,64,2,48,16]{1,3,4,2,0:T(8,128)} %fusion.42, bf16[48,6,16,1024,1]{3,1,2,0,4:T(8,128)(2,1)} %bitcast.355), kind=kOutput, calls=%fused_computation.229 | convolution fusion | flops 1209335808 | bytes 13369344 | tf_op jit(solution)/shard_map/oirbl,bolj->iorj/dot_general | solution.py:152
  484.5 34.7 %all_to_all.96 = bf16[64,12,1024]{2,1,0:T(8,128)(2,1)S(1)} all-to-all(bf16[64,12,1024]{2,1,0:T(8,128)(2,1)S(1)} %copy.146), channel_id=1, replica_groups=mesh['lat'=8,'lonr'=16] {'lonr'}, dimensions={0} | all-to-all | bytes 3145728 | tf_op jit(solution)/shard_map/all_to_all | solution.py:181
  519.2 1.3 copy.173
  520.6 3.5 copy.149
  524.1 3.6 all-to-all-start.4
  527.7 10.0 %pad_maximum_fusion = f32[2048,768,2]{1,0,2:T(8,128)} fusion(f32[2048,768,1]{1,0,2:T(8,128)} %get-tuple-element.661, f32[2048,768,1]{1,0,2:T(8,128)} %copy-done), kind=kLoop, calls=%fused_computation.191 | loop fusion | flops 3145728 | bytes 25165824 | tf_op jit(solution)/shard_map/stack | solution.py:84
  537.7 19.4 %copy.152 = f32[2048,768,2]{0,2,1:T(2,128)} copy(f32[2048,768,2]{1,0,2:T(8,128)} %pad_maximum_fusion) | data formatting | bytes 25165824 | tf_op jit(solution)/shard_map/stack | solution.py:84
  557.1 15.8 %stack.267 = f32[2048,1536]{0,1:T(8,128)} reshape(f32[2048,768,2]{0,2,1:T(2,128)} %copy.152) | data formatting | bytes 25165824 | tf_op jit(solution)/shard_map/stack | solution.py:84
  573.3 1.3 copy-done.2
  574.6 3.1 copy.175
  577.7 9.3 %fusion.65 = bf16[4,128,2048]{2,1,0:T(8,128)(2,1)} fusion(bf16[4,1536,128]{2,1,0:T(8,128)(2,1)S(1)} %bitcast.348, f32[2048,1536]{0,1:T(8,128)} %stack.267, f32[1536]{0:T(1024)S(1)} %mul.2352), kind=kOutput, calls=%fused_computation.233 | convolution fusion | flops 3228565504 | bytes 16259072 | tf_op jit(solution)/shard_map/acj,ck->ajk/dot_general | solution.py:184
  587.0 4.2 copy.155
  591.3 3.7 all-to-all-start.5
  595.0 1.1 slice.189
  596.1 1.9 slice.191
  598.2 1.2 copy.159
  599.4 5.9 copy.160
  605.4 6.0 copy.161
  611.3 14.4 %all-to-all-done.5 = bf16[4,128,2048]{1,0,2:T(4,128)(2,1)S(1)} async-done(((bf16[4,128,2048]{1,0,2:T(4,128)(2,1)}), bf16[4,128,2048]{1,0,2:T(4,128)(2,1)S(1)}, u32[]{:S(2)}, u32[]{:S(2)}) %all-to-all-start.5) | async-done | bytes 2097184 | tf_op jit(solution)/shard_map/all_to_all | solution.py:183
  626.1 2.4 fusion.111
  628.5 1.9 copy.156
  630.4 2.9 copy.158
  633.3 6.8 %fusion.81 = (f32[40,128,128]{2,1,0:T(8,128)}, f32[40,128,128]{2,1,0:T(8,128)}) fusion(f32[40,128,128]{2,1,0:T(8,128)} %param.11, f32[8,128,128]{2,1,0:T(8,128)S(1)} %copy.157, f32[32,128,128]{2,1,0:T(8,128)S(1)} %bitcast.350, f32[40,128,128]{2,1,0:T(8,128)} %param.12, f32[8,128,128]{2,1,0:T(8,128)S(1)} %copy.159, f32[32,128,128]{2,1,0:T(8,128)} %bitcast.351), kind=kLoop, calls=%fused_computation.257 | loop fusion | flops 3932160 | bytes 15728640 | tf_op jit(solution)/shard_map/add | solution.py:195
  (1430 shorter events, 180.4 us)
Async XLA Ops:
  17.5 18.2 %collective-permute-start.3 = (f32[2,40,3,128]{3,1,2,0:T(8,128)S(1)}, f32[2,40,3,128]{3,1,2,0:T(8,128)S(1)}, u32[]{:S(2)}, u32[]{:S(2)}) collective-permute-start(f32[2,40,3,128]{3,1,2,0:T(8,128)S(1)} %copy.135), channel_id=1, source_target_pairs={{16,0},{32,16},{48,32},{64,48},{80,64},{96,80},{112,96},{17,1},{33... | collective-permute-start | bytes 368648 | tf_op jit(solution)/shard_map/ppermute | solution.py:26
  22.1 16.7 %collective-permute-start.2 = (f32[2,40,3,128]{3,1,2,0:T(8,128)S(1)}, f32[2,40,3,128]{3,1,2,0:T(8,128)}, u32[]{:S(2)}, u32[]{:S(2)}) collective-permute-start(f32[2,40,3,128]{3,1,2,0:T(8,128)S(1)} %copy.134), channel_id=1, source_target_pairs={{0,16},{16,32},{32,48},{48,64},{64,80},{80,96},{96,112},{1,17},{17... | collective-permute-start | bytes 368648 | tf_op jit(solution)/shard_map/ppermute | solution.py:24
  30.0 32.5 %collective-permute-start.1 = (f32[2,40,128,3]{2,1,3,0:T(8,128)S(1)}, f32[2,40,128,3]{2,1,3,0:T(8,128)S(1)}, u32[]{:S(2)}, u32[]{:S(2)}) collective-permute-start(f32[2,40,128,3]{2,1,3,0:T(8,128)S(1)} %get-tuple-element.655), channel_id=1, source_target_pairs={{1,0},{2,1},{3,2},{4,3},{5,4},{6,5},{7,6},{8,7},{9,8},{10,9},{11,1... | collective-permute-start | bytes 368648 | tf_op jit(solution)/shard_map/ppermute | solution.py:26
  35.4 27.2 %collective-permute-start = (f32[2,40,128,3]{2,1,3,0:T(8,128)S(1)}, f32[2,40,128,3]{2,1,3,0:T(8,128)S(1)}, u32[]{:S(2)}, u32[]{:S(2)}) collective-permute-start(f32[2,40,128,3]{2,1,3,0:T(8,128)S(1)} %get-tuple-element.654), channel_id=1, source_target_pairs={{0,1},{1,2},{2,3},{3,4},{4,5},{5,6},{6,7},{7,8},{8,9},{9,10},{10,1... | collective-permute-start | bytes 368648 | tf_op jit(solution)/shard_map/ppermute | solution.py:24
  55.4 7.2 %copy-start.1 = (f32[40,128,128]{1,0,2:T(8,128)S(1)}, f32[40,128,128]{1,0,2:T(8,128)}, u32[]{:S(2)}) copy-start(f32[40,128,128]{1,0,2:T(8,128)} %copy.132) | copy-start | bytes 7864324
  87.2 1.5 copy-start.3
  87.2 2.3 copy-start.4
  89.6 9.9 %copy-start.5 = (s32[768]{0:T(1024)S(1)}, s32[768]{0:T(1024)}, u32[]{:S(2)}) copy-start(s32[768]{0:T(1024)} %param.13) | copy-start | bytes 9220
  92.3 68.7 %all-to-all-start = ((bf16[64,128,128]{1,2,0:T(8,128)(2,1)}), bf16[64,128,128]{1,2,0:T(8,128)(2,1)}, u32[]{:S(2)}, u32[]{:S(2)}) async-start(bf16[64,128,128]{1,2,0:T(8,128)(2,1)} %copy.138), calls=%async_computation | async-start | bytes 4194304 | tf_op jit(solution)/shard_map/all_to_all | solution.py:174
  125.2 2.8 copy-start
  181.1 26.4 %all-to-all-start.1 = ((bf16[4,1536,128]{2,0,1:T(4,128)(2,1)}), bf16[4,1536,128]{2,0,1:T(4,128)(2,1)S(1)}, u32[]{:S(2)}, u32[]{:S(2)}) async-start(bf16[4,1536,128]{2,0,1:T(4,128)(2,1)} %copy.140), calls=%async_computation.1 | async-start | bytes 3145728 | tf_op jit(solution)/shard_map/all_to_all | solution.py:178
  214.6 235.1 %all-to-all-start.2 = ((bf16[4,192,1024]{2,0,1:T(4,128)(2,1)}), bf16[4,192,1024]{2,0,1:T(4,128)(2,1)S(1)}, u32[]{:S(2)}, u32[]{:S(2)}) async-start(bf16[4,192,1024]{2,0,1:T(4,128)(2,1)} %copy.142), calls=%async_computation.2 | async-start | bytes 3145728 | tf_op jit(solution)/shard_map/all_to_all | solution.py:179
  524.1 49.2 %all-to-all-start.4 = ((bf16[4,192,1024]{1,0,2:T(4,128)(2,1)}), bf16[4,192,1024]{1,0,2:T(4,128)(2,1)S(1)}, u32[]{:S(2)}, u32[]{:S(2)}) async-start(bf16[4,192,1024]{1,0,2:T(4,128)(2,1)} %copy.149), calls=%async_computation.4 | async-start | bytes 4194304 | tf_op jit(solution)/shard_map/all_to_all | solution.py:182
  573.3 1.3 copy-start.2
  591.3 34.5 %all-to-all-start.5 = ((bf16[4,128,2048]{1,0,2:T(4,128)(2,1)}), bf16[4,128,2048]{1,0,2:T(4,128)(2,1)S(1)}, u32[]{:S(2)}, u32[]{:S(2)}) async-start(bf16[4,128,2048]{1,0,2:T(4,128)(2,1)} %copy.155), calls=%async_computation.5 | async-start | bytes 4194304 | tf_op jit(solution)/shard_map/all_to_all | solution.py:183
where the time goes:
time: 648 us; the launch traced here: 641 us
  local copies, waits for them, and re-layouts  236 us (36%)
  other arithmetic  200 us (31%)
  loops' own time  50.6 us (8%)
  matrix products  45.2 us (7%)
  starting transfers between devices  37.3 us (6%)
  waiting for transfers between devices  35.6 us (5%)
  blocking collectives  34.7 us (5%)
    while x720, other arithmetic  75.1 us
    another operation x1, loops' own time, legendre_tables(): lax.scan(block_step, (initial, initial, initial), block_ids)  50.6 us
    dynamic_update_slice x48, local copies, waits for them, and re-layouts, legendre_tables(): lax.scan(block_step, (initial, initial, initial), block_ids)  40.8 us
    another operation x2, local copies, waits for them, and re-layouts, fourier_tables(): stacked = jnp.stack((jnp.cos(angles), jnp.sin(angles)), axis=2)  35.2 us
    all_to_all x1, blocking collectives, per_device(): lax.all_to_all(returned, 'lonr', split_axis=0, concat_axis=1, tiled=True)  34.7 us
    dynamic_slice x48, local copies, waits for them, and re-layouts, legendre_tables(): lax.scan(block_step, (initial, initial, initial), block_ids)  31.8 us
    convert_element_type x2, local copies, waits for them, and re-layouts, fourier_tables(): forward_table = stacked.reshape(lon_count, -1).astype(jnp.bfloat16)  26.6 us
    cos x1, other arithmetic, fourier_tables(): stacked = jnp.stack((jnp.cos(angles), jnp.sin(angles)), axis=2)  25.7 us
  transfers between devices with their start and end apart: 9, of which 2 were waited for; matrix products, arithmetic and copies ran while one was open for 52% of the time, Pallas kernels for 0%

commit v1 on v0

v1 whole, which is shorter than its diff:
```python
import math

import jax
import jax.numpy as jnp
from jax import lax
from jax.experimental import pallas as pl
from jax.experimental.pallas import tpu as pltpu
from jax.sharding import PartitionSpec as P

FLEV = 32
LEV = 40
NLAT = 1024
NLON = 2048
ORDERS = 768
PAIRS = ORDERS // 2
ROWS = 128
COLS = 128
F32 = jnp.float32
BF16 = jnp.bfloat16

gamma_three_halves = 0.5 * math.log(math.pi) - math.log(2.0)


def lane_ids(shape):
    return lax.broadcasted_iota(jnp.int32, shape, len(shape) - 1)


def edges_kernel(s_ref, u_ref, v_ref, east_ref, west_ref, south_ref, north_ref):
    lane = lane_ids((8, 128))

    def one_pair(q, carry):
        east = jnp.zeros((8, 128), F32)
        west = jnp.zeros((8, 128), F32)
        for i in range(32):
            s = s_ref[2 * q + i // 16, pl.ds(8 * (i % 16), 8), :]
            u = u_ref[2 * q + i // 16, pl.ds(8 * (i % 16), 8), :]
            s_end = pltpu.roll(s, (4 * i - 125) % 128, 1)
            u_end = pltpu.roll(u, (4 * i + 3 - 127) % 128, 1)
            s_top = pltpu.roll(s, 4 * i, 1) if i else s
            mine = (lane >= 4 * i) & (lane < 4 * i + 3)
            east = jnp.where(mine, s_end, jnp.where(lane == 4 * i + 3, u_end, east))
            west = jnp.where(mine, s_top, west)
        east_ref[q] = east
        west_ref[q] = west
        return carry

    lax.fori_loop(0, 4, one_pair, 0)
    for lev in range(8):
        south_ref[lev, 0:3, :] = s_ref[lev, 125:128, :]
        south_ref[lev, 3:4, :] = v_ref[lev, 7:8, :]
        north_ref[lev] = s_ref[lev, 0:4, :]


def edges(entropy, zonal, merid):
    whole = pl.BlockSpec((8, ROWS, COLS), lambda g: (g, 0, 0))
    return pl.pallas_call(
        edges_kernel,
        grid=(LEV // 8,),
        in_specs=[whole, whole, pl.BlockSpec((8, 8, COLS), lambda g: (g, ROWS // 8 - 1, 0))],
        out_specs=[
            pl.BlockSpec((4, 8, 128), lambda g: (g, 0, 0)),
            pl.BlockSpec((4, 8, 128), lambda g: (g, 0, 0)),
            pl.BlockSpec((8, 4, 128), lambda g: (g, 0, 0)),
            pl.BlockSpec((8, 4, 128), lambda g: (g, 0, 0)),
        ],
        out_shape=[
            jax.ShapeDtypeStruct((LEV // 2, 8, 128), F32),
            jax.ShapeDtypeStruct((LEV // 2, 8, 128), F32),
            jax.ShapeDtypeStruct((LEV, 4, 128), F32),
            jax.ShapeDtypeStruct((LEV, 4, 128), F32),
        ],
        name="edges",
    )(entropy, zonal, merid)


def stencil(x0, x1, x2, x3, x4, x5):
    return (37.0 * (x2 + x3) - 8.0 * (x1 + x4) + (x0 + x5)) * (1.0 / 60.0)


def tend_kernel(
    s_ref, u_ref, v_ref, hw_ref, he_ref, ow_ref, hn_ref, hs_ref, fs_ref, rc_ref,
    item_ref, ent_ref, pres_ref, ext, mext,
):
    step = pl.program_id(0)
    lane = lane_ids((ROWS, COLS))
    last = lane == COLS - 1

    def level(q, half):
        lev = 2 * q + half
        s = s_ref[lev]
        u = u_ref[lev]
        west = hw_ref[q]
        east = he_ref[q]
        own = ow_ref[q]
        edge = stencil(
            pltpu.roll(west, 3, 1), pltpu.roll(west, 2, 1), pltpu.roll(west, 1, 1),
            pltpu.roll(own, 3, 1), pltpu.roll(own, 2, 1), pltpu.roll(own, 1, 1),
        )
        edge = edge * west
        tiles = range(16 * half, 16 * half + 16)
        s_west = jnp.concatenate([pltpu.roll(west, (125 - 4 * i) % 128, 1) for i in tiles])
        u_west = jnp.concatenate([pltpu.roll(west, (124 - 4 * i) % 128, 1) for i in tiles])
        z_west = jnp.concatenate([pltpu.roll(edge, (124 - 4 * i) % 128, 1) for i in tiles])
        s_east = jnp.concatenate([pltpu.roll(east, (128 - 4 * i) % 128, 1) for i in tiles])
        e_face = stencil(
            pltpu.roll(jnp.where(lane >= COLS - 2, s_west, s), 2, 1),
            pltpu.roll(jnp.where(last, s_west, s), 1, 1),
            s,
            pltpu.roll(jnp.where(lane < 1, s_east, s), 127, 1),
            pltpu.roll(jnp.where(lane < 2, s_east, s), 126, 1),
            pltpu.roll(jnp.where(lane < 3, s_east, s), 125, 1),
        )
        z = u * e_face
        dz = z - pltpu.roll(jnp.where(last, z_west, z), 1, 1)
        du = u - pltpu.roll(jnp.where(last, u_west, u), 1, 1)
        ext[5:8, :] = hn_ref[lev, 0:3, :]
        ext[8:136, :] = s
        ext[136:139, :] = hs_ref[lev, 0:3, :]
        n_face = stencil(*[ext[6 + o:134 + o, :] for o in range(6)])
        n_top = stencil(*[ext[5 + o:6 + o, :] for o in range(6)])
        fv = v_ref[lev] * fs_ref[8:136, :]
        fv_top = hn_ref[lev, 3:4, :] * fs_ref[7:8, :]
        m = fv * n_face
        mext[0, 7:8, :] = fv_top * n_top
        mext[0, 8:136, :] = m
        mext[1, 7:8, :] = fv_top
        mext[1, 8:136, :] = fv
        rc = rc_ref[...]
        ent = -(dz + (m - mext[0, 7:135, :]) * rc)
        pres = -0.3 * (du + (fv - mext[1, 7:135, :]) * rc)
        return lev, ent, pres

    @pl.when(step < FLEV // 8)
    def _():
        def body(q, carry):
            for half in range(2):
                lev, ent, pres = level(q, half)
                item_ref[0, lev] = ent.astype(BF16)
                item_ref[1, lev] = pres.astype(BF16)
            return carry

        lax.fori_loop(0, 4, body, 0)

    @pl.when(step == FLEV // 8)
    def _():
        def body(q, carry):
            for half in range(2):
                lev, ent, pres = level(q, half)
                ent_ref[lev] = ent
                pres_ref[lev] = pres
            return carry

        lax.fori_loop(0, 4, body, 0)


def tendencies(s, u, v, from_west, from_east, own_west, from_north, from_south, fs, rc):
    whole = pl.BlockSpec((8, ROWS, COLS), lambda g: (g, 0, 0))
    packed = pl.BlockSpec((4, 8, 128), lambda g: (g, 0, 0))
    rows4 = pl.BlockSpec((8, 4, 128), lambda g: (g, 0, 0))
    tail = pl.BlockSpec((8, ROWS, COLS), lambda g: (0, 0, 0))
    return pl.pallas_call(
        tend_kernel,
        grid=(LEV // 8,),
        in_specs=[
            whole, whole, whole, packed, packed, packed, rows4, rows4,
            pl.BlockSpec((136, 128), lambda g: (0, 0)),
            pl.BlockSpec((128, 128), lambda g: (0, 0)),
        ],
        out_specs=[
            pl.BlockSpec((2, 8, ROWS, COLS), lambda g: (0, jnp.minimum(g, FLEV // 8 - 1), 0, 0)),
            tail, tail,
        ],
        out_shape=[
            jax.ShapeDtypeStruct((2, FLEV, ROWS, COLS), BF16),
            jax.ShapeDtypeStruct((LEV - FLEV, ROWS, COLS), F32),
            jax.ShapeDtypeStruct((LEV - FLEV, ROWS, COLS), F32),
        ],
        scratch_shapes=[pltpu.VMEM((144, 128), F32), pltpu.VMEM((2, 136, 128), F32)],
        name="tendencies",
    )(s, u, v, from_west, from_east, own_west, from_north, from_south, fs, rc)


def table_kernel(base_ref, turn_ref, out_ref):
    for par in range(2):
        c = base_ref[par, 0]
        s = base_ref[par, 1]
        for b in range(8):
            tc = jnp.broadcast_to(turn_ref[par, :, b:b + 1], c.shape)
            ts = jnp.broadcast_to(turn_ref[par, :, 8 + b:9 + b], c.shape)
            out_ref[par, 0, :, 128 * b:128 * b + 128] = (c * tc - s * ts).astype(BF16)
            out_ref[par, 1, :, 128 * b:128 * b + 128] = (s * tc + c * ts).astype(BF16)


def fourier_table(even_odd):
    def angles(steps):
        product = (even_odd[:, :, None] * steps[None, None, :]) % NLON
        return (2.0 * math.pi / NLON) * product.astype(F32)

    near = angles(jnp.arange(128, dtype=jnp.int32))
    far = angles(128 * jnp.arange(8, dtype=jnp.int32))
    base = jnp.stack((jnp.cos(near), jnp.sin(near)), axis=1)
    turn = jnp.concatenate((jnp.cos(far), jnp.sin(far)), axis=2)
    tile = 96
    return pl.pallas_call(
        table_kernel,
        grid=(PAIRS // tile,),
        in_specs=[
            pl.BlockSpec((2, 2, tile, 128), lambda g: (0, 0, g, 0)),
            pl.BlockSpec((2, tile, 16), lambda g: (0, g, 0)),
        ],
        out_specs=pl.BlockSpec((2, 2, tile, NLON // 2), lambda g: (0, 0, g, 0)),
        out_shape=jax.ShapeDtypeStruct((2, 2, PAIRS, NLON // 2), BF16),
        name="longitude_table",
    )(base, turn)


def forward_kernel(x_ref, t_ref, o_ref, fold, rows):
    @pl.when(pl.program_id(0) == 0)
    def _():
        for a in range(4):
            for b in range(8):
                lo = x_ref[b, a].astype(F32)
                hi = x_ref[b + 8, a].astype(F32)
                fold[0, 128 * a:128 * a + 128, 128 * b:128 * b + 128] = (lo + hi).astype(BF16)
                fold[1, 128 * a:128 * a + 128, 128 * b:128 * b + 128] = (lo - hi).astype(BF16)

    tile = t_ref.shape[2]
    for par in range(2):
        for ri in range(2):
            res = lax.dot_general(
                t_ref[par, ri], fold[par], (((1,), (1,)), ((), ())), preferred_element_type=F32
            )
            for a in range(4):
                rows[pl.ds(8 * par + 2 * a + ri, tile, stride=16), :] = res[:, 128 * a:128 * a + 128]
    o_ref[...] = rows[...].reshape(o_ref.shape).astype(BF16)


def forward(x, table):
    tile = 96
    return pl.pallas_call(
        forward_kernel,
        grid=(PAIRS // tile,),
        in_specs=[
            pl.BlockSpec((16, 4, 128, 128), lambda g: (0, 0, 0, 0)),
            pl.BlockSpec((2, 2, tile, NLON // 2), lambda g: (0, 0, g, 0)),
        ],
        out_specs=pl.BlockSpec((tile // 3, 48, 128), lambda g: (g, 0, 0)),
        out_shape=jax.ShapeDtypeStruct((128, 48, 128), BF16),
        scratch_shapes=[
            pltpu.VMEM((2, 512, NLON // 2), BF16),
            pltpu.VMEM((16 * tile, 128), F32),
        ],
        name="forward",
    )(x, table)


CHUNK = 128


def legendre_kernel(a_ref, b_ref, m_ref, cos_ref, start_ref, w_ref, ana_ref, syn_ref, rows, state):
    chunk = pl.program_id(0)
    upper = lax.broadcasted_iota(jnp.int32, (8, 128), 0) < 4

    @pl.when(chunk == 0)
    def _():
        state[...] = jnp.zeros_like(state)

    cosine = [cos_ref[8 * v:8 * v + 8, :] for v in range(3)]
    orders = [m_ref[8 * v:8 * v + 8, :] for v in range(3)]

    def body(it, carry):
        prev, curr, logs, scale = carry
        for k in range(4):
            local = it * 4 + k
            degree = chunk * CHUNK + local
            nxt = []
            new_logs = []
            new_scale = []
            for v in range(3):
                at = degree * 6 + 2 * v
                a = jnp.where(upper, a_ref[at], a_ref[at + 1])
                b = jnp.where(upper, b_ref[at], b_ref[at + 1])
                first = orders[v] == degree
                start = start_ref[8 * v:8 * v + 8, :]
                val = jnp.where(first, 1.0, (a * cosine[v]) * curr[v] - b * prev[v])
                lg = jnp.where(first, start, logs[v])
                sc = jnp.where(first, start_ref[24 + 8 * v:32 + 8 * v, :], scale[v])
                row = pl.multiple_of(local * 24, 8) + 8 * v
                rows[pl.ds(row, 8), :] = val * sc
                nxt.append(val)
                new_logs.append(lg)
                new_scale.append(sc)
            prev, curr, logs, scale = curr, nxt, new_logs, new_scale
        grow = [jnp.maximum(1.0, jnp.maximum(jnp.abs(p), jnp.abs(c))) for p, c in zip(prev, curr)]
        inv = [1.0 / g for g in grow]
        prev = [p * i for p, i in zip(prev, inv)]
        curr = [c * i for c, i in zip(curr, inv)]
        logs = [l + jnp.log(g) for l, g in zip(logs, grow)]
        scale = [jnp.where(s > -1.0, jnp.where(o <= chunk * CHUNK + it * 4 + 3, jnp.exp(l), 0.0), 0.0)
                 for s, l, o in zip(scale, logs, orders)]
        return prev, curr, logs, scale

    init = tuple([state[24 * n + 8 * v:24 * n + 8 * v + 8, :] for v in range(3)] for n in range(4))
    final = lax.fori_loop(0, CHUNK // 4, body, init)
    for n in range(4):
        for v in range(3):
            state[24 * n + 8 * v:24 * n + 8 * v + 8, :] = final[n][v]
    for o in range(6):
        for jb in range(4):
            val = rows[pl.ds(4 * o + jb, CHUNK, stride=24), :]
            syn_ref[o, :, 128 * jb:128 * jb + 128] = val.astype(BF16)
            ana_ref[o, :, 128 * jb:128 * jb + 128] = (val * w_ref[jb:jb + 1, :]).astype(BF16)


def legendre_tables(orders):
    half = NLAT // 2
    colatitude = math.pi * (jnp.arange(half, dtype=F32) + 0.5) / NLAT
    sine = jnp.sin(colatitude)
    order_f = orders.astype(F32)
    log_start = (
        -0.5 * math.log(2.0)
        + 0.5 * (lax.lgamma(order_f + 1.5) - gamma_three_halves - lax.lgamma(order_f + 1.0))
    )[:, None] + order_f[:, None] * jnp.log(sine)[None, :]
    log_start = log_start.reshape(24, 128)
    start = jnp.concatenate((log_start, jnp.exp(log_start)))
    cosine = jnp.tile(jnp.cos(colatitude).reshape(4, 128), (6, 1))
    weight = (sine * (math.pi / NLAT)).reshape(4, 128)
    deg = jnp.arange(ORDERS, dtype=F32)[:, None]
    running = orders[None, :] < jnp.arange(ORDERS, dtype=jnp.int32)[:, None]
    denom_a = jnp.maximum(deg * deg - order_f * order_f, 1.0)
    coef_a = jnp.where(running, jnp.sqrt(jnp.maximum(4.0 * deg * deg - 1.0, 0.0) / denom_a), 0.0)
    numer_b = jnp.maximum((deg - 1.0) * (deg - 1.0) - order_f * order_f, 0.0)
    denom_b = jnp.maximum(4.0 * (deg - 1.0) * (deg - 1.0) - 1.0, 1.0)
    coef_b = coef_a * jnp.sqrt(numer_b / denom_b)
    order_rows = jnp.broadcast_to(jnp.repeat(orders, 4)[:, None], (24, 128))
    smem = pl.BlockSpec(memory_space=pltpu.SMEM)
    full = pl.BlockSpec((24, 128), lambda g: (0, 0))
    table = pl.BlockSpec((6, CHUNK, half), lambda g: (0, g, 0))
    return pl.pallas_call(
        legendre_kernel,
        grid=(ORDERS // CHUNK,),
        in_specs=[
            smem, smem, full, full,
            pl.BlockSpec((48, 128), lambda g: (0, 0)),
            pl.BlockSpec((4, 128), lambda g: (0, 0)),
        ],
        out_specs=[table, table],
        out_shape=[jax.ShapeDtypeStruct((6, ORDERS, half), BF16)] * 2,
        scratch_shapes=[pltpu.VMEM((CHUNK * 24, 128), F32), pltpu.VMEM((96, 128), F32)],
        name="legendre_tables",
    )(coef_a.reshape(-1), coef_b.reshape(-1), order_rows, cosine, start, weight)


def filter_kernel(slot_ref, ord_ref, f_ref, ana_ref, syn_ref, spec_ref, back_ref):
    o = pl.program_id(0)
    order = ord_ref[o]
    sub = lax.broadcasted_iota(jnp.int32, (128, 128), 0)
    flip = jnp.where(sub + lane_ids((128, 128)) == 127, 1.0, 0.0).astype(BF16)
    plus = []
    minus = []
    for c in range(4):
        north = f_ref[c, :, 0].astype(F32).reshape(128, 128)
        south = f_ref[7 - c, :, 0].astype(F32).reshape(128, 128).astype(BF16)
        south = jnp.dot(south, flip, preferred_element_type=F32)
        plus.append((north + south).astype(BF16))
        minus.append((north - south).astype(BF16))
    both = jnp.concatenate(
        [jnp.concatenate(plus, axis=1), jnp.concatenate(minus, axis=1)], axis=0
    )
    coef = lax.dot_general(
        both, ana_ref[0], (((1,), (1,)), ((), ())), preferred_element_type=F32
    )
    even = ((lane_ids((128, ORDERS)) - order) & 1) == 0
    spec = jnp.where(even, coef[:128], coef[128:])
    spec_ref[0] = spec
    parts = jnp.concatenate([jnp.where(even, spec, 0.0), jnp.where(even, 0.0, spec)], axis=0)
    grid = jnp.dot(parts.astype(BF16), syn_ref[0], preferred_element_type=F32)
    factor = jnp.where(order == 0, 0.5, 1.0)
    north = (grid[:128] + grid[128:]) * factor
    south = ((grid[:128] - grid[128:]) * factor).astype(BF16)
    for c in range(4):
        cut = slice(128 * c, 128 * c + 128)
        back_ref[c, :, 0] = north[:, cut].reshape(16, 8, 128).astype(BF16)
        turned = jnp.dot(south[:, cut], flip, preferred_element_type=F32)
        back_ref[7 - c, :, 0] = turned.reshape(16, 8, 128).astype(BF16)


def legendre_filter(fourier, analysis, synthesis, orders, slots):
    half = NLAT // 2
    blocks = pl.BlockSpec((8, 16, 1, 8, 128), lambda o, *_: (0, 0, o, 0, 0))
    table = pl.BlockSpec((1, ORDERS, half), lambda o, *_: (o, 0, 0))
    return pl.pallas_call(
        filter_kernel,
        grid_spec=pltpu.PrefetchScalarGridSpec(
            num_scalar_prefetch=2,
            grid=(6,),
            in_specs=[blocks, table, table],
            out_specs=[
                pl.BlockSpec((1, 128, ORDERS), lambda o, slot, order: (slot[o], 0, 0)),
                blocks,
            ],
        ),
        out_shape=[
            jax.ShapeDtypeStruct((6, 128, ORDERS), F32),
            jax.ShapeDtypeStruct((8, 16, 6, 8, 128), BF16),
        ],
        name="legendre_filter",
    )(slots, orders, fourier, analysis, synthesis)


def inverse_kernel(y_ref, t_ref, o_ref, rows):
    @pl.when(pl.program_id(0) == 0)
    def _():
        rows[...] = y_ref[...].astype(F32).reshape(rows.shape)

    a = pl.program_id(0)
    sums = []
    for par in range(2):
        parts = [rows[pl.ds(8 * par + 2 * a + ri, PAIRS, stride=16), :].astype(BF16) for ri in range(2)]
        total = None
        for ri in range(2):
            res = lax.dot_general(
                parts[ri], t_ref[par, ri], (((0,), (0,)), ((), ())), preferred_element_type=F32
            )
            total = res if total is None else total + res
        sums.append(total * (2.0 / NLON))
    low = (sums[0] + sums[1]).astype(BF16)
    high = (sums[0] - sums[1]).astype(BF16)
    for b in range(8):
        o_ref[b, 0] = low[:, 128 * b:128 * b + 128]
        o_ref[b + 8, 0] = high[:, 128 * b:128 * b + 128]


def inverse(y, table):
    return pl.pallas_call(
        inverse_kernel,
        grid=(4,),
        in_specs=[
            pl.BlockSpec((128, 48, 128), lambda a: (0, 0, 0)),
            pl.BlockSpec((2, 2, PAIRS, NLON // 2), lambda a: (0, 0, 0, 0)),
        ],
        out_specs=pl.BlockSpec((16, 1, 128, 128), lambda a: (0, a, 0, 0)),
        out_shape=jax.ShapeDtypeStruct((16, 4, 128, 128), BF16),
        scratch_shapes=[pltpu.VMEM((128 * 48, 128), F32)],
        name="inverse",
    )(y, table)


def update_kernel(se_ref, sp_ref, f_ref, et_ref, pt_ref, oe_ref, op_ref):
    @pl.when(pl.program_id(0) < FLEV // 8)
    def _():
        oe_ref[...] = se_ref[...] + 0.5 * f_ref[0].astype(F32)
        op_ref[...] = sp_ref[...] + 0.5 * f_ref[1].astype(F32)

    @pl.when(pl.program_id(0) == FLEV // 8)
    def _():
        oe_ref[...] = se_ref[...] + 0.5 * et_ref[...]
        op_ref[...] = sp_ref[...] + 0.5 * pt_ref[...]


def update(start_entropy, start_pressure, filtered, ent_tail, pres_tail):
    whole = pl.BlockSpec((8, ROWS, COLS), lambda g: (g, 0, 0))
    tail = pl.BlockSpec((8, ROWS, COLS), lambda g: (0, 0, 0))
    return pl.pallas_call(
        update_kernel,
        grid=(LEV // 8,),
        in_specs=[
            whole, whole,
            pl.BlockSpec((2, 8, ROWS, COLS), lambda g: (0, jnp.minimum(g, FLEV // 8 - 1), 0, 0)),
            tail, tail,
        ],
        out_specs=[whole, whole],
        out_shape=[jax.ShapeDtypeStruct((LEV, ROWS, COLS), F32)] * 2,
        name="update",
    )(start_entropy, start_pressure, filtered, ent_tail, pres_tail)


def lat_factors():
    first = lax.axis_index("lat") * ROWS
    face = first - 8 + jnp.arange(136, dtype=jnp.int32)
    inside = (face >= 0) & (face < NLAT - 1)
    fs = jnp.where(inside, jnp.sin(math.pi * (face + 1).astype(F32) / NLAT), 0.0)
    row = first + jnp.arange(ROWS, dtype=jnp.int32)
    rc = 1.0 / jnp.sin(math.pi * (row.astype(F32) + 0.5) / NLAT)
    return jnp.broadcast_to(fs[:, None], (136, 128)), jnp.broadcast_to(rc[:, None], (128, 128))


def per_device(entropy, zonal_flux, meridional_flux, start_entropy, start_pressure, order_slot):
    n_lat = lax.axis_size("lat")
    n_lon = lax.axis_size("lonr")
    pairs = order_slot.reshape(PAIRS, 2)
    first_even = (pairs[:, 0] % 2) == 0
    even = jnp.where(first_even, pairs[:, 0], pairs[:, 1])
    odd = jnp.where(first_even, pairs[:, 1], pairs[:, 0])
    block = lax.axis_index("lat") * n_lon + lax.axis_index("lonr")
    both = jnp.stack((even, odd), axis=1)
    orders = lax.dynamic_slice_in_dim(both, block * 3, 3).reshape(6)
    swap = jnp.where(first_even, 0, 1).astype(jnp.int32)
    swap = lax.dynamic_slice_in_dim(swap, block * 3, 3)
    base = 2 * jnp.arange(3, dtype=jnp.int32)
    slots = jnp.stack((base + swap, base + 1 - swap), axis=1).reshape(6)

    east, west, south, north = edges(entropy, zonal_flux, meridional_flux)
    ring = range(n_lon)
    from_west = lax.ppermute(east, "lonr", [(i, (i + 1) % n_lon) for i in ring])
    from_east = lax.ppermute(west, "lonr", [((i + 1) % n_lon, i) for i in ring])
    from_north = lax.ppermute(south, "lat", [(i, i + 1) for i in range(n_lat - 1)])
    from_south = lax.ppermute(north, "lat", [(i + 1, i) for i in range(n_lat - 1)])
    table = fourier_table(jnp.stack((even, odd)))
    fs, rc = lat_factors()
    items, ent_tail, pres_tail = tendencies(
        entropy, zonal_flux, meridional_flux, from_west, from_east, west, from_north, from_south, fs, rc
    )
    grid = lax.all_to_all(
        items.reshape(16, 4, ROWS, COLS), "lonr", split_axis=0, concat_axis=0, tiled=True
    )
    analysis, synthesis = legendre_tables(orders)
    spectral = forward(grid, table)
    spectral = lax.all_to_all(
        spectral, ("lat", "lonr"), split_axis=0, concat_axis=0, tiled=True
    )
    spectrum, back = legendre_filter(
        spectral.reshape(8, 16, 6, 8, 128), analysis, synthesis, orders, slots
    )
    back = lax.all_to_all(
        back.reshape(128, 48, 128), ("lat", "lonr"), split_axis=0, concat_axis=0, tiled=True
    )
    filtered = inverse(back, table)
    filtered = lax.all_to_all(filtered, "lonr", split_axis=0, concat_axis=0, tiled=True)
    new_entropy, new_pressure = update(
        start_entropy, start_pressure, filtered.reshape(2, FLEV, ROWS, COLS), ent_tail, pres_tail
    )
    return new_entropy, new_pressure, spectrum.reshape(6, 64, 2, ORDERS)


def solution(mesh):
    cube = P(None, "lat", "lonr")
    return jax.shard_map(
        per_device,
        mesh=mesh,
        in_specs=(cube, cube, cube, cube, cube, P()),
        out_specs=(cube, cube, P(("lat", "lonr"), None, None, None)),
        check_vma=False,
    )
```

time: 648 us -> 209 us (0.32); the launches traced: 641 us -> 208 us
  local copies, waits for them, and re-layouts: 236 us -> 13.6 us
  other arithmetic: 200 us -> 5.94 us
  Pallas kernels: 0 us -> 76.6 us
  loops' own time: 50.6 us -> 0 us
  matrix products: 45.2 us -> 0 us
  waiting for transfers between devices: 35.6 us -> 52 us
  starting transfers between devices: 37.3 us -> 27.7 us
    pallas_call x0 -> x8, Pallas kernels: none -> 76.6 us  [the longest x1 16.5 us: tendencies(): pl.pallas_call(tend_kernel, grid=(LEV // 8,), in_specs=[whole, whole, who...]
    while x720 -> x0, other arithmetic: 75.1 us -> none
    another operation x1 -> x0, loops' own time: 50.6 us -> none  [legendre_tables(): lax.scan(block_step, (initial, initial, initial), block_ids)]
    dot_general x4 -> x0, matrix products: 45.2 us -> none  [the longest x1 16.8 us: legendre_filter(): jnp.einsum('oirbl,bolj->iorj', rounded, synthesis, preferred_element_type...]
    dynamic_update_slice x48 -> x0, local copies, waits for them, and re-layouts: 40.8 us -> none  [legendre_tables(): lax.scan(block_step, (initial, initial, initial), block_ids)]
    convert_element_type x4 -> x0, local copies, waits for them, and re-layouts: 39 us -> none  [the longest x2 26.6 us: fourier_tables(): forward_table = stacked.reshape(lon_count, -1).astype(jnp.bfloat16)]
    mul x340 -> x4, other arithmetic: 37.1 us -> 1.26 us  [the longest x1 0.64 us: legendre_tables(): weight = (sine * (math.pi / NLAT)).reshape(4, 128)]
    another operation x2, local copies, waits for them, and re-layouts: 35.2 us -> 0.69 us  [the longest x1 0.6 us: legendre_tables(): cosine = jnp.tile(jnp.cos(colatitude).reshape(4, 128), (6, 1))]
  transfers between devices with their start and end apart: 9 -> 7, of which waited for: 2 -> 4; matrix products, arithmetic and copies ran while one was open for 52% -> 7% of each run, Pallas kernels for 0% -> 10%
where the time goes in v1:
time: 209 us; the launch traced here: 208 us
  Pallas kernels  76.6 us (37%)
  waiting for transfers between devices  52 us (25%)
  blocking collectives  31.4 us (15%)
  starting transfers between devices  27.7 us (13%)
  local copies, waits for them, and re-layouts  13.6 us (7%)
  other arithmetic  5.94 us (3%)
    all_to_all x1, blocking collectives, per_device(): lax.all_to_all(back.reshape(128, 48, 128), ('lat', 'lonr'), split_axis=0,...  31.4 us
    all_to_all x1, waiting for transfers between devices, per_device(): lax.all_to_all(filtered, 'lonr', split_axis=0, concat_axis=0, tiled=True)  25.5 us
    all_to_all x1, waiting for transfers between devices, per_device(): lax.all_to_all(items.reshape(16, 4, ROWS, COLS), 'lonr', split_axis=0, co...  21.4 us
    pallas_call x1, Pallas kernels, tendencies(): pl.pallas_call(tend_kernel, grid=(LEV // 8,), in_specs=[whole, whole, who...  16.5 us
    pallas_call x1, Pallas kernels, legendre_tables(): pl.pallas_call(legendre_kernel, grid=(ORDERS // CHUNK,), in_specs=[smem,...  15.4 us
    pallas_call x1, Pallas kernels, legendre_filter(): pl.pallas_call(filter_kernel, grid_spec=pltpu.PrefetchScalarGridSpec(num_...  9.77 us
    pallas_call x1, Pallas kernels, forward(): pl.pallas_call(forward_kernel, grid=(PAIRS // tile,), in_specs=[pl.BlockS...  9.16 us
    all_to_all x1, starting transfers between devices, per_device(): lax.all_to_all(spectral, ('lat', 'lonr'), split_axis=0, concat_axis=0, ti...  8.48 us
  transfers between devices with their start and end apart: 7, of which 4 were waited for; matrix products, arithmetic and copies ran while one was open for 7% of the time, Pallas kernels for 10%

profile of v1, /device:TPU:0, one launch (start us, length us, event | category | flops | bytes accessed | tf_op | source)
XLA Modules:
  0.0 208.1 jit_solution(10874040392557607394)
XLA Ops:
  0.6 6.4 %edges.1 = (f32[20,8,128]{2,1,0:T(8,128)}, f32[20,8,128]{2,1,0:T(8,128)}, f32[40,4,128]{2,1,0:T(4,128)}, f32[40,4,128]{2,1,0:T(4,128)}) custom-call(f32[40,128,128]{2,1,0:T(8,128)} %s_ref.3, f32[40,128,128]{2,1,0:T(8,128)} %u_ref.3, f32[40,128,128]{2,1,0:T(8,128)} %v_ref.3), custom_call_target="tpu_custom_call" | custom-call | tf_op jit(solution)/shard_map/edges/pallas_call | solution.py:56
  7.0 1.7 collective-permute-start
  8.8 1.5 collective-permute-start.2
  10.2 1.3 collective-permute-start.3
  11.5 4.0 %collective-permute-start.1 = (f32[20,8,128]{2,1,0:T(8,128)}, f32[20,8,128]{2,1,0:T(8,128)S(1)}, u32[]{:S(2)}, u32[]{:S(2)}) collective-permute-start(f32[20,8,128]{2,1,0:T(8,128)} %get-tuple-element.17.ow_ref), channel_id=1, source_target_pairs={{1,0},{2,1},{3,2},{4,3},{5,4},{6,5},{7,6},{8,7},{9,8},{10,9},{11,1... | collective-permute-start | bytes 245768 | tf_op jit(solution)/shard_map/ppermute | solution.py:506
  15.6 0.0 collective-permute-done.hw_ref
  15.6 0.0 copy-start.4
  15.7 0.0 collective-permute-done.2.hn_ref
  15.7 0.0 collective-permute-done.3.hs_ref
  15.7 0.0 copy-start.6
  15.7 2.2 %collective-permute-done.1.he_ref = f32[20,8,128]{2,1,0:T(8,128)S(1)} collective-permute-done((f32[20,8,128]{2,1,0:T(8,128)}, f32[20,8,128]{2,1,0:T(8,128)S(1)}, u32[]{:S(2)}, u32[]{:S(2)}) %collective-permute-start.1) | collective-permute-done | bytes 81952 | tf_op jit(solution)/shard_map/ppermute | solution.py:506
  17.9 0.7 broadcast_in_dim.26.rc_ref
  18.6 0.7 broadcast_in_dim.24.fs_ref
  19.3 16.5 %tendencies.1 = (bf16[2,32,128,128]{3,2,1,0:T(8,128)(2,1)}, f32[8,128,128]{2,1,0:T(8,128)}, f32[8,128,128]{2,1,0:T(8,128)}) custom-call(f32[40,128,128]{2,1,0:T(8,128)} %s_ref.3, f32[40,128,128]{2,1,0:T(8,128)} %u_ref.3, f32[40,128,128]{2,1,0:T(8,128)} %v_ref.3, f32[20,8,128]{2,1,0:T(8,128)} %copy-done.4, f32[20,8,128]{2,1,0:T(8,128)} %copy-done.7, ...), custom_call_target="tpu_custom_call" | custom-call | tf_op jit(solution)/shard_map/tendencies/pallas_call | solution.py:161
  35.8 0.0 copy-start.9
  35.8 7.0 %all-to-all-start = ((bf16[16,4,128,128]{3,2,1,0:T(8,128)(2,1)}), bf16[16,4,128,128]{3,2,1,0:T(8,128)(2,1)S(1)}, u32[]{:S(2)}, u32[]{:S(2)}) async-start(bf16[16,4,128,128]{3,2,1,0:T(8,128)(2,1)} %bitcast.12), calls=%async_computation | async-start | bytes 4194304 | tf_op jit(solution)/shard_map/all_to_all | solution.py:514
  42.8 0.2 reshape.426
  43.0 0.3 slice_reduce_fusion
  43.3 0.2 fusion.14
  43.5 0.9 copy.15.turn_ref
  44.4 1.6 fusion.9
  46.0 0.9 pad_maximum_fusion.base_ref
  47.0 4.9 %longitude_table.1.t_ref = bf16[2,2,384,1024]{3,2,1,0:T(8,128)(2,1)} custom-call(f32[2,2,384,128]{3,2,1,0:T(8,128)} %pad_maximum_fusion.base_ref, f32[2,384,16]{2,1,0:T(8,128)} %copy.15.turn_ref), custom_call_target="tpu_custom_call" | custom-call | tf_op jit(solution)/shard_map/longitude_table/pallas_call | solution.py:204
  51.9 0.1 add_bitcast_fusion
  52.0 21.4 %all-to-all-done.x_ref = bf16[16,4,128,128]{3,2,1,0:T(8,128)(2,1)S(1)} async-done(((bf16[16,4,128,128]{3,2,1,0:T(8,128)(2,1)}), bf16[16,4,128,128]{3,2,1,0:T(8,128)(2,1)S(1)}, u32[]{:S(2)}, u32[]{:S(2)}) %all-to-all-start) | async-done | bytes 2097184 | tf_op jit(solution)/shard_map/all_to_all | solution.py:514
  73.3 1.3 copy-done
  74.7 9.2 %forward.1 = bf16[128,48,128]{2,1,0:T(8,128)(2,1)} custom-call(bf16[16,4,128,128]{3,2,1,0:T(8,128)(2,1)} %copy-done, bf16[2,2,384,1024]{3,2,1,0:T(8,128)(2,1)} %longitude_table.1.t_ref), custom_call_target="tpu_custom_call" | custom-call | tf_op jit(solution)/shard_map/forward/pallas_call | solution.py:240
  83.8 8.5 %all-to-all-start.1 = ((bf16[128,48,128]{2,1,0:T(8,128)(2,1)}), bf16[128,48,128]{2,1,0:T(8,128)(2,1)S(1)}, u32[]{:S(2)}, u32[]{:S(2)}) async-start(bf16[128,48,128]{2,1,0:T(8,128)(2,1)} %forward.1), calls=%async_computation.1 | async-start | bytes 3145728 | tf_op jit(solution)/shard_map/all_to_all | solution.py:519
  92.3 0.1 copy.11
  92.4 0.6 reshape.427.slot_ref
  93.1 0.1 copy.13
  93.1 0.1 copy.12
  93.3 0.1 fusion.28
  93.4 0.1 copy.14
  93.5 0.1 reshape.428.ord_ref
  93.5 0.1 multiply_add_fusion.1
  93.6 0.1 add.222
  93.7 0.1 add.223
  93.8 0.1 mul.206
  93.8 0.1 mul.207
  93.9 0.1 broadcast_in_dim.29
  94.0 0.1 broadcast_in_dim.30
  94.1 0.5 divide_sqrt_fusion
  94.6 0.3 sqrt.18
  94.9 0.3 reshape.435.a_ref
  95.1 0.6 mul.204.b_ref
  95.7 0.1 fusion.26
  95.8 0.6 fusion.25.w_ref
  96.5 0.1 fusion.35
  96.6 0.6 pad_maximum_fusion.2.start_ref
  97.2 0.6 tile.8
  97.8 0.7 broadcast_in_dim.54.m_ref
  98.4 0.0 copy-done.3
  98.4 15.4 %legendre_tables.1 = (bf16[6,768,512]{2,1,0:T(8,128)(2,1)}, bf16[6,768,512]{2,1,0:T(8,128)(2,1)}) custom-call(f32[4608]{0:T(1024)} %copy-done.3, f32[4608]{0:T(1024)} %mul.204.b_ref, s32[24,128]{1,0:T(8,128)} %broadcast_in_dim.54.m_ref, f32[24,128]{1,0:T(8,128)} %bitcast.15, f32[48,128]{1,0:T(8,128)} %pad_maximum_fusion.2.start_ref, f32[4,128]{1,0:T(4,128)} %fusion.25.w_ref), custom_call_target="tpu_custom_call" | custom-call | tf_op jit(solution)/shard_map/legendre_tables/pallas_call | solution.py:339
  113.8 2.9 %all-to-all-done.1 = bf16[128,48,128]{2,1,0:T(8,128)(2,1)S(1)} async-done(((bf16[128,48,128]{2,1,0:T(8,128)(2,1)}), bf16[128,48,128]{2,1,0:T(8,128)(2,1)S(1)}, u32[]{:S(2)}, u32[]{:S(2)}) %all-to-all-start.1) | async-done | bytes 1572896 | tf_op jit(solution)/shard_map/all_to_all | solution.py:519
  116.8 1.1 copy-done.2
  117.9 9.8 %legendre_filter.1 = (f32[6,128,768]{2,1,0:T(8,128)}, bf16[8,16,6,8,128]{4,3,2,1,0:T(8,128)(2,1)}) custom-call(s32[6]{0:T(128)} %reshape.427.slot_ref, s32[6]{0:T(128)} %copy-done.8, bf16[8,16,6,8,128]{4,3,2,1,0:T(8,128)(2,1)} %bitcast.11, bf16[6,768,512]{2,1,0:T(8,128)(2,1)} %get-tuple-element.21.ana_ref, bf16[6,768,512]{2,1,0:T(8,128)(2,1)} %get-tuple-element.22.syn_ref), custom_call_target="tpu_custom_call" | custom-call | tf_op jit(solution)/shard_map/legendre_filter/pallas_call | solution.py:392
  127.7 31.4 %all_to_all.20.y_ref = bf16[128,48,128]{2,1,0:T(8,128)(2,1)} all-to-all(bf16[128,48,128]{2,1,0:T(8,128)(2,1)} %bitcast.13), channel_id=1, replica_groups=mesh['lat'=8,'lonr'=16] {'lat','lonr'}, dimensions={0} | all-to-all | bytes 3145728 | tf_op jit(solution)/shard_map/all_to_all | solution.py:525
  159.1 7.3 %inverse.1 = bf16[16,4,128,128]{3,2,1,0:T(8,128)(2,1)} custom-call(bf16[128,48,128]{2,1,0:T(8,128)(2,1)} %all_to_all.20.y_ref, bf16[2,2,384,1024]{3,2,1,0:T(8,128)(2,1)} %longitude_table.1.t_ref), custom_call_target="tpu_custom_call" | custom-call | tf_op jit(solution)/shard_map/inverse/pallas_call | solution.py:435
  166.4 3.7 %all-to-all-start.3 = ((bf16[16,4,128,128]{3,2,1,0:T(8,128)(2,1)}), bf16[16,4,128,128]{3,2,1,0:T(8,128)(2,1)S(1)}, u32[]{:S(2)}, u32[]{:S(2)}) async-start(bf16[16,4,128,128]{3,2,1,0:T(8,128)(2,1)} %inverse.1), calls=%async_computation.3 | async-start | bytes 4194304 | tf_op jit(solution)/shard_map/all_to_all | solution.py:529
  170.1 4.0 %reshape.433 = f32[6,64,2,768]{3,2,1,0:T(2,128)} reshape(f32[6,128,768]{2,1,0:T(8,128)} %get-tuple-element.28) | data formatting | bytes 4718592 | tf_op jit(solution)/shard_map/reshape | solution.py:533
  174.1 25.5 %all-to-all-done.3 = bf16[16,4,128,128]{3,2,1,0:T(8,128)(2,1)S(1)} async-done(((bf16[16,4,128,128]{3,2,1,0:T(8,128)(2,1)}), bf16[16,4,128,128]{3,2,1,0:T(8,128)(2,1)S(1)}, u32[]{:S(2)}, u32[]{:S(2)}) %all-to-all-start.3) | async-done | bytes 2097184 | tf_op jit(solution)/shard_map/all_to_all | solution.py:529
  199.6 1.3 copy-done.1
  200.9 7.2 %update.1 = (f32[40,128,128]{2,1,0:T(8,128)}, f32[40,128,128]{2,1,0:T(8,128)}) custom-call(f32[40,128,128]{2,1,0:T(8,128)} %se_ref.1, f32[40,128,128]{2,1,0:T(8,128)} %sp_ref.1, bf16[2,32,128,128]{3,2,1,0:T(8,128)(2,1)} %bitcast.10, f32[8,128,128]{2,1,0:T(8,128)} %get-tuple-element.24.et_ref, f32[8,128,128]{2,1,0:T(8,128)} %get-tuple-element.25.pt_ref), custom_call_target="tpu_custom_call" | custom-call | tf_op jit(solution)/shard_map/update/pallas_call | solution.py:464
  (26 shorter events, 0.2 us)
Async XLA Ops:
  7.0 8.6 %collective-permute-start = (f32[20,8,128]{2,1,0:T(8,128)}, f32[20,8,128]{2,1,0:T(8,128)S(1)}, u32[]{:S(2)}, u32[]{:S(2)}) collective-permute-start(f32[20,8,128]{2,1,0:T(8,128)} %get-tuple-element.16), channel_id=1, source_target_pairs={{0,1},{1,2},{2,3},{3,4},{4,5},{5,6},{6,7},{7,8},{8,9},{9,10},{10,1... | collective-permute-start | bytes 245768 | tf_op jit(solution)/shard_map/ppermute | solution.py:505
  8.8 6.9 %collective-permute-start.2 = (f32[40,4,128]{2,1,0:T(4,128)}, f32[40,4,128]{2,1,0:T(4,128)S(1)}, u32[]{:S(2)}, u32[]{:S(2)}) collective-permute-start(f32[40,4,128]{2,1,0:T(4,128)} %get-tuple-element.18), channel_id=1, source_target_pairs={{0,16},{16,32},{32,48},{48,64},{64,80},{80,96},{96,112},{1,17},{17... | collective-permute-start | bytes 245768 | tf_op jit(solution)/shard_map/ppermute | solution.py:507
  10.2 5.4 %collective-permute-start.3 = (f32[40,4,128]{2,1,0:T(4,128)}, f32[40,4,128]{2,1,0:T(4,128)S(1)}, u32[]{:S(2)}, u32[]{:S(2)}) collective-permute-start(f32[40,4,128]{2,1,0:T(4,128)} %get-tuple-element.19), channel_id=1, source_target_pairs={{16,0},{32,16},{48,32},{64,48},{80,64},{96,80},{112,96},{17,1},{33... | collective-permute-start | bytes 245768 | tf_op jit(solution)/shard_map/ppermute | solution.py:508
  11.5 6.4 %collective-permute-start.1 = (f32[20,8,128]{2,1,0:T(8,128)}, f32[20,8,128]{2,1,0:T(8,128)S(1)}, u32[]{:S(2)}, u32[]{:S(2)}) collective-permute-start(f32[20,8,128]{2,1,0:T(8,128)} %get-tuple-element.17.ow_ref), channel_id=1, source_target_pairs={{1,0},{2,1},{3,2},{4,3},{5,4},{6,5},{7,6},{8,7},{9,8},{10,9},{11,1... | collective-permute-start | bytes 245768 | tf_op jit(solution)/shard_map/ppermute | solution.py:506
  15.6 3.7 %copy-start.4 = (f32[20,8,128]{2,1,0:T(8,128)}, f32[20,8,128]{2,1,0:T(8,128)S(1)}, u32[]{:S(2)}) copy-start(f32[20,8,128]{2,1,0:T(8,128)S(1)} %collective-permute-done.hw_ref) | copy-start | bytes 245764
  15.7 3.7 %copy-start.5 = (f32[40,4,128]{2,1,0:T(4,128)}, f32[40,4,128]{2,1,0:T(4,128)S(1)}, u32[]{:S(2)}) copy-start(f32[40,4,128]{2,1,0:T(4,128)S(1)} %collective-permute-done.2.hn_ref) | copy-start | bytes 245764
  15.7 3.6 %copy-start.6 = (f32[40,4,128]{2,1,0:T(4,128)}, f32[40,4,128]{2,1,0:T(4,128)S(1)}, u32[]{:S(2)}) copy-start(f32[40,4,128]{2,1,0:T(4,128)S(1)} %collective-permute-done.3.hs_ref) | copy-start | bytes 245764
  17.9 1.4 copy-start.7
  35.8 7.0 %copy-start.9 = (s32[768]{0:T(1024)S(1)}, s32[768]{0:T(1024)}, u32[]{:S(2)}) copy-start(s32[768]{0:T(1024)} %param.11) | copy-start | bytes 9220
  35.8 37.5 %all-to-all-start = ((bf16[16,4,128,128]{3,2,1,0:T(8,128)(2,1)}), bf16[16,4,128,128]{3,2,1,0:T(8,128)(2,1)S(1)}, u32[]{:S(2)}, u32[]{:S(2)}) async-start(bf16[16,4,128,128]{3,2,1,0:T(8,128)(2,1)} %bitcast.12), calls=%async_computation | async-start | bytes 4194304 | tf_op jit(solution)/shard_map/all_to_all | solution.py:514
  73.3 1.3 copy-start
  83.8 32.9 %all-to-all-start.1 = ((bf16[128,48,128]{2,1,0:T(8,128)(2,1)}), bf16[128,48,128]{2,1,0:T(8,128)(2,1)S(1)}, u32[]{:S(2)}, u32[]{:S(2)}) async-start(bf16[128,48,128]{2,1,0:T(8,128)(2,1)} %forward.1), calls=%async_computation.1 | async-start | bytes 3145728 | tf_op jit(solution)/shard_map/all_to_all | solution.py:519
  93.5 23.2 %copy-start.8 = (s32[6]{0:T(128)}, s32[6]{0:T(128)S(1)}, u32[]{:S(2)}) copy-start(s32[6]{0:T(128)S(1)} %reshape.428.ord_ref) | copy-start | bytes 76
  95.1 3.3 %copy-start.3 = (f32[4608]{0:T(1024)}, f32[4608]{0:T(1024)S(1)}, u32[]{:S(2)}) copy-start(f32[4608]{0:T(1024)S(1)} %reshape.435.a_ref) | copy-start | bytes 55300
  116.8 1.1 copy-start.2
  166.4 33.2 %all-to-all-start.3 = ((bf16[16,4,128,128]{3,2,1,0:T(8,128)(2,1)}), bf16[16,4,128,128]{3,2,1,0:T(8,128)(2,1)S(1)}, u32[]{:S(2)}, u32[]{:S(2)}) async-start(bf16[16,4,128,128]{3,2,1,0:T(8,128)(2,1)} %inverse.1), calls=%async_computation.3 | async-start | bytes 4194304 | tf_op jit(solution)/shard_map/all_to_all | solution.py:529
  199.6 1.3 copy-start.1

commit v2 on v1

v2 whole, which is shorter than its diff:
```python
import math

import jax
import jax.numpy as jnp
from jax import lax
from jax.experimental import pallas as pl
from jax.experimental.pallas import tpu as pltpu
import numpy as np
from jax.sharding import PartitionSpec as P

FLEV = 32
LEV = 40
NLAT = 1024
NLON = 2048
ORDERS = 768
PAIRS = ORDERS // 2
ROWS = 128
COLS = 128
F32 = jnp.float32
BF16 = jnp.bfloat16

gamma_three_halves = 0.5 * math.log(math.pi) - math.log(2.0)


def vmem(mib):
    return pltpu.CompilerParams(vmem_limit_bytes=mib << 20)


IN_VMEM = pl.BlockSpec(memory_space=pltpu.VMEM)


def in_vmem(x):
    return pltpu.with_memory_space_constraint(x, pltpu.VMEM)


def lane_ids(shape):
    return lax.broadcasted_iota(jnp.int32, shape, len(shape) - 1)


def edges_kernel(
    first_ref, s_any, u_any, v_ref, east_ref, west_ref, south_ref, north_ref, fs_ref, rc_ref,
    s_ref, u_ref, sems
):
    lane = lane_ids((8, 128))
    group = lane >> 3
    flux = (lane & 7) == 7
    parts = LEV // 8

    def fetch(n, g):
        at = pl.ds(8 * g, 8)
        src = (s_any, u_any)[n]
        dst = (s_ref, u_ref)[n]
        return pltpu.make_async_copy(src.at[at], dst.at[at], sems.at[n, g])

    for g in range(parts):
        for n in range(2):
            fetch(n, g).start()
    at = first_ref[0] - 8 + lax.broadcasted_iota(jnp.int32, (136, 128), 0)
    sines = jnp.sin((math.pi / NLAT) * (at + 1).astype(F32))
    fs_ref[...] = jnp.where((at >= 0) & (at < NLAT - 1), sines, 0.0)
    rc_ref[...] = 1.0 / jnp.sin((math.pi / NLAT) * (at[8:].astype(F32) + 0.5))

    def one_pair(q, carry):
        for half in range(2):
            lev = 2 * q + half
            east = jnp.zeros((8, 128), F32)
            west = jnp.zeros((8, 128), F32)
            for i in range(16):
                s = s_ref[lev, pl.ds(8 * i, 8), :]
                u = u_ref[lev, pl.ds(8 * i, 8), :]
                s_end = pltpu.roll(s, (8 * i + 7) % 128, 1)
                u_end = pltpu.roll(u, (8 * i + 8) % 128, 1)
                s_top = pltpu.roll(s, 8 * i, 1) if i else s
                mine = group == i
                east = jnp.where(mine, jnp.where(flux, u_end, s_end), east)
                west = jnp.where(mine, s_top, west)
            east_ref[lev] = east
            west_ref[lev] = west
            south_ref[lev, 0:3, :] = s_ref[lev, 125:128, :]
            north_ref[lev] = s_ref[lev, 0:4, :]
        return carry

    for g in range(parts):
        for n in range(2):
            fetch(n, g).wait()
        lax.fori_loop(4 * g, 4 * g + 4, one_pair, 0)
    for lev in range(LEV):
        south_ref[lev, 3:4, :] = v_ref[lev, 7:8, :]


def edges(first, entropy, zonal, merid):
    anywhere = pl.BlockSpec(memory_space=pl.ANY)
    return pl.pallas_call(
        edges_kernel,
        grid=(1,),
        in_specs=[pl.BlockSpec(memory_space=pltpu.SMEM), anywhere, anywhere, pl.BlockSpec((LEV, 8, COLS), lambda g: (0, ROWS // 8 - 1, 0))],
        out_specs=[pl.BlockSpec((LEV, n, 128), lambda g: (0, 0, 0)) for n in (8, 8, 4, 4)]
        + [pl.BlockSpec((n, 128), lambda g: (0, 0)) for n in (136, 128)],
        out_shape=[
            pltpu.HBM((LEV, 8, 128), F32),
            pltpu.HBM((LEV, 8, 128), F32),
            pltpu.HBM((LEV, 4, 128), F32),
            pltpu.HBM((LEV, 4, 128), F32),
            pltpu.HBM((136, 128), F32),
            pltpu.HBM((128, 128), F32),
        ],
        scratch_shapes=[pltpu.VMEM((LEV, ROWS, COLS), F32)] * 2
        + [pltpu.SemaphoreType.DMA((2, LEV // 8))],
        name="edges",
    )(first, entropy, zonal, merid)


def stencil(x0, x1, x2, x3, x4, x5):
    return (37.0 * (x2 + x3) - 8.0 * (x1 + x4) + (x0 + x5)) * (1.0 / 60.0)


def stencil_matrices():
    weights = {-2: 1.0, -1: -8.0, 0: 37.0, 1: 37.0, 2: -8.0, 3: 1.0}
    along = np.zeros((256, 256), np.float32)
    across = np.zeros((128, 136), np.float32)
    for face in range(128):
        for shift, weight in weights.items():
            cell = face + shift
            along[cell if 0 <= cell < 128 else 128 + cell % 128 if cell >= 128 else 128 + 7 + cell, face] = weight
            across[face, cell if 0 <= cell < 128 else 128 + 4 + cell % 128 if cell >= 128 else 128 + 3 + cell] = weight
    along[128 + 3, 128 + 127] = 1.0
    along[128 + 7, 128] = 1.0
    return along, across


def split(x):
    high = x.astype(BF16)
    return high, (x - high.astype(F32)).astype(BF16)


def tend_kernel(
    s_ref, u_ref, v_ref, hw_ref, he_ref, ow_ref, hn_ref, hs_ref, fs_ref, rc_ref, along_ref, across_ref,
    se_ref, sp_ref, item_ref, ent_ref, pres_ref, cells, face, mext,
):
    step = pl.program_id(0)
    lane = lane_ids((ROWS, COLS))
    small = lane_ids((8, 128)) & 7
    across = across_ref[...]

    def prepare(q, carry):
        for half in range(4):
            lev = 4 * q + half
            west = hw_ref[lev]
            own = ow_ref[lev]
            edge = stencil(
                pltpu.roll(west, 127, 1), pltpu.roll(west, 126, 1), pltpu.roll(west, 125, 1),
                pltpu.roll(own, 3, 1), pltpu.roll(own, 2, 1), pltpu.roll(own, 1, 1),
            )
            edge = edge * pltpu.roll(west, 124, 1)
            rim = jnp.where(small < 3, he_ref[lev], jnp.where(small == 3, edge, west))
            rim = jnp.concatenate([pltpu.roll(rim, (128 - 8 * i) % 128, 1) for i in range(16)])
            s = s_ref[lev]
            s_hi, s_lo = split(s)
            r_hi, r_lo = split(rim)
            at = pl.ds(pl.multiple_of(lev * 128, 128), 128)
            cells[at, 0:128] = s_hi
            cells[at, 128:256] = r_hi
            cells[at, 256:384] = s_lo
            cells[at, 384:512] = r_lo
            h_hi, h_lo = split(jnp.concatenate([hn_ref[lev], hs_ref[lev]]))
            n_face = jnp.dot(
                across, jnp.concatenate([s_hi, s_lo, h_hi, h_lo]), preferred_element_type=F32
            )
            face[lev, :, 256:384] = n_face
        return carry

    lax.fori_loop(0, 2, prepare, 0)
    for part in range(2):
        rows = slice(512 * part, 512 * part + 512)
        res = jnp.dot(cells[rows, :], along_ref[...], preferred_element_type=F32)
        face[4 * part:4 * part + 4, :, 0:256] = res.reshape(4, 128, 256)

    def level(lev, half):
        u = u_ref[lev]
        z = (u * (1.0 / 60.0)) * face[lev, :, 0:128]
        rim = face[lev, :, 128:256]
        dz = z - pltpu.roll(jnp.where(lane == COLS - 1, rim, z), 1, 1)
        du = u - jnp.where(lane == 0, rim, pltpu.roll(u, 1, 1))
        fv = v_ref[lev] * fs_ref[8:136, :]
        fv_top = hn_ref[lev, 3:4, :] * fs_ref[7:8, :]
        top = [hn_ref[lev, o:o + 1, :] for o in range(3)] + [s_ref[lev, o:o + 1, :] for o in range(3)]
        m = fv * (face[lev, :, 256:384] * (1.0 / 60.0))
        mext[half, 0, 7:8, :] = fv_top * stencil(*top)
        mext[half, 0, 8:136, :] = m
        mext[half, 1, 7:8, :] = fv_top
        mext[half, 1, 8:136, :] = fv
        rc = rc_ref[...]
        ent = -(dz + (m - mext[half, 0, 7:135, :]) * rc)
        pres = -0.3 * (du + (fv - mext[half, 1, 7:135, :]) * rc)
        return ent, pres

    @pl.when(step < FLEV // 8)
    def _():
        def body(q, carry):
            for half in range(4):
                ent, pres = level(4 * q + half, half)
                item_ref[0, 4 * q + half] = ent.astype(BF16)
                item_ref[1, 4 * q + half] = pres.astype(BF16)
            return carry

        lax.fori_loop(0, 2, body, 0)

    @pl.when(step == FLEV // 8)
    def _():
        def body(q, carry):
            for half in range(4):
                ent, pres = level(4 * q + half, half)
                lev = 4 * q + half
                ent_ref[lev] = se_ref[lev] + 0.5 * ent
                pres_ref[lev] = sp_ref[lev] + 0.5 * pres
            return carry

        lax.fori_loop(0, 2, body, 0)


def tendencies(
    s, u, v, from_west, from_east, own_west, from_north, from_south, fs, rc, start_entropy, start_pressure
):
    whole = pl.BlockSpec((8, ROWS, COLS), lambda g: (g, 0, 0))
    packed = pl.BlockSpec((8, 8, 128), lambda g: (g, 0, 0))
    rows4 = pl.BlockSpec((8, 4, 128), lambda g: (g, 0, 0))
    tail = pl.BlockSpec((8, ROWS, COLS), lambda g: (FLEV // 8, 0, 0))
    along, across = stencil_matrices()
    along = jnp.asarray(np.concatenate((along, along)), BF16)
    across = np.concatenate(
        (across[:, :128], across[:, :128], across[:, 128:], across[:, 128:]), axis=1
    )
    return pl.pallas_call(
        tend_kernel,
        grid=(LEV // 8,),
        in_specs=[
            whole, whole, whole, packed, packed, packed, rows4, rows4,
            pl.BlockSpec((136, 128), lambda g: (0, 0)),
            pl.BlockSpec((128, 128), lambda g: (0, 0)),
            pl.BlockSpec((512, 256), lambda g: (0, 0)),
            pl.BlockSpec((128, 272), lambda g: (0, 0)),
            tail, tail,
        ],
        out_specs=[
            pl.BlockSpec((2, 8, ROWS, COLS), lambda g: (0, jnp.minimum(g, FLEV // 8 - 1), 0, 0)),
            tail, tail,
        ],
        out_shape=[
            pltpu.HBM((2, FLEV, ROWS, COLS), BF16),
            pltpu.HBM((LEV, ROWS, COLS), F32),
            pltpu.HBM((LEV, ROWS, COLS), F32),
        ],
        scratch_shapes=[
            pltpu.VMEM((1024, 512), BF16),
            pltpu.VMEM((8, 128, 384), F32),
            pltpu.VMEM((4, 2, 136, 128), F32),
        ],
        name="tendencies",
    )(s, u, v, from_west, from_east, own_west, from_north, from_south, fs, rc,
      along, jnp.asarray(across, BF16), start_entropy, start_pressure)


def table_kernel(base_ref, turn_ref, out_ref):
    for par in range(2):
        c = base_ref[par, 0]
        s = base_ref[par, 1]
        for b in range(8):
            tc = jnp.broadcast_to(turn_ref[par, :, b:b + 1], c.shape)
            ts = jnp.broadcast_to(turn_ref[par, :, 8 + b:9 + b], c.shape)
            out_ref[par, 0, :, 128 * b:128 * b + 128] = (c * tc - s * ts).astype(BF16)
            out_ref[par, 1, :, 128 * b:128 * b + 128] = (s * tc + c * ts).astype(BF16)


def fourier_table(even_odd):
    def angles(steps):
        product = (even_odd[:, :, None] * steps[None, None, :]) % NLON
        return (2.0 * math.pi / NLON) * product.astype(F32)

    near = angles(jnp.arange(128, dtype=jnp.int32))
    far = angles(128 * jnp.arange(8, dtype=jnp.int32))
    base = jnp.stack((jnp.cos(near), jnp.sin(near)), axis=1)
    turn = jnp.concatenate((jnp.cos(far), jnp.sin(far)), axis=2)
    tile = 96
    return pl.pallas_call(
        table_kernel,
        grid=(PAIRS // tile,),
        in_specs=[
            pl.BlockSpec((2, 2, tile, 128), lambda g: (0, 0, g, 0)),
            pl.BlockSpec((2, tile, 16), lambda g: (0, g, 0)),
        ],
        out_specs=pl.BlockSpec((2, 2, tile, NLON // 2), lambda g: (0, 0, g, 0)),
        out_shape=pltpu.HBM((2, 2, PAIRS, NLON // 2), BF16),
        name="longitude_table",
    )(base, turn)


def forward_kernel(x_ref, t_ref, o_ref, fold, rows):
    par = pl.program_id(0)
    for a in range(4):
        for b in range(8):
            lo = x_ref[b, a]
            hi = x_ref[b + 8, a]
            fold[128 * a:128 * a + 128, 128 * b:128 * b + 128] = lo + jnp.where(par == 0, hi, -hi)
    res = lax.dot_general(
        t_ref[0].reshape(2 * PAIRS, NLON // 2), fold[...], (((1,), (1,)), ((), ())),
        preferred_element_type=F32,
    )
    for ri in range(2):
        for a in range(4):
            rows[pl.ds(8 * par + 2 * a + ri, PAIRS, stride=16), :] = (
                res[PAIRS * ri:PAIRS * ri + PAIRS, 128 * a:128 * a + 128]
            )

    @pl.when(par == 1)
    def _():
        o_ref[...] = rows[...].reshape(o_ref.shape).astype(BF16)


def forward(x, table):
    return pl.pallas_call(
        forward_kernel,
        grid=(2,),
        in_specs=[
            IN_VMEM,
            pl.BlockSpec((1, 2, PAIRS, NLON // 2), lambda g: (g, 0, 0, 0)),
        ],
        out_specs=pl.BlockSpec((128, 48, 128), lambda g: (0, 0, 0)),
        out_shape=pltpu.HBM((128, 48, 128), BF16),
        scratch_shapes=[
            pltpu.VMEM((512, NLON // 2), BF16),
            pltpu.VMEM((16 * PAIRS, 128), F32),
        ],
        compiler_params=vmem(56),
        name="forward",
    )(in_vmem(x), table)


CHUNK = 128


def legendre_kernel(a_ref, b_ref, m_ref, cos_ref, start_ref, w_ref, ana_ref, syn_ref, rows, state):
    chunk = pl.program_id(0)
    upper = lax.broadcasted_iota(jnp.int32, (8, 128), 0) < 4

    @pl.when(chunk == 0)
    def _():
        state[...] = jnp.zeros_like(state)

    cosine = [cos_ref[8 * v:8 * v + 8, :] for v in range(3)]
    orders = [m_ref[8 * v:8 * v + 8, :] for v in range(3)]

    def body(it, carry):
        prev, curr, logs, scale = carry
        for k in range(4):
            local = it * 4 + k
            degree = chunk * CHUNK + local
            nxt = []
            new_logs = []
            new_scale = []
            for v in range(3):
                at = degree * 6 + 2 * v
                a = jnp.where(upper, a_ref[at], a_ref[at + 1])
                b = jnp.where(upper, b_ref[at], b_ref[at + 1])
                first = orders[v] == degree
                start = start_ref[8 * v:8 * v + 8, :]
                val = jnp.where(first, 1.0, (a * cosine[v]) * curr[v] - b * prev[v])
                lg = jnp.where(first, start, logs[v])
                sc = jnp.where(first, start_ref[24 + 8 * v:32 + 8 * v, :], scale[v])
                row = pl.multiple_of(local * 24, 8) + 8 * v
                rows[pl.ds(row, 8), :] = val * sc
                nxt.append(val)
                new_logs.append(lg)
                new_scale.append(sc)
            prev, curr, logs, scale = curr, nxt, new_logs, new_scale
        grow = [jnp.maximum(1.0, jnp.maximum(jnp.abs(p), jnp.abs(c))) for p, c in zip(prev, curr)]
        inv = [1.0 / g for g in grow]
        prev = [p * i for p, i in zip(prev, inv)]
        curr = [c * i for c, i in zip(curr, inv)]
        logs = [l + jnp.log(g) for l, g in zip(logs, grow)]
        scale = [jnp.where(s > -1.0, jnp.where(o <= chunk * CHUNK + it * 4 + 3, jnp.exp(l), 0.0), 0.0)
                 for s, l, o in zip(scale, logs, orders)]
        return prev, curr, logs, scale

    init = tuple([state[24 * n + 8 * v:24 * n + 8 * v + 8, :] for v in range(3)] for n in range(4))
    final = lax.fori_loop(0, CHUNK // 4, body, init)
    for n in range(4):
        for v in range(3):
            state[24 * n + 8 * v:24 * n + 8 * v + 8, :] = final[n][v]
    for o in range(6):
        for jb in range(4):
            val = rows[pl.ds(4 * o + jb, CHUNK, stride=24), :]
            syn_ref[o, :, 128 * jb:128 * jb + 128] = val.astype(BF16)
            ana_ref[o, :, 128 * jb:128 * jb + 128] = (val * w_ref[jb:jb + 1, :]).astype(BF16)


def legendre_tables(orders):
    half = NLAT // 2
    colatitude = math.pi * (jnp.arange(half, dtype=F32) + 0.5) / NLAT
    sine = jnp.sin(colatitude)
    order_f = orders.astype(F32)
    log_start = (
        -0.5 * math.log(2.0)
        + 0.5 * (lax.lgamma(order_f + 1.5) - gamma_three_halves - lax.lgamma(order_f + 1.0))
    )[:, None] + order_f[:, None] * jnp.log(sine)[None, :]
    log_start = log_start.reshape(24, 128)
    start = jnp.concatenate((log_start, jnp.exp(log_start)))
    cosine = jnp.tile(jnp.cos(colatitude).reshape(4, 128), (6, 1))
    weight = (sine * (math.pi / NLAT)).reshape(4, 128)
    deg = jnp.arange(ORDERS, dtype=F32)[:, None]
    running = orders[None, :] < jnp.arange(ORDERS, dtype=jnp.int32)[:, None]
    denom_a = jnp.maximum(deg * deg - order_f * order_f, 1.0)
    coef_a = jnp.where(running, jnp.sqrt(jnp.maximum(4.0 * deg * deg - 1.0, 0.0) / denom_a), 0.0)
    numer_b = jnp.maximum((deg - 1.0) * (deg - 1.0) - order_f * order_f, 0.0)
    denom_b = jnp.maximum(4.0 * (deg - 1.0) * (deg - 1.0) - 1.0, 1.0)
    coef_b = coef_a * jnp.sqrt(numer_b / denom_b)
    order_rows = jnp.broadcast_to(jnp.repeat(orders, 4)[:, None], (24, 128))
    smem = pl.BlockSpec(memory_space=pltpu.SMEM)
    full = pl.BlockSpec((24, 128), lambda g: (0, 0))
    return pl.pallas_call(
        legendre_kernel,
        grid=(ORDERS // CHUNK,),
        in_specs=[
            smem, smem, full, full,
            pl.BlockSpec((48, 128), lambda g: (0, 0)),
            pl.BlockSpec((4, 128), lambda g: (0, 0)),
        ],
        out_specs=[pl.BlockSpec((6, CHUNK, half), lambda g: (0, g, 0))] * 2,
        out_shape=[pltpu.HBM((6, ORDERS, half), BF16)] * 2,
        scratch_shapes=[pltpu.VMEM((CHUNK * 24, 128), F32), pltpu.VMEM((96, 128), F32)],
        name="legendre_tables",
    )(coef_a.reshape(-1), coef_b.reshape(-1), order_rows, cosine, start, weight)


def filter_kernel(slot_ref, ord_ref, f_ref, ana_ref, syn_ref, spec_ref, back_ref):
    sub = lax.broadcasted_iota(jnp.int32, (128, 128), 0)
    flip = jnp.where(sub + lane_ids((128, 128)) == 127, 1.0, 0.0).astype(BF16)
    for k in range(2):
        o = 2 * pl.program_id(0) + k
        order = ord_ref[o]
        plus = []
        minus = []
        for c in range(4):
            north = f_ref[c, :, o].astype(F32).reshape(128, 128)
            south = f_ref[7 - c, :, o].astype(F32).reshape(128, 128).astype(BF16)
            south = jnp.dot(south, flip, preferred_element_type=F32)
            plus.append((north + south).astype(BF16))
            minus.append((north - south).astype(BF16))
        both = jnp.concatenate(
            [jnp.concatenate(plus, axis=1), jnp.concatenate(minus, axis=1)], axis=0
        )
        coef = lax.dot_general(
            both, ana_ref[k], (((1,), (1,)), ((), ())), preferred_element_type=F32
        )
        even = ((lane_ids((128, ORDERS)) - order) & 1) == 0
        spec = jnp.where(even, coef[:128], coef[128:])
        spec_ref[slot_ref[o] & 1] = spec
        parts = jnp.concatenate([jnp.where(even, spec, 0.0), jnp.where(even, 0.0, spec)], axis=0)
        grid = jnp.dot(parts.astype(BF16), syn_ref[k], preferred_element_type=F32)
        factor = jnp.where(order == 0, 0.5, 1.0)
        north = (grid[:128] + grid[128:]) * factor
        south = ((grid[:128] - grid[128:]) * factor).astype(BF16)
        for c in range(4):
            cut = slice(128 * c, 128 * c + 128)
            back_ref[c, :, k] = north[:, cut].reshape(16, 8, 128).astype(BF16)
            turned = jnp.dot(south[:, cut], flip, preferred_element_type=F32)
            back_ref[7 - c, :, k] = turned.reshape(16, 8, 128).astype(BF16)


def legendre_filter(fourier, analysis, synthesis, orders, slots):
    table = pl.BlockSpec((2, ORDERS, NLAT // 2), lambda p, *_: (p, 0, 0))
    blocks = pl.BlockSpec((8, 16, 2, 8, 128), lambda p, *_: (0, 0, p, 0, 0))
    return pl.pallas_call(
        filter_kernel,
        grid_spec=pltpu.PrefetchScalarGridSpec(
            num_scalar_prefetch=2,
            grid=(3,),
            in_specs=[IN_VMEM, table, table],
            out_specs=[
                pl.BlockSpec((2, 128, ORDERS), lambda p, *_: (p, 0, 0)),
                blocks,
            ],
        ),
        out_shape=[
            pltpu.HBM((6, 128, ORDERS), F32),
            pltpu.HBM((8, 16, 6, 8, 128), BF16),
        ],
        compiler_params=vmem(56),
        name="legendre_filter",
    )(slots, orders, in_vmem(fourier), analysis, synthesis)


def inverse_kernel(y_ref, t_ref, o_ref, rows, cols):
    @pl.when(pl.program_id(0) == 0)
    def _():
        rows[...] = y_ref[...].astype(F32).reshape(rows.shape)
        for par in range(2):
            for ri in range(2):
                for a in range(4):
                    cols[par, PAIRS * ri:PAIRS * ri + PAIRS, 128 * a:128 * a + 128] = (
                        rows[pl.ds(8 * par + 2 * a + ri, PAIRS, stride=16), :].astype(BF16)
                    )

    width = NLON // 2 // 2
    sums = []
    for par in range(2):
        res = lax.dot_general(
            cols[par], t_ref[par].reshape(2 * PAIRS, width), (((0,), (0,)), ((), ())),
            preferred_element_type=F32,
        )
        sums.append(res * (2.0 / NLON))
    low = (sums[0] + sums[1]).astype(BF16)
    high = (sums[0] - sums[1]).astype(BF16)
    for b in range(width // 128):
        o_ref[0, b] = low[:, 128 * b:128 * b + 128].reshape(4, 128, 128)
        o_ref[1, b] = high[:, 128 * b:128 * b + 128].reshape(4, 128, 128)


def inverse(y, table):
    steps = 2
    width = NLON // 2 // steps
    out = pl.pallas_call(
        inverse_kernel,
        grid=(steps,),
        in_specs=[
            IN_VMEM,
            pl.BlockSpec((2, 2, PAIRS, width), lambda g: (0, 0, 0, g)),
        ],
        out_specs=pl.BlockSpec((2, width // 128, 4, 128, 128), lambda g: (0, g, 0, 0, 0)),
        out_shape=pltpu.HBM((2, 8, 4, 128, 128), BF16),
        scratch_shapes=[
            pltpu.VMEM((128 * 48, 128), F32),
            pltpu.VMEM((2, 2 * PAIRS, 512), BF16),
        ],
        compiler_params=vmem(56),
        name="inverse",
    )(in_vmem(y), table)
    return out.reshape(16, 4, 128, 128)


def update_kernel(se_ref, sp_ref, f_ref, old_ent, old_pres, oe_ref, op_ref):
    at = pl.ds(8 * pl.program_id(0), 8)
    oe_ref[...] = se_ref[...] + 0.5 * f_ref[0, at].astype(F32)
    op_ref[...] = sp_ref[...] + 0.5 * f_ref[1, at].astype(F32)


def update(start_entropy, start_pressure, filtered, ent, pres):
    whole = pl.BlockSpec((8, ROWS, COLS), lambda g: (g, 0, 0))
    anywhere = pl.BlockSpec(memory_space=pl.ANY)
    return pl.pallas_call(
        update_kernel,
        grid=(FLEV // 8,),
        in_specs=[whole, whole, IN_VMEM, anywhere, anywhere],
        out_specs=[whole, whole],
        out_shape=[pltpu.HBM((LEV, ROWS, COLS), F32)] * 2,
        input_output_aliases={3: 0, 4: 1},
        compiler_params=vmem(56),
        name="update",
    )(start_entropy, start_pressure, in_vmem(filtered), ent, pres)


def per_device(entropy, zonal_flux, meridional_flux, start_entropy, start_pressure, order_slot):
    n_lat = lax.axis_size("lat")
    n_lon = lax.axis_size("lonr")
    pairs = order_slot.reshape(PAIRS, 2)
    first_even = (pairs[:, 0] % 2) == 0
    even = jnp.where(first_even, pairs[:, 0], pairs[:, 1])
    odd = jnp.where(first_even, pairs[:, 1], pairs[:, 0])
    block = lax.axis_index("lat") * n_lon + lax.axis_index("lonr")
    both = jnp.stack((even, odd), axis=1)
    orders = lax.dynamic_slice_in_dim(both, block * 3, 3).reshape(6)
    swap = jnp.where(first_even, 0, 1).astype(jnp.int32)
    swap = lax.dynamic_slice_in_dim(swap, block * 3, 3)
    base = 2 * jnp.arange(3, dtype=jnp.int32)
    slots = jnp.stack((base + swap, base + 1 - swap), axis=1).reshape(6)

    first = (lax.axis_index("lat") * ROWS).astype(jnp.int32).reshape(1)
    east, west, south, north, fs, rc = edges(first, entropy, zonal_flux, meridional_flux)
    ring = range(n_lon)
    from_west = lax.ppermute(east, "lonr", [(i, (i + 1) % n_lon) for i in ring])
    from_east = lax.ppermute(west, "lonr", [((i + 1) % n_lon, i) for i in ring])
    from_north = lax.ppermute(south, "lat", [(i, i + 1) for i in range(n_lat - 1)])
    from_south = lax.ppermute(north, "lat", [(i + 1, i) for i in range(n_lat - 1)])
    table = fourier_table(jnp.stack((even, odd)))
    items, ent, pres = tendencies(
        entropy, zonal_flux, meridional_flux, from_west, from_east, west, from_north, from_south,
        fs, rc, start_entropy, start_pressure,
    )
    grid = lax.all_to_all(
        items.reshape(16, 4, ROWS, COLS), "lonr", split_axis=0, concat_axis=0, tiled=True
    )
    analysis, synthesis = legendre_tables(orders)
    spectral = forward(grid, table)
    spectral = lax.all_to_all(
        spectral, ("lat", "lonr"), split_axis=0, concat_axis=0, tiled=True
    )
    spectrum, back = legendre_filter(
        spectral.reshape(8, 16, 6, 8, 128), analysis, synthesis, orders, slots
    )
    back = lax.all_to_all(
        back.reshape(128, 48, 128), ("lat", "lonr"), split_axis=0, concat_axis=0, tiled=True
    )
    filtered = inverse(back, table)
    filtered = lax.all_to_all(filtered, "lonr", split_axis=0, concat_axis=0, tiled=True)
    new_entropy, new_pressure = update(
        start_entropy, start_pressure, filtered.reshape(2, FLEV, ROWS, COLS), ent, pres
    )
    return new_entropy, new_pressure, spectrum.reshape(6, 64, 2, ORDERS)


def solution(mesh):
    cube = P(None, "lat", "lonr")
    return jax.shard_map(
        per_device,
        mesh=mesh,
        in_specs=(cube, cube, cube, cube, cube, P()),
        out_specs=(cube, cube, P(("lat", "lonr"), None, None, None)),
        check_vma=False,
    )
```

time: 209 us -> 191 us (0.914)
  Pallas kernels: 76.6 us -> 62.9 us
  local copies, waits for them, and re-layouts: 13.6 us -> 9.2 us
  starting transfers between devices: 27.7 us -> 30 us
    pallas_call x4, Pallas kernels: 30.1 us -> 22.8 us  [the longest x1 6.31 us: edges(): pl.pallas_call(edges_kernel, grid=(1,), in_specs=[pl.BlockSpec(memory_spa...]
    all_to_all x1, starting transfers between devices: 8.48 us -> 14.2 us  [per_device(): lax.all_to_all(spectral, ('lat', 'lonr'), split_axis=0, concat_axis=0, ti...]
    pallas_call x1, Pallas kernels: 16.5 us -> 11 us  [tendencies(): pl.pallas_call(tend_kernel, grid=(LEV // 8,), in_specs=[whole, whole, who...]
    ppermute x1, waiting for transfers between devices: 0.01 us -> 4.1 us  [per_device(): lax.ppermute(north, 'lat', [(i + 1, i) for i in range(n_lat - 1)])]
    all_to_all x1, waiting for transfers between devices: 21.4 us -> 17.8 us  [per_device(): lax.all_to_all(items.reshape(16, 4, ROWS, COLS), 'lonr', split_axis=0, co...]
    all_to_all x1, starting transfers between devices: 6.99 us -> 3.9 us  [per_device(): lax.all_to_all(items.reshape(16, 4, ROWS, COLS), 'lonr', split_axis=0, co...]
    unnamed x20 -> x14, local copies, waits for them, and re-layouts: 3.83 us -> 0.76 us
    ppermute x1, waiting for transfers between devices: 2.22 us -> 0.01 us  [per_device(): from_east = lax.ppermute(west, 'lonr', [((i + 1) % n_lon, i) for i in ring])]
  transfers between devices with their start and end apart: 7 -> 7, of which waited for: 4 -> 4; matrix products, arithmetic and copies ran while one was open for 7% -> 8% of each run, Pallas kernels for 10% -> 11%
where the time goes in v2:
time: 191 us; the launch traced here: 190 us
  Pallas kernels  62.9 us (33%)
  waiting for transfers between devices  50.3 us (26%)
  blocking collectives  31.4 us (16%)
  starting transfers between devices  30 us (16%)
  local copies, waits for them, and re-layouts  9.2 us (5%)
  other arithmetic  5.88 us (3%)
    all_to_all x1, blocking collectives, per_device(): lax.all_to_all(back.reshape(128, 48, 128), ('lat', 'lonr'), split_axis=0,...  31.4 us
    all_to_all x1, waiting for transfers between devices, per_device(): lax.all_to_all(filtered, 'lonr', split_axis=0, concat_axis=0, tiled=True)  25.5 us
    all_to_all x1, waiting for transfers between devices, per_device(): lax.all_to_all(items.reshape(16, 4, ROWS, COLS), 'lonr', split_axis=0, co...  17.8 us
    pallas_call x1, Pallas kernels, legendre_tables(): pl.pallas_call(legendre_kernel, grid=(ORDERS // CHUNK,), in_specs=[smem,...  15.4 us
    all_to_all x1, starting transfers between devices, per_device(): lax.all_to_all(spectral, ('lat', 'lonr'), split_axis=0, concat_axis=0, ti...  14.2 us
    pallas_call x1, Pallas kernels, tendencies(): pl.pallas_call(tend_kernel, grid=(LEV // 8,), in_specs=[whole, whole, who...  11 us
    pallas_call x1, Pallas kernels, legendre_filter(): pl.pallas_call(filter_kernel, grid_spec=pltpu.PrefetchScalarGridSpec(num_...  8.79 us
    pallas_call x1, Pallas kernels, edges(): pl.pallas_call(edges_kernel, grid=(1,), in_specs=[pl.BlockSpec(memory_spa...  6.31 us
  transfers between devices with their start and end apart: 7, of which 4 were waited for; matrix products, arithmetic and copies ran while one was open for 8% of the time, Pallas kernels for 11%

profile of v2, /device:TPU:0, one launch (start us, length us, event | category | flops | bytes accessed | tf_op | source)
XLA Modules:
  0.0 190.5 jit_solution(6671667666040258642)
XLA Ops:
  0.6 6.3 %edges.1 = (f32[40,8,128]{2,1,0:T(8,128)}, f32[40,8,128]{2,1,0:T(8,128)}, f32[40,4,128]{2,1,0:T(4,128)}, f32[40,4,128]{2,1,0:T(4,128)}, f32[136,128]{1,0:T(8,128)}, /*index=5*/f32[128,128]{1,0:T(8,128)}) custom-call(s32[1]{0:T(128)} %bitcast.2.first_ref, f32[40,128,128]{2,1,0:T(8,128)} %s_ref.1, f32[40,128,128]{2,1,0:T(8,128)} %u_ref.1, f32[40,128,128]{2,1,0:T(8,128)} %v_ref.3), custom_call_target="tpu_custom_call" | custom-call | tf_op jit(solution)/shard_map/edges/pallas_call | solution.py:93
  7.0 1.8 collective-permute-start
  8.7 3.7 %collective-permute-start.1 = (f32[40,8,128]{2,1,0:T(8,128)}, f32[40,8,128]{2,1,0:T(8,128)S(1)}, u32[]{:S(2)}, u32[]{:S(2)}) collective-permute-start(f32[40,8,128]{2,1,0:T(8,128)} %get-tuple-element.19.ow_ref), channel_id=1, source_target_pairs={{1,0},{2,1},{3,2},{4,3},{5,4},{6,5},{7,6},{8,7},{9,8},{10,9},{11,1... | collective-permute-start | bytes 491528 | tf_op jit(solution)/shard_map/ppermute | solution.py:580
  12.4 1.5 collective-permute-start.2
  13.9 1.3 collective-permute-start.3
  15.2 0.0 collective-permute-done.2.hn_ref
  15.2 0.0 copy-start.3
  15.2 4.1 %collective-permute-done.3.hs_ref = f32[40,4,128]{2,1,0:T(4,128)S(1)} collective-permute-done((f32[40,4,128]{2,1,0:T(4,128)}, f32[40,4,128]{2,1,0:T(4,128)S(1)}, u32[]{:S(2)}, u32[]{:S(2)}) %collective-permute-start.3) | collective-permute-done | bytes 81952 | tf_op jit(solution)/shard_map/ppermute | solution.py:582
  19.3 0.0 collective-permute-done.hw_ref
  19.3 0.0 collective-permute-done.1.he_ref
  19.3 0.0 copy-start.2
  19.3 0.0 copy-done.3
  19.3 0.6 copy-done.4
  19.9 0.1 copy-done.1
  20.0 0.1 copy-done.2
  20.1 11.0 %tendencies.1 = (bf16[2,32,128,128]{3,2,1,0:T(8,128)(2,1)}, f32[40,128,128]{2,1,0:T(8,128)}, f32[40,128,128]{2,1,0:T(8,128)}) custom-call(f32[40,128,128]{2,1,0:T(8,128)} %s_ref.1, f32[40,128,128]{2,1,0:T(8,128)} %u_ref.1, f32[40,128,128]{2,1,0:T(8,128)} %v_ref.3, f32[40,8,128]{2,1,0:T(8,128)} %copy-done.1, f32[40,8,128]{2,1,0:T(8,128)} %copy-done.2, ...), custom_call_target="tpu_custom_call" | custom-call | tf_op jit(solution)/shard_map/tendencies/pallas_call | solution.py:233
  31.0 0.0 copy-start.6
  31.0 3.9 %all-to-all-start = ((bf16[16,4,128,128]{3,2,1,0:T(8,128)(2,1)}), bf16[16,4,128,128]{3,2,1,0:T(8,128)(2,1)S(1)}, u32[]{:S(2)}, u32[]{:S(2)}) async-start(bf16[16,4,128,128]{3,2,1,0:T(8,128)(2,1)} %bitcast.15), calls=%async_computation | async-start | bytes 4194304 | tf_op jit(solution)/shard_map/all_to_all | solution.py:588
  35.0 0.0 copy-done.6
  35.0 0.2 reshape.411
  35.2 0.3 slice_reduce_fusion
  35.5 0.2 fusion.14
  35.7 0.9 copy.19.turn_ref
  36.6 1.6 fusion.9
  38.2 0.9 pad_maximum_fusion.base_ref
  39.1 4.9 %longitude_table.1.t_ref = bf16[2,2,384,1024]{3,2,1,0:T(8,128)(2,1)} custom-call(f32[2,2,384,128]{3,2,1,0:T(8,128)} %pad_maximum_fusion.base_ref, f32[2,384,16]{2,1,0:T(8,128)} %copy.19.turn_ref), custom_call_target="tpu_custom_call" | custom-call | tf_op jit(solution)/shard_map/longitude_table/pallas_call | solution.py:284
  44.0 0.1 add_bitcast_fusion
  44.1 17.8 %all-to-all-done.x_ref = bf16[16,4,128,128]{3,2,1,0:T(8,128)(2,1)S(1)} async-done(((bf16[16,4,128,128]{3,2,1,0:T(8,128)(2,1)}), bf16[16,4,128,128]{3,2,1,0:T(8,128)(2,1)S(1)}, u32[]{:S(2)}, u32[]{:S(2)}) %all-to-all-start) | async-done | bytes 2097184 | tf_op jit(solution)/shard_map/all_to_all | solution.py:588
  61.9 5.6 %forward.1 = bf16[128,48,128]{2,1,0:T(8,128)(2,1)} custom-call(bf16[16,4,128,128]{3,2,1,0:T(8,128)(2,1)S(1)} %all-to-all-done.x_ref, bf16[2,2,384,1024]{3,2,1,0:T(8,128)(2,1)} %longitude_table.1.t_ref), custom_call_target="tpu_custom_call" | custom-call | tf_op jit(solution)/shard_map/forward/pallas_call | solution.py:320
  67.5 14.2 %all-to-all-start.1 = ((bf16[128,48,128]{2,1,0:T(8,128)(2,1)}), bf16[128,48,128]{2,1,0:T(8,128)(2,1)S(1)}, u32[]{:S(2)}, u32[]{:S(2)}) async-start(bf16[128,48,128]{2,1,0:T(8,128)(2,1)} %forward.1), calls=%async_computation.1 | async-start | bytes 3145728 | tf_op jit(solution)/shard_map/all_to_all | solution.py:593
  81.8 0.1 copy.15
  81.9 0.7 reshape.412.slot_ref
  82.5 0.1 copy.17
  82.6 0.1 copy.16
  82.7 0.1 fusion.28
  82.8 0.1 copy.18
  82.9 0.1 reshape.413.ord_ref
  83.0 0.1 multiply_add_fusion.1
  83.1 0.1 add.173
  83.2 0.1 add.174
  83.3 0.1 mul.200
  83.3 0.1 mul.201
  83.4 0.1 broadcast_in_dim.18
  83.5 0.1 broadcast_in_dim.19
  83.6 0.5 divide_sqrt_fusion
  84.1 0.3 sqrt.18
  84.3 0.3 reshape.422.a_ref
  84.6 0.6 mul.198.b_ref
  85.2 0.1 fusion.26
  85.3 0.7 fusion.25.w_ref
  86.0 0.1 fusion.35
  86.1 0.6 pad_maximum_fusion.2.start_ref
  86.7 0.6 tile.8
  87.3 0.7 broadcast_in_dim.20.m_ref
  87.9 0.0 copy-done
  87.9 15.4 %legendre_tables.1 = (bf16[6,768,512]{2,1,0:T(8,128)(2,1)}, bf16[6,768,512]{2,1,0:T(8,128)(2,1)}) custom-call(f32[4608]{0:T(1024)} %copy-done, f32[4608]{0:T(1024)} %mul.198.b_ref, s32[24,128]{1,0:T(8,128)} %broadcast_in_dim.20.m_ref, f32[24,128]{1,0:T(8,128)} %bitcast.18, f32[48,128]{1,0:T(8,128)} %pad_maximum_fusion.2.start_ref, f32[4,128]{1,0:T(4,128)} %fusion.25.w_ref), custom_call_target="tpu_custom_call" | custom-call | tf_op jit(solution)/shard_map/legendre_tables/pallas_call | solution.py:419
  103.3 2.9 %all-to-all-done.1 = bf16[128,48,128]{2,1,0:T(8,128)(2,1)S(1)} async-done(((bf16[128,48,128]{2,1,0:T(8,128)(2,1)}), bf16[128,48,128]{2,1,0:T(8,128)(2,1)S(1)}, u32[]{:S(2)}, u32[]{:S(2)}) %all-to-all-start.1) | async-done | bytes 1572896 | tf_op jit(solution)/shard_map/all_to_all | solution.py:593
  106.2 8.8 %legendre_filter.1 = (f32[6,128,768]{2,1,0:T(8,128)}, bf16[8,16,6,8,128]{4,3,2,1,0:T(8,128)(2,1)}) custom-call(s32[6]{0:T(128)} %reshape.412.slot_ref, s32[6]{0:T(128)} %copy-done.5, bf16[8,16,6,8,128]{4,3,2,1,0:T(8,128)(2,1)S(1)} %bitcast.13, bf16[6,768,512]{2,1,0:T(8,128)(2,1)} %get-tuple-element.25.ana_ref, bf16[6,768,512]{2,1,0:T(8,128)(2,1)} %get-tuple-element.26.syn_ref), custom_call_target="tpu_custom_call" | custom-call | tf_op jit(solution)/shard_map/legendre_filter/pallas_call | solution.py:472
  115.0 31.4 %all_to_all.20.y_ref = bf16[128,48,128]{2,1,0:T(8,128)(2,1)S(1)} all-to-all(bf16[128,48,128]{2,1,0:T(8,128)(2,1)} %bitcast.16), channel_id=1, replica_groups=mesh['lat'=8,'lonr'=16] {'lat','lonr'}, dimensions={0} | all-to-all | bytes 3145728 | tf_op jit(solution)/shard_map/all_to_all | solution.py:599
  146.4 6.2 %inverse.1 = bf16[2,8,4,128,128]{4,3,2,1,0:T(8,128)(2,1)} custom-call(bf16[128,48,128]{2,1,0:T(8,128)(2,1)S(1)} %all_to_all.20.y_ref, bf16[2,2,384,1024]{3,2,1,0:T(8,128)(2,1)} %longitude_table.1.t_ref), custom_call_target="tpu_custom_call" | custom-call | tf_op jit(solution)/shard_map/inverse/pallas_call | solution.py:521
  152.6 3.7 %all-to-all-start.3 = ((bf16[16,4,128,128]{3,2,1,0:T(8,128)(2,1)}), bf16[16,4,128,128]{3,2,1,0:T(8,128)(2,1)S(1)}, u32[]{:S(2)}, u32[]{:S(2)}) async-start(bf16[16,4,128,128]{3,2,1,0:T(8,128)(2,1)} %bitcast.14), calls=%async_computation.3 | async-start | bytes 4194304 | tf_op jit(solution)/shard_map/all_to_all | solution.py:603
  156.3 4.0 %reshape.420 = f32[6,64,2,768]{3,2,1,0:T(2,128)} reshape(f32[6,128,768]{2,1,0:T(8,128)} %get-tuple-element.32) | data formatting | bytes 4718592 | tf_op jit(solution)/shard_map/reshape | solution.py:607
  160.3 25.5 %all-to-all-done.3 = bf16[16,4,128,128]{3,2,1,0:T(8,128)(2,1)S(1)} async-done(((bf16[16,4,128,128]{3,2,1,0:T(8,128)(2,1)}), bf16[16,4,128,128]{3,2,1,0:T(8,128)(2,1)S(1)}, u32[]{:S(2)}, u32[]{:S(2)}) %all-to-all-start.3) | async-done | bytes 2097184 | tf_op jit(solution)/shard_map/all_to_all | solution.py:603
  185.8 4.7 %update.1 = (f32[40,128,128]{2,1,0:T(8,128)}, f32[40,128,128]{2,1,0:T(8,128)}) custom-call(f32[40,128,128]{2,1,0:T(8,128)} %se_ref.3, f32[40,128,128]{2,1,0:T(8,128)} %sp_ref.3, bf16[2,32,128,128]{3,2,1,0:T(8,128)(2,1)S(1)} %bitcast.12, f32[40,128,128]{2,1,0:T(8,128)} %get-tuple-element.28.old_ent, ...), custom_call_target="tpu_custom_call", output_to_operand_aliasing={{0}: (3, {}), {1}: (4, {})} | custom-call | tf_op jit(solution)/shard_map/update/pallas_call | solution.py:549
  (16 shorter events, 0.1 us)
Async XLA Ops:
  7.0 12.4 %collective-permute-start = (f32[40,8,128]{2,1,0:T(8,128)}, f32[40,8,128]{2,1,0:T(8,128)S(1)}, u32[]{:S(2)}, u32[]{:S(2)}) collective-permute-start(f32[40,8,128]{2,1,0:T(8,128)} %get-tuple-element.18), channel_id=1, source_target_pairs={{0,1},{1,2},{2,3},{3,4},{4,5},{5,6},{6,7},{7,8},{8,9},{9,10},{10,1... | collective-permute-start | bytes 491528 | tf_op jit(solution)/shard_map/ppermute | solution.py:579
  8.7 10.6 %collective-permute-start.1 = (f32[40,8,128]{2,1,0:T(8,128)}, f32[40,8,128]{2,1,0:T(8,128)S(1)}, u32[]{:S(2)}, u32[]{:S(2)}) collective-permute-start(f32[40,8,128]{2,1,0:T(8,128)} %get-tuple-element.19.ow_ref), channel_id=1, source_target_pairs={{1,0},{2,1},{3,2},{4,3},{5,4},{6,5},{7,6},{8,7},{9,8},{10,9},{11,1... | collective-permute-start | bytes 491528 | tf_op jit(solution)/shard_map/ppermute | solution.py:580
  12.4 2.8 %collective-permute-start.2 = (f32[40,4,128]{2,1,0:T(4,128)}, f32[40,4,128]{2,1,0:T(4,128)S(1)}, u32[]{:S(2)}, u32[]{:S(2)}) collective-permute-start(f32[40,4,128]{2,1,0:T(4,128)} %get-tuple-element.20), channel_id=1, source_target_pairs={{0,16},{16,32},{32,48},{48,64},{64,80},{80,96},{96,112},{1,17},{17... | collective-permute-start | bytes 245768 | tf_op jit(solution)/shard_map/ppermute | solution.py:581
  13.9 5.4 %collective-permute-start.3 = (f32[40,4,128]{2,1,0:T(4,128)}, f32[40,4,128]{2,1,0:T(4,128)S(1)}, u32[]{:S(2)}, u32[]{:S(2)}) collective-permute-start(f32[40,4,128]{2,1,0:T(4,128)} %get-tuple-element.21), channel_id=1, source_target_pairs={{16,0},{32,16},{48,32},{64,48},{80,64},{96,80},{112,96},{17,1},{33... | collective-permute-start | bytes 245768 | tf_op jit(solution)/shard_map/ppermute | solution.py:582
  15.2 4.1 %copy-start.3 = (f32[40,4,128]{2,1,0:T(4,128)}, f32[40,4,128]{2,1,0:T(4,128)S(1)}, u32[]{:S(2)}) copy-start(f32[40,4,128]{2,1,0:T(4,128)S(1)} %collective-permute-done.2.hn_ref) | copy-start | bytes 245764
  19.3 0.6 copy-start.4
  19.3 0.7 copy-start.1
  19.3 0.8 copy-start.2
  31.0 3.9 %copy-start.6 = (s32[768]{0:T(1024)S(1)}, s32[768]{0:T(1024)}, u32[]{:S(2)}) copy-start(s32[768]{0:T(1024)} %param.13) | copy-start | bytes 9220
  31.0 30.9 %all-to-all-start = ((bf16[16,4,128,128]{3,2,1,0:T(8,128)(2,1)}), bf16[16,4,128,128]{3,2,1,0:T(8,128)(2,1)S(1)}, u32[]{:S(2)}, u32[]{:S(2)}) async-start(bf16[16,4,128,128]{3,2,1,0:T(8,128)(2,1)} %bitcast.15), calls=%async_computation | async-start | bytes 4194304 | tf_op jit(solution)/shard_map/all_to_all | solution.py:588
  67.5 38.7 %all-to-all-start.1 = ((bf16[128,48,128]{2,1,0:T(8,128)(2,1)}), bf16[128,48,128]{2,1,0:T(8,128)(2,1)S(1)}, u32[]{:S(2)}, u32[]{:S(2)}) async-start(bf16[128,48,128]{2,1,0:T(8,128)(2,1)} %forward.1), calls=%async_computation.1 | async-start | bytes 3145728 | tf_op jit(solution)/shard_map/all_to_all | solution.py:593
  83.0 23.2 %copy-start.5 = (s32[6]{0:T(128)}, s32[6]{0:T(128)S(1)}, u32[]{:S(2)}) copy-start(s32[6]{0:T(128)S(1)} %reshape.413.ord_ref) | copy-start | bytes 76
  84.6 3.3 %copy-start = (f32[4608]{0:T(1024)}, f32[4608]{0:T(1024)S(1)}, u32[]{:S(2)}) copy-start(f32[4608]{0:T(1024)S(1)} %reshape.422.a_ref) | copy-start | bytes 55300
  152.6 33.2 %all-to-all-start.3 = ((bf16[16,4,128,128]{3,2,1,0:T(8,128)(2,1)}), bf16[16,4,128,128]{3,2,1,0:T(8,128)(2,1)S(1)}, u32[]{:S(2)}, u32[]{:S(2)}) async-start(bf16[16,4,128,128]{3,2,1,0:T(8,128)(2,1)} %bitcast.14), calls=%async_computation.3 | async-start | bytes 4194304 | tf_op jit(solution)/shard_map/all_to_all | solution.py:603

commit v3 on v2

--- a/solution.py
+++ b/solution.py
@@ -37,13 +37,22 @@
     return lax.broadcasted_iota(jnp.int32, shape, len(shape) - 1)
 
 
+def sine_of(n):
+    x = jnp.minimum(n, NLAT - n) * (math.pi / NLAT)
+    square = x * x
+    total = jnp.full_like(x, 1.0 / math.factorial(13))
+    for power in (11, 9, 7, 5, 3, 1):
+        total = total * square + (-1.0) ** (power // 2) / math.factorial(power)
+    return total * x
+
+
 def edges_kernel(
-    first_ref, s_any, u_any, v_ref, east_ref, west_ref, south_ref, north_ref, fs_ref, rc_ref,
+    first_ref, s_any, u_any, v_ref, side_ref, south_ref, north_ref, fs_ref, rc_ref,
     s_ref, u_ref, sems
 ):
     lane = lane_ids((8, 128))
-    group = lane >> 3
-    flux = (lane & 7) == 7
+    owner = ((lane + 3) & 127) >> 3
+    part = lane & 7
     parts = LEV // 8
 
     def fetch(n, g):
@@ -56,26 +65,21 @@
         for n in range(2):
             fetch(n, g).start()
     at = first_ref[0] - 8 + lax.broadcasted_iota(jnp.int32, (136, 128), 0)
-    sines = jnp.sin((math.pi / NLAT) * (at + 1).astype(F32))
+    sines = sine_of((at + 1).astype(F32))
     fs_ref[...] = jnp.where((at >= 0) & (at < NLAT - 1), sines, 0.0)
-    rc_ref[...] = 1.0 / jnp.sin((math.pi / NLAT) * (at[8:].astype(F32) + 0.5))
-
-    def one_pair(q, carry):
-        for half in range(2):
-            lev = 2 * q + half
-            east = jnp.zeros((8, 128), F32)
-            west = jnp.zeros((8, 128), F32)
+    rc_ref[...] = 1.0 / sine_of(at[8:].astype(F32) + 0.5)
+
+    def four_levels(q, carry):
+        for k in range(4):
+            lev = 4 * q + k
+            side = jnp.zeros((8, 128), F32)
+            flux = jnp.zeros((8, 128), F32)
             for i in range(16):
                 s = s_ref[lev, pl.ds(8 * i, 8), :]
                 u = u_ref[lev, pl.ds(8 * i, 8), :]
-                s_end = pltpu.roll(s, (8 * i + 7) % 128, 1)
-                u_end = pltpu.roll(u, (8 * i + 8) % 128, 1)
-                s_top = pltpu.roll(s, 8 * i, 1) if i else s
-                mine = group == i
-                east = jnp.where(mine, jnp.where(flux, u_end, s_end), east)
-                west = jnp.where(mine, s_top, west)
-            east_ref[lev] = east
-            west_ref[lev] = west
+                side = jnp.where(owner == i, pltpu.roll(s, 8 * i, 1) if i else s, side)
+                flux = jnp.where(owner == i, pltpu.roll(u, 8 * i, 1) if i else u, flux)
+            side_ref[lev] = jnp.where(part == 4, pltpu.roll(flux, 125, 1), side)
             south_ref[lev, 0:3, :] = s_ref[lev, 125:128, :]
             north_ref[lev] = s_ref[lev, 0:4, :]
         return carry
@@ -83,7 +87,7 @@
     for g in range(parts):
         for n in range(2):
             fetch(n, g).wait()
-        lax.fori_loop(4 * g, 4 * g + 4, one_pair, 0)
+        lax.fori_loop(2 * g, 2 * g + 2, four_levels, 0)
     for lev in range(LEV):
         south_ref[lev, 3:4, :] = v_ref[lev, 7:8, :]
 
@@ -94,10 +98,9 @@
         edges_kernel,
         grid=(1,),
         in_specs=[pl.BlockSpec(memory_space=pltpu.SMEM), anywhere, anywhere, pl.BlockSpec((LEV, 8, COLS), lambda g: (0, ROWS // 8 - 1, 0))],
-        out_specs=[pl.BlockSpec((LEV, n, 128), lambda g: (0, 0, 0)) for n in (8, 8, 4, 4)]
+        out_specs=[pl.BlockSpec((LEV, n, 128), lambda g: (0, 0, 0)) for n in (8, 4, 4)]
         + [pl.BlockSpec((n, 128), lambda g: (0, 0)) for n in (136, 128)],
         out_shape=[
-            pltpu.HBM((LEV, 8, 128), F32),
             pltpu.HBM((LEV, 8, 128), F32),
             pltpu.HBM((LEV, 4, 128), F32),
             pltpu.HBM((LEV, 4, 128), F32),
@@ -121,10 +124,10 @@
     for face in range(128):
         for shift, weight in weights.items():
             cell = face + shift
-            along[cell if 0 <= cell < 128 else 128 + cell % 128 if cell >= 128 else 128 + 7 + cell, face] = weight
+            along[cell if 0 <= cell < 128 else 128 + cell % 128 if cell >= 128 else 256 + cell, face] = weight
             across[face, cell if 0 <= cell < 128 else 128 + 4 + cell % 128 if cell >= 128 else 128 + 3 + cell] = weight
     along[128 + 3, 128 + 127] = 1.0
-    along[128 + 7, 128] = 1.0
+    along[128 + 124, 128] = 1.0
     return along, across
 
 
@@ -142,40 +145,36 @@
     small = lane_ids((8, 128)) & 7
     across = across_ref[...]
 
-    def prepare(q, carry):
-        for half in range(4):
-            lev = 4 * q + half
-            west = hw_ref[lev]
-            own = ow_ref[lev]
-            edge = stencil(
-                pltpu.roll(west, 127, 1), pltpu.roll(west, 126, 1), pltpu.roll(west, 125, 1),
-                pltpu.roll(own, 3, 1), pltpu.roll(own, 2, 1), pltpu.roll(own, 1, 1),
-            )
-            edge = edge * pltpu.roll(west, 124, 1)
-            rim = jnp.where(small < 3, he_ref[lev], jnp.where(small == 3, edge, west))
-            rim = jnp.concatenate([pltpu.roll(rim, (128 - 8 * i) % 128, 1) for i in range(16)])
-            s = s_ref[lev]
-            s_hi, s_lo = split(s)
-            r_hi, r_lo = split(rim)
-            at = pl.ds(pl.multiple_of(lev * 128, 128), 128)
-            cells[at, 0:128] = s_hi
-            cells[at, 128:256] = r_hi
-            cells[at, 256:384] = s_lo
-            cells[at, 384:512] = r_lo
-            h_hi, h_lo = split(jnp.concatenate([hn_ref[lev], hs_ref[lev]]))
-            n_face = jnp.dot(
-                across, jnp.concatenate([s_hi, s_lo, h_hi, h_lo]), preferred_element_type=F32
-            )
-            face[lev, :, 256:384] = n_face
-        return carry
-
-    lax.fori_loop(0, 2, prepare, 0)
-    for part in range(2):
+    def prepare(lev):
+        west = hw_ref[lev]
+        own = ow_ref[lev]
+        edge = stencil(
+            pltpu.roll(west, 6, 1), pltpu.roll(west, 5, 1), pltpu.roll(west, 4, 1),
+            pltpu.roll(own, 3, 1), pltpu.roll(own, 2, 1), pltpu.roll(own, 1, 1),
+        )
+        edge = edge * pltpu.roll(west, 7, 1)
+        rim = jnp.where(small < 3, he_ref[lev], jnp.where(small == 3, edge, west))
+        rim = jnp.concatenate([pltpu.roll(rim, (128 - 8 * i) % 128, 1) for i in range(16)])
+        s = s_ref[lev]
+        s_hi, s_lo = split(s)
+        r_hi, r_lo = split(rim)
+        at = slice(128 * lev, 128 * lev + 128)
+        cells[at, 0:128] = s_hi
+        cells[at, 128:256] = r_hi
+        cells[at, 256:384] = s_lo
+        cells[at, 384:512] = r_lo
+        h_hi, h_lo = split(jnp.concatenate([hn_ref[lev], hs_ref[lev]]))
+        face[lev, :, 256:384] = jnp.dot(
+            across, jnp.concatenate([s_hi, s_lo, h_hi, h_lo]), preferred_element_type=F32
+        )
+
+    def multiply(part):
         rows = slice(512 * part, 512 * part + 512)
         res = jnp.dot(cells[rows, :], along_ref[...], preferred_element_type=F32)
         face[4 * part:4 * part + 4, :, 0:256] = res.reshape(4, 128, 256)
 
-    def level(lev, half):
+    def level(lev, put):
+        half = lev % 4
         u = u_ref[lev]
         z = (u * (1.0 / 60.0)) * face[lev, :, 0:128]
         rim = face[lev, :, 128:256]
@@ -190,32 +189,37 @@
         mext[half, 1, 7:8, :] = fv_top
         mext[half, 1, 8:136, :] = fv
         rc = rc_ref[...]
-        ent = -(dz + (m - mext[half, 0, 7:135, :]) * rc)
-        pres = -0.3 * (du + (fv - mext[half, 1, 7:135, :]) * rc)
-        return ent, pres
+        put(
+            lev,
+            -(dz + (m - mext[half, 0, 7:135, :]) * rc),
+            -0.3 * (du + (fv - mext[half, 1, 7:135, :]) * rc),
+        )
+
+    def put_items(lev, ent, pres):
+        item_ref[0, lev] = ent.astype(BF16)
+        item_ref[1, lev] = pres.astype(BF16)
+
+    def put_tail(lev, ent, pres):
+        ent_ref[lev] = se_ref[lev] + 0.5 * ent
+        pres_ref[lev] = sp_ref[lev] + 0.5 * pres
+
+    def run(put):
+        for lev in range(4):
+            prepare(lev)
+        multiply(0)
+        for lev in range(4, 8):
+            prepare(lev)
+        multiply(1)
+        for lev in range(8):
+            level(lev, put)
 
     @pl.when(step < FLEV // 8)
     def _():
-        def body(q, carry):
-            for half in range(4):
-                ent, pres = level(4 * q + half, half)
-                item_ref[0, 4 * q + half] = ent.astype(BF16)
-                item_ref[1, 4 * q + half] = pres.astype(BF16)
-            return carry
-
-        lax.fori_loop(0, 2, body, 0)
+        run(put_items)
 
     @pl.when(step == FLEV // 8)
     def _():
-        def body(q, carry):
-            for half in range(4):
-                ent, pres = level(4 * q + half, half)
-                lev = 4 * q + half
-                ent_ref[lev] = se_ref[lev] + 0.5 * ent
-                pres_ref[lev] = sp_ref[lev] + 0.5 * pres
-            return carry
-
-        lax.fori_loop(0, 2, body, 0)
+        run(put_tail)
 
 
 def tendencies(
@@ -294,15 +298,25 @@
     )(base, turn)
 
 
-def forward_kernel(x_ref, t_ref, o_ref, fold, rows):
+def forward_kernel(x_ref, t_any, o_ref, fold, rows, t_ref, sems):
     par = pl.program_id(0)
+
+    def fetch(n):
+        return pltpu.make_async_copy(t_any.at[n], t_ref.at[n], sems.at[n])
+
+    @pl.when(par == 0)
+    def _():
+        fetch(0).start()
+        fetch(1).start()
+
     for a in range(4):
         for b in range(8):
             lo = x_ref[b, a]
             hi = x_ref[b + 8, a]
             fold[128 * a:128 * a + 128, 128 * b:128 * b + 128] = lo + jnp.where(par == 0, hi, -hi)
+    fetch(par).wait()
     res = lax.dot_general(
-        t_ref[0].reshape(2 * PAIRS, NLON // 2), fold[...], (((1,), (1,)), ((), ())),
+        t_ref[par].reshape(2 * PAIRS, NLON // 2), fold[...], (((1,), (1,)), ((), ())),
         preferred_element_type=F32,
     )
     for ri in range(2):
@@ -322,13 +336,15 @@
         grid=(2,),
         in_specs=[
             IN_VMEM,
-            pl.BlockSpec((1, 2, PAIRS, NLON // 2), lambda g: (g, 0, 0, 0)),
+            pl.BlockSpec(memory_space=pl.ANY),
         ],
         out_specs=pl.BlockSpec((128, 48, 128), lambda g: (0, 0, 0)),
         out_shape=pltpu.HBM((128, 48, 128), BF16),
         scratch_shapes=[
             pltpu.VMEM((512, NLON // 2), BF16),
             pltpu.VMEM((16 * PAIRS, 128), F32),
+            pltpu.VMEM((2, 2, PAIRS, NLON // 2), BF16),
+            pltpu.SemaphoreType.DMA((2,)),
         ],
         compiler_params=vmem(56),
         name="forward",
@@ -489,9 +505,21 @@
     )(slots, orders, in_vmem(fourier), analysis, synthesis)
 
 
-def inverse_kernel(y_ref, t_ref, o_ref, rows, cols):
-    @pl.when(pl.program_id(0) == 0)
+def inverse_kernel(y_ref, t_any, o_ref, rows, cols, t_ref, sems):
+    step = pl.program_id(0)
+    width = NLON // 2 // 2
+
+    def fetch(n, par):
+        at = pl.ds(pl.multiple_of(n * width, width), width)
+        return pltpu.make_async_copy(
+            t_any.at[par, :, :, at], t_ref.at[n, par], sems.at[n, par]
+        )
+
+    @pl.when(step == 0)
     def _():
+        for n in range(2):
+            for par in range(2):
+                fetch(n, par).start()
         rows[...] = y_ref[...].astype(F32).reshape(rows.shape)
         for par in range(2):
             for ri in range(2):
@@ -500,11 +528,11 @@
                         rows[pl.ds(8 * par + 2 * a + ri, PAIRS, stride=16), :].astype(BF16)
                     )
 
-    width = NLON // 2 // 2
     sums = []
     for par in range(2):
+        fetch(step, par).wait()
         res = lax.dot_general(
-            cols[par], t_ref[par].reshape(2 * PAIRS, width), (((0,), (0,)), ((), ())),
+            cols[par], t_ref[step, par].reshape(2 * PAIRS, width), (((0,), (0,)), ((), ())),
             preferred_element_type=F32,
         )
         sums.append(res * (2.0 / NLON))
@@ -523,13 +551,15 @@
         grid=(steps,),
         in_specs=[
             IN_VMEM,
-            pl.BlockSpec((2, 2, PAIRS, width), lambda g: (0, 0, 0, g)),
+            pl.BlockSpec(memory_space=pl.ANY),
         ],
         out_specs=pl.BlockSpec((2, width // 128, 4, 128, 128), lambda g: (0, g, 0, 0, 0)),
         out_shape=pltpu.HBM((2, 8, 4, 128, 128), BF16),
         scratch_shapes=[
             pltpu.VMEM((128 * 48, 128), F32),
             pltpu.VMEM((2, 2 * PAIRS, 512), BF16),
+            pltpu.VMEM((steps, 2, 2, PAIRS, width), BF16),
+            pltpu.SemaphoreType.DMA((steps, 2)),
         ],
         compiler_params=vmem(56),
         name="inverse",
@@ -574,15 +604,15 @@
     slots = jnp.stack((base + swap, base + 1 - swap), axis=1).reshape(6)
 
     first = (lax.axis_index("lat") * ROWS).astype(jnp.int32).reshape(1)
-    east, west, south, north, fs, rc = edges(first, entropy, zonal_flux, meridional_flux)
+    side, south, north, fs, rc = edges(first, entropy, zonal_flux, meridional_flux)
     ring = range(n_lon)
-    from_west = lax.ppermute(east, "lonr", [(i, (i + 1) % n_lon) for i in ring])
-    from_east = lax.ppermute(west, "lonr", [((i + 1) % n_lon, i) for i in ring])
+    from_west = lax.ppermute(side, "lonr", [(i, (i + 1) % n_lon) for i in ring])
+    from_east = lax.ppermute(side, "lonr", [((i + 1) % n_lon, i) for i in ring])
     from_north = lax.ppermute(south, "lat", [(i, i + 1) for i in range(n_lat - 1)])
     from_south = lax.ppermute(north, "lat", [(i + 1, i) for i in range(n_lat - 1)])
     table = fourier_table(jnp.stack((even, odd)))
     items, ent, pres = tendencies(
-        entropy, zonal_flux, meridional_flux, from_west, from_east, west, from_north, from_south,
+        entropy, zonal_flux, meridional_flux, from_west, from_east, side, from_north, from_south,
         fs, rc, start_entropy, start_pressure,
     )
     grid = lax.all_to_all(

time: 191 us -> 192 us (level)
  Pallas kernels: 62.9 us -> 59.6 us
  waiting for transfers between devices: 50.3 us -> 52.5 us
    ppermute x2, waiting for transfers between devices: 0.01 us -> 2.36 us  [the longest x1 2.36 us: per_device(): from_west = lax.ppermute(side, 'lonr', [(i, (i + 1) % n_lon) for i in ring])]
  transfers between devices with their start and end apart: 7 -> 7, of which waited for: 4 -> 5; matrix products, arithmetic and copies ran while one was open for 8% -> 8% of each run, Pallas kernels for 11% -> 11%
where the time goes in v3:
time: 192 us; the launch traced here: 191 us
  Pallas kernels  59.6 us (31%)
  waiting for transfers between devices  52.5 us (27%)
  blocking collectives  31.4 us (16%)
  starting transfers between devices  31.3 us (16%)
  local copies, waits for them, and re-layouts  9.12 us (5%)
  other arithmetic  5.88 us (3%)
    all_to_all x1, blocking collectives, per_device(): lax.all_to_all(back.reshape(128, 48, 128), ('lat', 'lonr'), split_axis=0,...  31.4 us
    all_to_all x1, waiting for transfers between devices, per_device(): lax.all_to_all(filtered, 'lonr', split_axis=0, concat_axis=0, tiled=True)  25.5 us
    all_to_all x1, waiting for transfers between devices, per_device(): lax.all_to_all(items.reshape(16, 4, ROWS, COLS), 'lonr', split_axis=0, co...  17.9 us
    pallas_call x1, Pallas kernels, legendre_tables(): pl.pallas_call(legendre_kernel, grid=(ORDERS // CHUNK,), in_specs=[smem,...  15.4 us
    all_to_all x1, starting transfers between devices, per_device(): lax.all_to_all(spectral, ('lat', 'lonr'), split_axis=0, concat_axis=0, ti...  15 us
    pallas_call x1, Pallas kernels, tendencies(): pl.pallas_call(tend_kernel, grid=(LEV // 8,), in_specs=[whole, whole, who...  9.56 us
    pallas_call x1, Pallas kernels, legendre_filter(): pl.pallas_call(filter_kernel, grid_spec=pltpu.PrefetchScalarGridSpec(num_...  8.79 us
    pallas_call x1, Pallas kernels, forward(): pl.pallas_call(forward_kernel, grid=(2,), in_specs=[IN_VMEM, pl.BlockSpec...  5.61 us
  transfers between devices with their start and end apart: 7, of which 5 were waited for; matrix products, arithmetic and copies ran while one was open for 8% of the time, Pallas kernels for 11%

profile of v3, /device:TPU:0, one launch (start us, length us, event | category | flops | bytes accessed | tf_op | source)
XLA Modules:
  0.0 190.6 jit_solution(2422408733811177227)
XLA Ops:
  0.6 5.4 %edges.1 = (f32[40,8,128]{2,1,0:T(8,128)}, f32[40,4,128]{2,1,0:T(4,128)}, f32[40,4,128]{2,1,0:T(4,128)}, f32[136,128]{1,0:T(8,128)}, f32[128,128]{1,0:T(8,128)}) custom-call(s32[1]{0:T(128)} %bitcast.2.first_ref, f32[40,128,128]{2,1,0:T(8,128)} %s_ref.1, f32[40,128,128]{2,1,0:T(8,128)} %u_ref.1, f32[40,128,128]{2,1,0:T(8,128)} %v_ref.3), custom_call_target="tpu_custom_call" | custom-call | tf_op jit(solution)/shard_map/edges/pallas_call | solution.py:97
  6.0 5.4 %collective-permute-start.1 = (f32[40,8,128]{2,1,0:T(8,128)}, f32[40,8,128]{2,1,0:T(8,128)S(1)}, u32[]{:S(2)}, u32[]{:S(2)}) collective-permute-start(f32[40,8,128]{2,1,0:T(8,128)} %get-tuple-element.17.ow_ref), channel_id=1, source_target_pairs={{1,0},{2,1},{3,2},{4,3},{5,4},{6,5},{7,6},{8,7},{9,8},{10,9},{11,1... | collective-permute-start | bytes 491528 | tf_op jit(solution)/shard_map/ppermute | solution.py:610
  11.4 0.0 collective-permute-start
  11.4 1.5 collective-permute-start.2
  12.9 1.3 collective-permute-start.3
  14.2 0.0 collective-permute-done.2.hn_ref
  14.2 0.0 copy-start.3
  14.2 4.0 %collective-permute-done.3.hs_ref = f32[40,4,128]{2,1,0:T(4,128)S(1)} collective-permute-done((f32[40,4,128]{2,1,0:T(4,128)}, f32[40,4,128]{2,1,0:T(4,128)S(1)}, u32[]{:S(2)}, u32[]{:S(2)}) %collective-permute-start.3) | collective-permute-done | bytes 81952 | tf_op jit(solution)/shard_map/ppermute | solution.py:612
  18.2 0.0 collective-permute-done.1.he_ref
  18.2 2.4 %collective-permute-done.hw_ref = f32[40,8,128]{2,1,0:T(8,128)S(1)} collective-permute-done((f32[40,8,128]{2,1,0:T(8,128)}, f32[40,8,128]{2,1,0:T(8,128)S(1)}, u32[]{:S(2)}, u32[]{:S(2)}) %collective-permute-start) | collective-permute-done | bytes 163872 | tf_op jit(solution)/shard_map/ppermute | solution.py:609
  20.6 0.0 copy-done.3
  20.6 0.0 copy-done.4
  20.6 0.0 copy-done.1
  20.6 0.7 copy-done.2
  21.3 9.6 %tendencies.1 = (bf16[2,32,128,128]{3,2,1,0:T(8,128)(2,1)}, f32[40,128,128]{2,1,0:T(8,128)}, f32[40,128,128]{2,1,0:T(8,128)}) custom-call(f32[40,128,128]{2,1,0:T(8,128)} %s_ref.1, f32[40,128,128]{2,1,0:T(8,128)} %u_ref.1, f32[40,128,128]{2,1,0:T(8,128)} %v_ref.3, f32[40,8,128]{2,1,0:T(8,128)} %copy-done.2, f32[40,8,128]{2,1,0:T(8,128)} %copy-done.1, ...), custom_call_target="tpu_custom_call" | custom-call | tf_op jit(solution)/shard_map/tendencies/pallas_call | solution.py:237
  30.8 0.0 copy-start.6
  30.9 4.5 %all-to-all-start = ((bf16[16,4,128,128]{3,2,1,0:T(8,128)(2,1)}), bf16[16,4,128,128]{3,2,1,0:T(8,128)(2,1)S(1)}, u32[]{:S(2)}, u32[]{:S(2)}) async-start(bf16[16,4,128,128]{3,2,1,0:T(8,128)(2,1)} %bitcast.15), calls=%async_computation | async-start | bytes 4194304 | tf_op jit(solution)/shard_map/all_to_all | solution.py:618
  35.3 0.0 copy-done.6
  35.3 0.2 reshape.411
  35.5 0.3 slice_reduce_fusion
  35.8 0.2 fusion.14
  36.0 0.9 copy.19.turn_ref
  37.0 1.6 fusion.9
  38.6 0.9 pad_maximum_fusion.base_ref
  39.5 4.9 %longitude_table.1.t_any = bf16[2,2,384,1024]{3,2,1,0:T(8,128)(2,1)} custom-call(f32[2,2,384,128]{3,2,1,0:T(8,128)} %pad_maximum_fusion.base_ref, f32[2,384,16]{2,1,0:T(8,128)} %copy.19.turn_ref), custom_call_target="tpu_custom_call" | custom-call | tf_op jit(solution)/shard_map/longitude_table/pallas_call | solution.py:288
  44.4 0.1 add_bitcast_fusion
  44.5 17.9 %all-to-all-done.x_ref = bf16[16,4,128,128]{3,2,1,0:T(8,128)(2,1)S(1)} async-done(((bf16[16,4,128,128]{3,2,1,0:T(8,128)(2,1)}), bf16[16,4,128,128]{3,2,1,0:T(8,128)(2,1)S(1)}, u32[]{:S(2)}, u32[]{:S(2)}) %all-to-all-start) | async-done | bytes 2097184 | tf_op jit(solution)/shard_map/all_to_all | solution.py:618
  62.3 5.6 %forward.1 = bf16[128,48,128]{2,1,0:T(8,128)(2,1)} custom-call(bf16[16,4,128,128]{3,2,1,0:T(8,128)(2,1)S(1)} %all-to-all-done.x_ref, bf16[2,2,384,1024]{3,2,1,0:T(8,128)(2,1)} %longitude_table.1.t_any), custom_call_target="tpu_custom_call" | custom-call | tf_op jit(solution)/shard_map/forward/pallas_call | solution.py:334
  68.0 15.0 %all-to-all-start.1 = ((bf16[128,48,128]{2,1,0:T(8,128)(2,1)}), bf16[128,48,128]{2,1,0:T(8,128)(2,1)S(1)}, u32[]{:S(2)}, u32[]{:S(2)}) async-start(bf16[128,48,128]{2,1,0:T(8,128)(2,1)} %forward.1), calls=%async_computation.1 | async-start | bytes 3145728 | tf_op jit(solution)/shard_map/all_to_all | solution.py:623
  83.0 0.1 copy.15
  83.1 0.7 reshape.412.slot_ref
  83.8 0.1 copy.17
  83.8 0.1 copy.16
  84.0 0.1 fusion.28
  84.1 0.1 copy.18
  84.2 0.1 reshape.413.ord_ref
  84.3 0.1 multiply_add_fusion.1
  84.3 0.1 add.173
  84.4 0.1 add.174
  84.5 0.1 mul.200
  84.6 0.1 mul.201
  84.6 0.1 broadcast_in_dim.18
  84.7 0.1 broadcast_in_dim.19
  84.8 0.5 divide_sqrt_fusion
  85.3 0.3 sqrt.18
  85.6 0.3 reshape.422.a_ref
  85.8 0.6 mul.198.b_ref
  86.4 0.1 fusion.26
  86.5 0.7 fusion.25.w_ref
  87.2 0.1 fusion.35
  87.3 0.6 pad_maximum_fusion.2.start_ref
  87.9 0.6 tile.8
  88.5 0.7 broadcast_in_dim.20.m_ref
  89.2 0.0 copy-done
  89.2 15.4 %legendre_tables.1 = (bf16[6,768,512]{2,1,0:T(8,128)(2,1)}, bf16[6,768,512]{2,1,0:T(8,128)(2,1)}) custom-call(f32[4608]{0:T(1024)} %copy-done, f32[4608]{0:T(1024)} %mul.198.b_ref, s32[24,128]{1,0:T(8,128)} %broadcast_in_dim.20.m_ref, f32[24,128]{1,0:T(8,128)} %bitcast.18, f32[48,128]{1,0:T(8,128)} %pad_maximum_fusion.2.start_ref, f32[4,128]{1,0:T(4,128)} %fusion.25.w_ref), custom_call_target="tpu_custom_call" | custom-call | tf_op jit(solution)/shard_map/legendre_tables/pallas_call | solution.py:435
  104.6 2.7 %all-to-all-done.1 = bf16[128,48,128]{2,1,0:T(8,128)(2,1)S(1)} async-done(((bf16[128,48,128]{2,1,0:T(8,128)(2,1)}), bf16[128,48,128]{2,1,0:T(8,128)(2,1)S(1)}, u32[]{:S(2)}, u32[]{:S(2)}) %all-to-all-start.1) | async-done | bytes 1572896 | tf_op jit(solution)/shard_map/all_to_all | solution.py:623
  107.3 0.0 copy-done.5
  107.3 8.8 %legendre_filter.1 = (f32[6,128,768]{2,1,0:T(8,128)}, bf16[8,16,6,8,128]{4,3,2,1,0:T(8,128)(2,1)}) custom-call(s32[6]{0:T(128)} %reshape.412.slot_ref, s32[6]{0:T(128)} %copy-done.5, bf16[8,16,6,8,128]{4,3,2,1,0:T(8,128)(2,1)S(1)} %bitcast.13, bf16[6,768,512]{2,1,0:T(8,128)(2,1)} %get-tuple-element.23.ana_ref, bf16[6,768,512]{2,1,0:T(8,128)(2,1)} %get-tuple-element.24.syn_ref), custom_call_target="tpu_custom_call" | custom-call | tf_op jit(solution)/shard_map/legendre_filter/pallas_call | solution.py:488
  116.1 31.4 %all_to_all.20.y_ref = bf16[128,48,128]{2,1,0:T(8,128)(2,1)S(1)} all-to-all(bf16[128,48,128]{2,1,0:T(8,128)(2,1)} %bitcast.16), channel_id=1, replica_groups=mesh['lat'=8,'lonr'=16] {'lat','lonr'}, dimensions={0} | all-to-all | bytes 3145728 | tf_op jit(solution)/shard_map/all_to_all | solution.py:629
  147.4 5.3 %inverse.1 = bf16[2,8,4,128,128]{4,3,2,1,0:T(8,128)(2,1)} custom-call(bf16[128,48,128]{2,1,0:T(8,128)(2,1)S(1)} %all_to_all.20.y_ref, bf16[2,2,384,1024]{3,2,1,0:T(8,128)(2,1)} %longitude_table.1.t_any), custom_call_target="tpu_custom_call" | custom-call | tf_op jit(solution)/shard_map/inverse/pallas_call | solution.py:549
  152.7 3.7 %all-to-all-start.3 = ((bf16[16,4,128,128]{3,2,1,0:T(8,128)(2,1)}), bf16[16,4,128,128]{3,2,1,0:T(8,128)(2,1)S(1)}, u32[]{:S(2)}, u32[]{:S(2)}) async-start(bf16[16,4,128,128]{3,2,1,0:T(8,128)(2,1)} %bitcast.14), calls=%async_computation.3 | async-start | bytes 4194304 | tf_op jit(solution)/shard_map/all_to_all | solution.py:633
  156.5 4.0 %reshape.420 = f32[6,64,2,768]{3,2,1,0:T(2,128)} reshape(f32[6,128,768]{2,1,0:T(8,128)} %get-tuple-element.30) | data formatting | bytes 4718592 | tf_op jit(solution)/shard_map/reshape | solution.py:637
  160.5 25.5 %all-to-all-done.3 = bf16[16,4,128,128]{3,2,1,0:T(8,128)(2,1)S(1)} async-done(((bf16[16,4,128,128]{3,2,1,0:T(8,128)(2,1)}), bf16[16,4,128,128]{3,2,1,0:T(8,128)(2,1)S(1)}, u32[]{:S(2)}, u32[]{:S(2)}) %all-to-all-start.3) | async-done | bytes 2097184 | tf_op jit(solution)/shard_map/all_to_all | solution.py:633
  186.0 4.7 %update.1 = (f32[40,128,128]{2,1,0:T(8,128)}, f32[40,128,128]{2,1,0:T(8,128)}) custom-call(f32[40,128,128]{2,1,0:T(8,128)} %se_ref.3, f32[40,128,128]{2,1,0:T(8,128)} %sp_ref.3, bf16[2,32,128,128]{3,2,1,0:T(8,128)(2,1)S(1)} %bitcast.12, f32[40,128,128]{2,1,0:T(8,128)} %get-tuple-element.26.old_ent, ...), custom_call_target="tpu_custom_call", output_to_operand_aliasing={{0}: (3, {}), {1}: (4, {})} | custom-call | tf_op jit(solution)/shard_map/update/pallas_call | solution.py:579
  (16 shorter events, 0.1 us)
Async XLA Ops:
  6.0 12.2 %collective-permute-start.1 = (f32[40,8,128]{2,1,0:T(8,128)}, f32[40,8,128]{2,1,0:T(8,128)S(1)}, u32[]{:S(2)}, u32[]{:S(2)}) collective-permute-start(f32[40,8,128]{2,1,0:T(8,128)} %get-tuple-element.17.ow_ref), channel_id=1, source_target_pairs={{1,0},{2,1},{3,2},{4,3},{5,4},{6,5},{7,6},{8,7},{9,8},{10,9},{11,1... | collective-permute-start | bytes 491528 | tf_op jit(solution)/shard_map/ppermute | solution.py:610
  11.4 9.2 %collective-permute-start = (f32[40,8,128]{2,1,0:T(8,128)}, f32[40,8,128]{2,1,0:T(8,128)S(1)}, u32[]{:S(2)}, u32[]{:S(2)}) collective-permute-start(f32[40,8,128]{2,1,0:T(8,128)} %get-tuple-element.17.ow_ref), channel_id=1, source_target_pairs={{0,1},{1,2},{2,3},{3,4},{4,5},{5,6},{6,7},{7,8},{8,9},{9,10},{10,1... | collective-permute-start | bytes 491528 | tf_op jit(solution)/shard_map/ppermute | solution.py:609
  11.4 2.8 %collective-permute-start.2 = (f32[40,4,128]{2,1,0:T(4,128)}, f32[40,4,128]{2,1,0:T(4,128)S(1)}, u32[]{:S(2)}, u32[]{:S(2)}) collective-permute-start(f32[40,4,128]{2,1,0:T(4,128)} %get-tuple-element.18), channel_id=1, source_target_pairs={{0,16},{16,32},{32,48},{48,64},{64,80},{80,96},{96,112},{1,17},{17... | collective-permute-start | bytes 245768 | tf_op jit(solution)/shard_map/ppermute | solution.py:611
  12.9 5.4 %collective-permute-start.3 = (f32[40,4,128]{2,1,0:T(4,128)}, f32[40,4,128]{2,1,0:T(4,128)S(1)}, u32[]{:S(2)}, u32[]{:S(2)}) collective-permute-start(f32[40,4,128]{2,1,0:T(4,128)} %get-tuple-element.19), channel_id=1, source_target_pairs={{16,0},{32,16},{48,32},{64,48},{80,64},{96,80},{112,96},{17,1},{33... | collective-permute-start | bytes 245768 | tf_op jit(solution)/shard_map/ppermute | solution.py:612
  14.2 6.4 %copy-start.3 = (f32[40,4,128]{2,1,0:T(4,128)}, f32[40,4,128]{2,1,0:T(4,128)S(1)}, u32[]{:S(2)}) copy-start(f32[40,4,128]{2,1,0:T(4,128)S(1)} %collective-permute-done.2.hn_ref) | copy-start | bytes 245764
  18.2 2.4 %copy-start.4 = (f32[40,4,128]{2,1,0:T(4,128)}, f32[40,4,128]{2,1,0:T(4,128)S(1)}, u32[]{:S(2)}) copy-start(f32[40,4,128]{2,1,0:T(4,128)S(1)} %collective-permute-done.3.hs_ref) | copy-start | bytes 245764
  18.2 2.4 %copy-start.1 = (f32[40,8,128]{2,1,0:T(8,128)}, f32[40,8,128]{2,1,0:T(8,128)S(1)}, u32[]{:S(2)}) copy-start(f32[40,8,128]{2,1,0:T(8,128)S(1)} %collective-permute-done.1.he_ref) | copy-start | bytes 491524
  20.6 0.7 copy-start.2
  30.8 4.5 %copy-start.6 = (s32[768]{0:T(1024)S(1)}, s32[768]{0:T(1024)}, u32[]{:S(2)}) copy-start(s32[768]{0:T(1024)} %param.13) | copy-start | bytes 9220
  30.9 31.5 %all-to-all-start = ((bf16[16,4,128,128]{3,2,1,0:T(8,128)(2,1)}), bf16[16,4,128,128]{3,2,1,0:T(8,128)(2,1)S(1)}, u32[]{:S(2)}, u32[]{:S(2)}) async-start(bf16[16,4,128,128]{3,2,1,0:T(8,128)(2,1)} %bitcast.15), calls=%async_computation | async-start | bytes 4194304 | tf_op jit(solution)/shard_map/all_to_all | solution.py:618
  68.0 39.3 %all-to-all-start.1 = ((bf16[128,48,128]{2,1,0:T(8,128)(2,1)}), bf16[128,48,128]{2,1,0:T(8,128)(2,1)S(1)}, u32[]{:S(2)}, u32[]{:S(2)}) async-start(bf16[128,48,128]{2,1,0:T(8,128)(2,1)} %forward.1), calls=%async_computation.1 | async-start | bytes 3145728 | tf_op jit(solution)/shard_map/all_to_all | solution.py:623
  84.2 23.0 %copy-start.5 = (s32[6]{0:T(128)}, s32[6]{0:T(128)S(1)}, u32[]{:S(2)}) copy-start(s32[6]{0:T(128)S(1)} %reshape.413.ord_ref) | copy-start | bytes 76
  85.8 3.3 %copy-start = (f32[4608]{0:T(1024)}, f32[4608]{0:T(1024)S(1)}, u32[]{:S(2)}) copy-start(f32[4608]{0:T(1024)S(1)} %reshape.422.a_ref) | copy-start | bytes 55300
  152.7 33.2 %all-to-all-start.3 = ((bf16[16,4,128,128]{3,2,1,0:T(8,128)(2,1)}), bf16[16,4,128,128]{3,2,1,0:T(8,128)(2,1)S(1)}, u32[]{:S(2)}, u32[]{:S(2)}) async-start(bf16[16,4,128,128]{3,2,1,0:T(8,128)(2,1)} %bitcast.14), calls=%async_computation.3 | async-start | bytes 4194304 | tf_op jit(solution)/shard_map/all_to_all | solution.py:633

commit v4 on v3

--- a/solution.py
+++ b/solution.py
@@ -1,3 +1,4 @@
+import functools
 import math
 
 import jax
@@ -136,26 +137,26 @@
     return high, (x - high.astype(F32)).astype(BF16)
 
 
-def tend_kernel(
-    s_ref, u_ref, v_ref, hw_ref, he_ref, ow_ref, hn_ref, hs_ref, fs_ref, rc_ref, along_ref, across_ref,
-    se_ref, sp_ref, item_ref, ent_ref, pres_ref, cells, face, mext,
-):
-    step = pl.program_id(0)
+def tend_kernel(*refs):
+    (s_ref, u_ref, v_ref, hw_ref, he_ref, ow_ref, hn_ref, hs_ref, fs_ref, rc_ref, along_ref,
+     across_ref) = refs[:12]
+    cells, face, mext = refs[-3:]
+    wide = s_ref.shape[1]
     lane = lane_ids((ROWS, COLS))
     small = lane_ids((8, 128)) & 7
     across = across_ref[...]
 
     def prepare(lev):
-        west = hw_ref[lev]
-        own = ow_ref[lev]
+        west = hw_ref[lev // wide, lev % wide]
+        own = ow_ref[lev // wide, lev % wide]
         edge = stencil(
             pltpu.roll(west, 6, 1), pltpu.roll(west, 5, 1), pltpu.roll(west, 4, 1),
             pltpu.roll(own, 3, 1), pltpu.roll(own, 2, 1), pltpu.roll(own, 1, 1),
         )
         edge = edge * pltpu.roll(west, 7, 1)
-        rim = jnp.where(small < 3, he_ref[lev], jnp.where(small == 3, edge, west))
+        rim = jnp.where(small < 3, he_ref[lev // wide, lev % wide], jnp.where(small == 3, edge, west))
         rim = jnp.concatenate([pltpu.roll(rim, (128 - 8 * i) % 128, 1) for i in range(16)])
-        s = s_ref[lev]
+        s = s_ref[lev // wide, lev % wide]
         s_hi, s_lo = split(s)
         r_hi, r_lo = split(rim)
         at = slice(128 * lev, 128 * lev + 128)
@@ -163,7 +164,7 @@
         cells[at, 128:256] = r_hi
         cells[at, 256:384] = s_lo
         cells[at, 384:512] = r_lo
-        h_hi, h_lo = split(jnp.concatenate([hn_ref[lev], hs_ref[lev]]))
+        h_hi, h_lo = split(jnp.concatenate([hn_ref[lev // wide, lev % wide], hs_ref[lev // wide, lev % wide]]))
         face[lev, :, 256:384] = jnp.dot(
             across, jnp.concatenate([s_hi, s_lo, h_hi, h_lo]), preferred_element_type=F32
         )
@@ -173,95 +174,98 @@
         res = jnp.dot(cells[rows, :], along_ref[...], preferred_element_type=F32)
         face[4 * part:4 * part + 4, :, 0:256] = res.reshape(4, 128, 256)
 
-    def level(lev, put):
+    def level(lev):
         half = lev % 4
-        u = u_ref[lev]
+        u = u_ref[lev // wide, lev % wide]
         z = (u * (1.0 / 60.0)) * face[lev, :, 0:128]
         rim = face[lev, :, 128:256]
         dz = z - pltpu.roll(jnp.where(lane == COLS - 1, rim, z), 1, 1)
         du = u - jnp.where(lane == 0, rim, pltpu.roll(u, 1, 1))
-        fv = v_ref[lev] * fs_ref[8:136, :]
-        fv_top = hn_ref[lev, 3:4, :] * fs_ref[7:8, :]
-        top = [hn_ref[lev, o:o + 1, :] for o in range(3)] + [s_ref[lev, o:o + 1, :] for o in range(3)]
+        fv = v_ref[lev // wide, lev % wide] * fs_ref[8:136, :]
+        fv_top = hn_ref[lev // wide, lev % wide, 3:4, :] * fs_ref[7:8, :]
+        top = [hn_ref[lev // wide, lev % wide, o:o + 1, :] for o in range(3)] + [s_ref[lev // wide, lev % wide, o:o + 1, :] for o in range(3)]
         m = fv * (face[lev, :, 256:384] * (1.0 / 60.0))
         mext[half, 0, 7:8, :] = fv_top * stencil(*top)
         mext[half, 0, 8:136, :] = m
         mext[half, 1, 7:8, :] = fv_top
         mext[half, 1, 8:136, :] = fv
         rc = rc_ref[...]
-        put(
-            lev,
-            -(dz + (m - mext[half, 0, 7:135, :]) * rc),
-            -0.3 * (du + (fv - mext[half, 1, 7:135, :]) * rc),
-        )
-
-    def put_items(lev, ent, pres):
-        item_ref[0, lev] = ent.astype(BF16)
-        item_ref[1, lev] = pres.astype(BF16)
-
-    def put_tail(lev, ent, pres):
-        ent_ref[lev] = se_ref[lev] + 0.5 * ent
-        pres_ref[lev] = sp_ref[lev] + 0.5 * pres
-
-    def run(put):
-        for lev in range(4):
-            prepare(lev)
-        multiply(0)
-        for lev in range(4, 8):
-            prepare(lev)
-        multiply(1)
-        for lev in range(8):
-            level(lev, put)
-
-    @pl.when(step < FLEV // 8)
-    def _():
-        run(put_items)
-
-    @pl.when(step == FLEV // 8)
-    def _():
-        run(put_tail)
-
-
-def tendencies(
-    s, u, v, from_west, from_east, own_west, from_north, from_south, fs, rc, start_entropy, start_pressure
-):
-    whole = pl.BlockSpec((8, ROWS, COLS), lambda g: (g, 0, 0))
-    packed = pl.BlockSpec((8, 8, 128), lambda g: (g, 0, 0))
-    rows4 = pl.BlockSpec((8, 4, 128), lambda g: (g, 0, 0))
-    tail = pl.BlockSpec((8, ROWS, COLS), lambda g: (FLEV // 8, 0, 0))
+        ent = -(dz + (m - mext[half, 0, 7:135, :]) * rc)
+        pres = -0.3 * (du + (fv - mext[half, 1, 7:135, :]) * rc)
+        return ent, pres
+
+    def put(lev, ent, pres):
+        if len(refs) == 16:
+            item_ref = refs[12]
+            item_ref[0, lev // 2, lev % 2] = ent.astype(BF16)
+            item_ref[1, lev // 2, lev % 2] = pres.astype(BF16)
+        else:
+            se_ref, sp_ref, ent_ref, pres_ref = refs[12:16]
+            ent_ref[lev] = se_ref[lev] + 0.5 * ent
+            pres_ref[lev] = sp_ref[lev] + 0.5 * pres
+
+    for lev in range(4):
+        prepare(lev)
+    multiply(0)
+    for lev in range(4, 8):
+        prepare(lev)
+    multiply(1)
+    for lev in range(8):
+        put(lev, *level(lev))
+
+
+def tendencies(fields, halos, factors, starts=None, half=None):
+    groups = LEV // 4
+    if half is None:
+        deep, wide, steps = 2, 4, 1
+
+        def at(g):
+            return (FLEV // 8, 0)
+    else:
+        deep, wide, steps = 4, 2, 2
+
+        def at(g):
+            return (g, half)
+
+    def spec(rows):
+        return pl.BlockSpec((deep, wide, rows, 128), lambda g: at(g) + (0, 0))
+
     along, across = stencil_matrices()
     along = jnp.asarray(np.concatenate((along, along)), BF16)
     across = np.concatenate(
         (across[:, :128], across[:, :128], across[:, 128:], across[:, 128:]), axis=1
     )
+    operands = [x.reshape(groups, 4, *x.shape[1:]) for x in (*fields, *halos)]
+    in_specs = [spec(x.shape[2]) for x in operands]
+    operands += [*factors, along, jnp.asarray(across, BF16)]
+    in_specs += [
+        pl.BlockSpec((136, 128), lambda g: (0, 0)),
+        pl.BlockSpec((128, 128), lambda g: (0, 0)),
+        pl.BlockSpec((512, 256), lambda g: (0, 0)),
+        pl.BlockSpec((128, 272), lambda g: (0, 0)),
+    ]
+    if half is None:
+        tail = pl.BlockSpec((8, ROWS, COLS), lambda g: (FLEV // 8, 0, 0))
+        operands += starts
+        in_specs += [tail, tail]
+        out_specs = [tail, tail]
+        out_shape = [pltpu.HBM((LEV, ROWS, COLS), F32)] * 2
+    else:
+        out_specs = pl.BlockSpec((2, 4, 2, ROWS, COLS), lambda g: (0, g, 0, 0, 0))
+        out_shape = pltpu.HBM((2, 8, 2, ROWS, COLS), BF16)
     return pl.pallas_call(
         tend_kernel,
-        grid=(LEV // 8,),
-        in_specs=[
-            whole, whole, whole, packed, packed, packed, rows4, rows4,
-            pl.BlockSpec((136, 128), lambda g: (0, 0)),
-            pl.BlockSpec((128, 128), lambda g: (0, 0)),
-            pl.BlockSpec((512, 256), lambda g: (0, 0)),
-            pl.BlockSpec((128, 272), lambda g: (0, 0)),
-            tail, tail,
-        ],
-        out_specs=[
-            pl.BlockSpec((2, 8, ROWS, COLS), lambda g: (0, jnp.minimum(g, FLEV // 8 - 1), 0, 0)),
-            tail, tail,
-        ],
-        out_shape=[
-            pltpu.HBM((2, FLEV, ROWS, COLS), BF16),
-            pltpu.HBM((LEV, ROWS, COLS), F32),
-            pltpu.HBM((LEV, ROWS, COLS), F32),
-        ],
+        grid=(steps,),
+        in_specs=in_specs,
+        out_specs=out_specs,
+        out_shape=out_shape,
         scratch_shapes=[
             pltpu.VMEM((1024, 512), BF16),
             pltpu.VMEM((8, 128, 384), F32),
             pltpu.VMEM((4, 2, 136, 128), F32),
         ],
-        name="tendencies",
-    )(s, u, v, from_west, from_east, own_west, from_north, from_south, fs, rc,
-      along, jnp.asarray(across, BF16), start_entropy, start_pressure)
+        name="tendencies" if half is not None else "tail",
+    )(*operands)
 
 
 def table_kernel(base_ref, turn_ref, out_ref):
@@ -298,7 +302,11 @@
     )(base, turn)
 
 
-def forward_kernel(x_ref, t_any, o_ref, fold, rows, t_ref, sems):
+def forward_kernel(half, *refs):
+    if half == 0:
+        x_ref, t_any, rows, fold, t_ref, sems = refs
+    else:
+        x_ref, t_any, r_any, o_ref, fold, t_ref, sems, rows = refs
     par = pl.program_id(0)
 
     def fetch(n):
@@ -307,9 +315,11 @@
     @pl.when(par == 0)
     def _():
         fetch(0).start()
+        if half:
+            pltpu.make_async_copy(r_any, rows, sems.at[2]).start()
         fetch(1).start()
 
-    for a in range(4):
+    for a in range(2):
         for b in range(8):
             lo = x_ref[b, a]
             hi = x_ref[b + 8, a]
@@ -319,36 +329,50 @@
         t_ref[par].reshape(2 * PAIRS, NLON // 2), fold[...], (((1,), (1,)), ((), ())),
         preferred_element_type=F32,
     )
+    if half:
+        @pl.when(par == 0)
+        def _():
+            pltpu.make_async_copy(r_any, rows, sems.at[2]).wait()
+
     for ri in range(2):
-        for a in range(4):
-            rows[pl.ds(8 * par + 2 * a + ri, PAIRS, stride=16), :] = (
+        for a in range(2):
+            rows[pl.ds(8 * par + 2 * (2 * half + a) + ri, PAIRS, stride=16), :] = (
                 res[PAIRS * ri:PAIRS * ri + PAIRS, 128 * a:128 * a + 128]
             )
 
-    @pl.when(par == 1)
-    def _():
-        o_ref[...] = rows[...].reshape(o_ref.shape).astype(BF16)
-
-
-def forward(x, table):
+    if half:
+        @pl.when(par == 1)
+        def _():
+            o_ref[...] = rows[...].reshape(o_ref.shape).astype(BF16)
+
+
+def forward(x, table, rows=None):
+    half = 0 if rows is None else 1
+    anywhere = pl.BlockSpec(memory_space=pl.ANY)
+    buffers = [
+        pltpu.VMEM((256, NLON // 2), BF16),
+        pltpu.VMEM((2, 2, PAIRS, NLON // 2), BF16),
+        pltpu.SemaphoreType.DMA((3,)),
+    ]
+    if half == 0:
+        operands = [in_vmem(x), table]
+        out_specs = pl.BlockSpec((16 * PAIRS, 128), lambda g: (0, 0))
+        out_shape = pltpu.HBM((16 * PAIRS, 128), F32)
+    else:
+        operands = [in_vmem(x), table, rows]
+        out_specs = pl.BlockSpec((128, 48, 128), lambda g: (0, 0, 0))
+        out_shape = pltpu.HBM((128, 48, 128), BF16)
+        buffers.append(pltpu.VMEM((16 * PAIRS, 128), F32))
     return pl.pallas_call(
-        forward_kernel,
+        functools.partial(forward_kernel, half),
         grid=(2,),
-        in_specs=[
-            IN_VMEM,
-            pl.BlockSpec(memory_space=pl.ANY),
-        ],
-        out_specs=pl.BlockSpec((128, 48, 128), lambda g: (0, 0, 0)),
-        out_shape=pltpu.HBM((128, 48, 128), BF16),
-        scratch_shapes=[
-            pltpu.VMEM((512, NLON // 2), BF16),
-            pltpu.VMEM((16 * PAIRS, 128), F32),
-            pltpu.VMEM((2, 2, PAIRS, NLON // 2), BF16),
-            pltpu.SemaphoreType.DMA((2,)),
-        ],
+        in_specs=[IN_VMEM] + [anywhere] * (len(operands) - 1),
+        out_specs=out_specs,
+        out_shape=out_shape,
+        scratch_shapes=buffers,
         compiler_params=vmem(56),
         name="forward",
-    )(in_vmem(x), table)
+    )(*operands)
 
 
 CHUNK = 128
@@ -450,8 +474,11 @@
 def filter_kernel(slot_ref, ord_ref, f_ref, ana_ref, syn_ref, spec_ref, back_ref):
     sub = lax.broadcasted_iota(jnp.int32, (128, 128), 0)
     flip = jnp.where(sub + lane_ids((128, 128)) == 127, 1.0, 0.0).astype(BF16)
-    for k in range(2):
-        o = 2 * pl.program_id(0) + k
+    pair = pl.program_id(0)
+    above = (ord_ref[2 * pair] < ORDERS // 2).astype(jnp.int32)
+    for k, low in ((above, ORDERS // 2), (1 - above, 0)):
+        width = ORDERS - low
+        o = 2 * pair + k
         order = ord_ref[o]
         plus = []
         minus = []
@@ -465,13 +492,15 @@
             [jnp.concatenate(plus, axis=1), jnp.concatenate(minus, axis=1)], axis=0
         )
         coef = lax.dot_general(
-            both, ana_ref[k], (((1,), (1,)), ((), ())), preferred_element_type=F32
+            both, ana_ref[k, low:, :], (((1,), (1,)), ((), ())), preferred_element_type=F32
         )
-        even = ((lane_ids((128, ORDERS)) - order) & 1) == 0
+        even = ((lane_ids((128, width)) - order) & 1) == 0
         spec = jnp.where(even, coef[:128], coef[128:])
-        spec_ref[slot_ref[o] & 1] = spec
+        if low:
+            spec_ref[slot_ref[o] & 1, :, :low] = jnp.zeros((128, low), F32)
+        spec_ref[slot_ref[o] & 1, :, low:] = spec
         parts = jnp.concatenate([jnp.where(even, spec, 0.0), jnp.where(even, 0.0, spec)], axis=0)
-        grid = jnp.dot(parts.astype(BF16), syn_ref[k], preferred_element_type=F32)
+        grid = jnp.dot(parts.astype(BF16), syn_ref[k, low:, :], preferred_element_type=F32)
         factor = jnp.where(order == 0, 0.5, 1.0)
         north = (grid[:128] + grid[128:]) * factor
         south = ((grid[:128] - grid[128:]) * factor).astype(BF16)
@@ -611,15 +640,20 @@
     from_north = lax.ppermute(south, "lat", [(i, i + 1) for i in range(n_lat - 1)])
     from_south = lax.ppermute(north, "lat", [(i + 1, i) for i in range(n_lat - 1)])
     table = fourier_table(jnp.stack((even, odd)))
-    items, ent, pres = tendencies(
-        entropy, zonal_flux, meridional_flux, from_west, from_east, side, from_north, from_south,
-        fs, rc, start_entropy, start_pressure,
-    )
-    grid = lax.all_to_all(
-        items.reshape(16, 4, ROWS, COLS), "lonr", split_axis=0, concat_axis=0, tiled=True
-    )
+    fields = (entropy, zonal_flux, meridional_flux)
+    halos = (from_west, from_east, side, from_north, from_south)
+
+    def exchange(items):
+        return lax.all_to_all(
+            items.reshape(16, 2, ROWS, COLS), "lonr", split_axis=0, concat_axis=0, tiled=True
+        )
+
+    first_items = exchange(tendencies(fields, halos, (fs, rc), half=0))
+    second_items = exchange(tendencies(fields, halos, (fs, rc), half=1))
+    ent, pres = tendencies(fields, halos, (fs, rc), starts=[start_entropy, start_pressure])
+    rows = forward(first_items, table)
+    spectral = forward(second_items, table, rows)
     analysis, synthesis = legendre_tables(orders)
-    spectral = forward(grid, table)
     spectral = lax.all_to_all(
         spectral, ("lat", "lonr"), split_axis=0, concat_axis=0, tiled=True
     )

time: 192 us -> 190 us (0.990)
  Pallas kernels: 59.6 us -> 66.8 us
  waiting for transfers between devices: 52.5 us -> 46.4 us
  starting transfers between devices: 31.3 us -> 29.1 us
    pallas_call x2 -> x5, Pallas kernels: 15.2 us -> 22.7 us  [the longest x3 12.7 us: tendencies(): pl.pallas_call(tend_kernel, grid=(steps,), in_specs=in_specs, out_specs=o...]
    all_to_all x1, starting transfers between devices: 15 us -> 8.35 us  [per_device(): lax.all_to_all(spectral, ('lat', 'lonr'), split_axis=0, concat_axis=0, ti...]
    all_to_all x1 -> x2, starting transfers between devices: 4.46 us -> 8.79 us  [exchange(): lax.all_to_all(items.reshape(16, 2, ROWS, COLS), 'lonr', split_axis=0, co...]
    all_to_all x1, waiting for transfers between devices: 25.5 us -> 21.6 us  [per_device(): lax.all_to_all(filtered, 'lonr', split_axis=0, concat_axis=0, tiled=True)]
    ppermute x1, waiting for transfers between devices: 2.36 us -> 0.01 us  [per_device(): from_west = lax.ppermute(side, 'lonr', [(i, (i + 1) % n_lon) for i in ring])]
    all_to_all x1 -> x2, waiting for transfers between devices: 17.9 us -> 17.9 us  [exchange(): lax.all_to_all(items.reshape(16, 2, ROWS, COLS), 'lonr', split_axis=0, co...]
  transfers between devices with their start and end apart: 7 -> 8, of which waited for: 5 -> 5; matrix products, arithmetic and copies ran while one was open for 8% -> 7% of each run, Pallas kernels for 11% -> 18%
where the time goes in v4:
time: 190 us
  Pallas kernels  66.8 us (35%)
  waiting for transfers between devices  46.4 us (24%)
  blocking collectives  31.3 us (16%)
  starting transfers between devices  29.1 us (15%)
  local copies, waits for them, and re-layouts  9.1 us (5%)
  other arithmetic  5.86 us (3%)
    all_to_all x1, blocking collectives, per_device(): lax.all_to_all(back.reshape(128, 48, 128), ('lat', 'lonr'), split_axis=0,...  31.3 us
    all_to_all x1, waiting for transfers between devices, per_device(): lax.all_to_all(filtered, 'lonr', split_axis=0, concat_axis=0, tiled=True)  21.6 us
    all_to_all x2, waiting for transfers between devices, exchange(): lax.all_to_all(items.reshape(16, 2, ROWS, COLS), 'lonr', split_axis=0, co...  17.9 us
    pallas_call x1, Pallas kernels, legendre_tables(): pl.pallas_call(legendre_kernel, grid=(ORDERS // CHUNK,), in_specs=[smem,...  15.4 us
    pallas_call x3, Pallas kernels, tendencies(): pl.pallas_call(tend_kernel, grid=(steps,), in_specs=in_specs, out_specs=o...  12.7 us
    pallas_call x2, Pallas kernels, forward(): pl.pallas_call(functools.partial(forward_kernel, half), grid=(2,), in_spe...  9.99 us
    all_to_all x2, starting transfers between devices, exchange(): lax.all_to_all(items.reshape(16, 2, ROWS, COLS), 'lonr', split_axis=0, co...  8.79 us
    pallas_call x1, Pallas kernels, legendre_filter(): pl.pallas_call(filter_kernel, grid_spec=pltpu.PrefetchScalarGridSpec(num_...  8.57 us
  transfers between devices with their start and end apart: 8, of which 5 were waited for; matrix products, arithmetic and copies ran while one was open for 7% of the time, Pallas kernels for 18%

profile of v4, /device:TPU:0, one launch (start us, length us, event | category | flops | bytes accessed | tf_op | source)
XLA Modules:
  0.0 189.5 jit_solution(4666070069021058189)
XLA Ops:
  0.6 5.4 %edges.1 = (f32[40,8,128]{2,1,0:T(8,128)}, f32[40,4,128]{2,1,0:T(4,128)}, f32[40,4,128]{2,1,0:T(4,128)}, f32[136,128]{1,0:T(8,128)}, f32[128,128]{1,0:T(8,128)}) custom-call(s32[1]{0:T(128)} %bitcast.5.first_ref, f32[40,128,128]{2,1,0:T(8,128)} %s_any.1, f32[40,128,128]{2,1,0:T(8,128)} %u_any.1, f32[40,128,128]{2,1,0:T(8,128)} %v_ref.1), custom_call_target="tpu_custom_call" | custom-call | tf_op jit(solution)/shard_map/edges/pallas_call | solution.py:98
  6.0 1.8 collective-permute-start
  7.8 3.7 %collective-permute-start.1 = (f32[40,8,128]{2,1,0:T(8,128)}, f32[40,8,128]{2,1,0:T(8,128)S(1)}, u32[]{:S(2)}, u32[]{:S(2)}) collective-permute-start(f32[40,8,128]{2,1,0:T(8,128)} %get-tuple-element.16), channel_id=1, source_target_pairs={{1,0},{2,1},{3,2},{4,3},{5,4},{6,5},{7,6},{8,7},{9,8},{10,9},{11,1... | collective-permute-start | bytes 491528 | tf_op jit(solution)/shard_map/ppermute | solution.py:639
  11.5 1.5 collective-permute-start.2
  12.9 1.3 collective-permute-start.3
  14.2 0.0 collective-permute-done.2
  14.3 0.0 copy-start.2
  14.3 4.1 %collective-permute-done.3 = f32[40,4,128]{2,1,0:T(4,128)S(1)} collective-permute-done((f32[40,4,128]{2,1,0:T(4,128)}, f32[40,4,128]{2,1,0:T(4,128)S(1)}, u32[]{:S(2)}, u32[]{:S(2)}) %collective-permute-start.3) | collective-permute-done | bytes 81952 | tf_op jit(solution)/shard_map/ppermute | solution.py:641
  18.4 0.0 collective-permute-done
  18.4 0.0 collective-permute-done.1
  18.4 0.6 copy-done.3
  19.0 0.1 copy-done
  19.1 0.0 copy-done.1
  19.1 4.4 %tendencies.3 = bf16[2,8,2,128,128]{4,3,2,1,0:T(8,128)(2,1)} custom-call(f32[10,4,128,128]{3,2,1,0:T(8,128)} %bitcast.23, f32[10,4,128,128]{3,2,1,0:T(8,128)} %bitcast.26, f32[10,4,128,128]{3,2,1,0:T(8,128)} %bitcast.29, f32[10,4,8,128]{3,2,1,0:T(8,128)} %bitcast.39, f32[10,4,8,128]{3,2,1,0:T(8,128)} %bitcast.42, f32[10,4,8,128]{3,2,1,0:T(8,128)} %bitcast.36, ...), custom_call_target="tpu_custom_call" | custom-call | tf_op jit(solution)/shard_map/tendencies/pallas_call | solution.py:256
  23.5 3.9 %all-to-all-start.1 = ((bf16[16,2,128,128]{3,2,1,0:T(8,128)(2,1)}), bf16[16,2,128,128]{3,2,1,0:T(8,128)(2,1)S(1)}, u32[]{:S(2)}, u32[]{:S(2)}) async-start(bf16[16,2,128,128]{3,2,1,0:T(8,128)(2,1)} %bitcast.34), calls=%async_computation.1 | async-start | bytes 2097152 | tf_op jit(solution)/shard_map/all_to_all | solution.py:647
  27.4 0.2 reshape.454
  27.6 0.3 slice_reduce_fusion
  27.9 4.4 %tendencies.2 = bf16[2,8,2,128,128]{4,3,2,1,0:T(8,128)(2,1)} custom-call(f32[10,4,128,128]{3,2,1,0:T(8,128)} %bitcast.24, f32[10,4,128,128]{3,2,1,0:T(8,128)} %bitcast.27, f32[10,4,128,128]{3,2,1,0:T(8,128)} %bitcast.30, f32[10,4,8,128]{3,2,1,0:T(8,128)} %bitcast.40, f32[10,4,8,128]{3,2,1,0:T(8,128)} %bitcast.43, f32[10,4,8,128]{3,2,1,0:T(8,128)} %bitcast.37, ...), custom_call_target="tpu_custom_call" | custom-call | tf_op jit(solution)/shard_map/tendencies/pallas_call | solution.py:256
  32.3 11.6 %all-to-all-done.1.refs_0_ = bf16[16,2,128,128]{3,2,1,0:T(8,128)(2,1)S(1)} async-done(((bf16[16,2,128,128]{3,2,1,0:T(8,128)(2,1)}), bf16[16,2,128,128]{3,2,1,0:T(8,128)(2,1)S(1)}, u32[]{:S(2)}, u32[]{:S(2)}) %all-to-all-start.1) | async-done | bytes 1048608 | tf_op jit(solution)/shard_map/all_to_all | solution.py:647
  44.0 4.9 %all-to-all-start = ((bf16[16,2,128,128]{3,2,1,0:T(8,128)(2,1)}), bf16[16,2,128,128]{3,2,1,0:T(8,128)(2,1)S(1)}, u32[]{:S(2)}, u32[]{:S(2)}) async-start(bf16[16,2,128,128]{3,2,1,0:T(8,128)(2,1)} %bitcast.33), calls=%async_computation | async-start | bytes 2097152 | tf_op jit(solution)/shard_map/all_to_all | solution.py:647
  48.9 0.2 fusion.14
  49.1 0.9 copy.23.turn_ref
  50.0 1.6 fusion.9
  51.6 0.9 pad_maximum_fusion.base_ref
  52.5 4.9 %longitude_table.1.refs_1_.t_any = bf16[2,2,384,1024]{3,2,1,0:T(8,128)(2,1)} custom-call(f32[2,2,384,128]{3,2,1,0:T(8,128)} %pad_maximum_fusion.base_ref, f32[2,384,16]{2,1,0:T(8,128)} %copy.23.turn_ref), custom_call_target="tpu_custom_call" | custom-call | tf_op jit(solution)/shard_map/longitude_table/pallas_call | solution.py:292
  57.4 0.1 add_bitcast_fusion
  57.5 4.7 %forward.2.refs_2_ = f32[6144,128]{1,0:T(8,128)} custom-call(bf16[16,2,128,128]{3,2,1,0:T(8,128)(2,1)S(1)} %all-to-all-done.1.refs_0_, bf16[2,2,384,1024]{3,2,1,0:T(8,128)(2,1)} %longitude_table.1.refs_1_.t_any), custom_call_target="tpu_custom_call" | custom-call | tf_op jit(solution)/shard_map/forward/pallas_call | solution.py:366
  62.2 6.3 %all-to-all-done.refs_0_ = bf16[16,2,128,128]{3,2,1,0:T(8,128)(2,1)S(1)} async-done(((bf16[16,2,128,128]{3,2,1,0:T(8,128)(2,1)}), bf16[16,2,128,128]{3,2,1,0:T(8,128)(2,1)S(1)}, u32[]{:S(2)}, u32[]{:S(2)}) %all-to-all-start) | async-done | bytes 1048608 | tf_op jit(solution)/shard_map/all_to_all | solution.py:647
  68.5 5.3 %forward.3 = bf16[128,48,128]{2,1,0:T(8,128)(2,1)} custom-call(bf16[16,2,128,128]{3,2,1,0:T(8,128)(2,1)S(1)} %all-to-all-done.refs_0_, bf16[2,2,384,1024]{3,2,1,0:T(8,128)(2,1)} %longitude_table.1.refs_1_.t_any, f32[6144,128]{1,0:T(8,128)} %forward.2.refs_2_), custom_call_target="tpu_custom_call" | custom-call | tf_op jit(solution)/shard_map/forward/pallas_call | solution.py:366
  73.8 8.4 %all-to-all-start.2 = ((bf16[128,48,128]{2,1,0:T(8,128)(2,1)}), bf16[128,48,128]{2,1,0:T(8,128)(2,1)S(1)}, u32[]{:S(2)}, u32[]{:S(2)}) async-start(bf16[128,48,128]{2,1,0:T(8,128)(2,1)} %forward.3), calls=%async_computation.2 | async-start | bytes 3145728 | tf_op jit(solution)/shard_map/all_to_all | solution.py:657
  82.2 0.1 copy.19
  82.3 0.6 reshape.455.slot_ref
  82.9 0.1 copy.20
  83.0 0.1 copy.21
  83.1 0.1 fusion.28
  83.2 0.1 copy.22
  83.3 0.1 reshape.456.ord_ref
  83.4 0.1 multiply_add_fusion.1
  83.5 0.5 divide_sqrt_fusion
  84.0 0.3 reshape.474.a_ref
  84.2 0.3 sqrt.18
  84.5 0.1 broadcast_in_dim.18
  84.6 0.1 broadcast_in_dim.19
  84.6 0.1 mul.200
  84.7 0.1 mul.201
  84.8 0.1 add.173
  84.9 0.1 add.174
  84.9 0.6 mul.198.b_ref
  85.6 0.1 fusion.26
  85.7 0.7 fusion.25.w_ref
  86.3 0.1 fusion.35
  86.4 0.6 pad_maximum_fusion.2.start_ref
  87.0 0.7 broadcast_in_dim.20.m_ref
  87.7 0.6 tile.8
  88.3 15.4 %legendre_tables.1 = (bf16[6,768,512]{2,1,0:T(8,128)(2,1)}, bf16[6,768,512]{2,1,0:T(8,128)(2,1)}) custom-call(f32[4608]{0:T(1024)} %copy-done.4, f32[4608]{0:T(1024)} %mul.198.b_ref, s32[24,128]{1,0:T(8,128)} %broadcast_in_dim.20.m_ref, f32[24,128]{1,0:T(8,128)} %bitcast.52, f32[48,128]{1,0:T(8,128)} %pad_maximum_fusion.2.start_ref, f32[4,128]{1,0:T(4,128)} %fusion.25.w_ref), custom_call_target="tpu_custom_call" | custom-call | tf_op jit(solution)/shard_map/legendre_tables/pallas_call | solution.py:459
  103.7 2.8 %all-to-all-done.2 = bf16[128,48,128]{2,1,0:T(8,128)(2,1)S(1)} async-done(((bf16[128,48,128]{2,1,0:T(8,128)(2,1)}), bf16[128,48,128]{2,1,0:T(8,128)(2,1)S(1)}, u32[]{:S(2)}, u32[]{:S(2)}) %all-to-all-start.2) | async-done | bytes 1572896 | tf_op jit(solution)/shard_map/all_to_all | solution.py:657
  106.5 8.6 %legendre_filter.1 = (f32[6,128,768]{2,1,0:T(8,128)}, bf16[8,16,6,8,128]{4,3,2,1,0:T(8,128)(2,1)}) custom-call(s32[6]{0:T(128)} %reshape.455.slot_ref, s32[6]{0:T(128)} %copy-done.5, bf16[8,16,6,8,128]{4,3,2,1,0:T(8,128)(2,1)S(1)} %bitcast.22, bf16[6,768,512]{2,1,0:T(8,128)(2,1)} %get-tuple-element.21.ana_ref, bf16[6,768,512]{2,1,0:T(8,128)(2,1)} %get-tuple-element.22.syn_ref), custom_call_target="tpu_custom_call" | custom-call | tf_op jit(solution)/shard_map/legendre_filter/pallas_call | solution.py:517
  115.0 31.3 %all_to_all.25.y_ref = bf16[128,48,128]{2,1,0:T(8,128)(2,1)S(1)} all-to-all(bf16[128,48,128]{2,1,0:T(8,128)(2,1)} %bitcast.35), channel_id=1, replica_groups=mesh['lat'=8,'lonr'=16] {'lat','lonr'}, dimensions={0} | all-to-all | bytes 3145728 | tf_op jit(solution)/shard_map/all_to_all | solution.py:663
  146.3 5.3 %inverse.1 = bf16[2,8,4,128,128]{4,3,2,1,0:T(8,128)(2,1)} custom-call(bf16[128,48,128]{2,1,0:T(8,128)(2,1)S(1)} %all_to_all.25.y_ref, bf16[2,2,384,1024]{3,2,1,0:T(8,128)(2,1)} %longitude_table.1.refs_1_.t_any), custom_call_target="tpu_custom_call" | custom-call | tf_op jit(solution)/shard_map/inverse/pallas_call | solution.py:578
  151.6 3.7 %all-to-all-start.4 = ((bf16[16,4,128,128]{3,2,1,0:T(8,128)(2,1)}), bf16[16,4,128,128]{3,2,1,0:T(8,128)(2,1)S(1)}, u32[]{:S(2)}, u32[]{:S(2)}) async-start(bf16[16,4,128,128]{3,2,1,0:T(8,128)(2,1)} %bitcast.32), calls=%async_computation.4 | async-start | bytes 4194304 | tf_op jit(solution)/shard_map/all_to_all | solution.py:667
  155.4 3.9 %tail.1 = (f32[40,128,128]{2,1,0:T(8,128)}, f32[40,128,128]{2,1,0:T(8,128)}) custom-call(f32[10,4,128,128]{3,2,1,0:T(8,128)} %bitcast.25, f32[10,4,128,128]{3,2,1,0:T(8,128)} %bitcast.28, f32[10,4,128,128]{3,2,1,0:T(8,128)} %bitcast.31, f32[10,4,8,128]{3,2,1,0:T(8,128)} %bitcast.41, f32[10,4,8,128]{3,2,1,0:T(8,128)} %bitcast.44, f32[10,4,8,128]{3,2,1,0:T(8,128)} %bitcast.38, ...), custom_call_target="tpu_custom_call" | custom-call | tf_op jit(solution)/shard_map/tail/pallas_call | solution.py:256
  159.2 4.0 %reshape.472 = f32[6,64,2,768]{3,2,1,0:T(2,128)} reshape(f32[6,128,768]{2,1,0:T(8,128)} %get-tuple-element.28) | data formatting | bytes 4718592 | tf_op jit(solution)/shard_map/reshape | solution.py:671
  163.2 21.6 %all-to-all-done.4 = bf16[16,4,128,128]{3,2,1,0:T(8,128)(2,1)S(1)} async-done(((bf16[16,4,128,128]{3,2,1,0:T(8,128)(2,1)}), bf16[16,4,128,128]{3,2,1,0:T(8,128)(2,1)S(1)}, u32[]{:S(2)}, u32[]{:S(2)}) %all-to-all-start.4) | async-done | bytes 2097184 | tf_op jit(solution)/shard_map/all_to_all | solution.py:667
  184.8 4.7 %update.1 = (f32[40,128,128]{2,1,0:T(8,128)}, f32[40,128,128]{2,1,0:T(8,128)}) custom-call(f32[40,128,128]{2,1,0:T(8,128)} %se_ref.1, f32[40,128,128]{2,1,0:T(8,128)} %sp_ref.1, bf16[2,32,128,128]{3,2,1,0:T(8,128)(2,1)S(1)} %bitcast.21, f32[40,128,128]{2,1,0:T(8,128)} %get-tuple-element.24.old_ent, ...), custom_call_target="tpu_custom_call", output_to_operand_aliasing={{0}: (3, {}), {1}: (4, {})} | custom-call | tf_op jit(solution)/shard_map/update/pallas_call | solution.py:608
  (21 shorter events, 0.1 us)
Async XLA Ops:
  6.0 12.4 %collective-permute-start = (f32[40,8,128]{2,1,0:T(8,128)}, f32[40,8,128]{2,1,0:T(8,128)S(1)}, u32[]{:S(2)}, u32[]{:S(2)}) collective-permute-start(f32[40,8,128]{2,1,0:T(8,128)} %get-tuple-element.16), channel_id=1, source_target_pairs={{0,1},{1,2},{2,3},{3,4},{4,5},{5,6},{6,7},{7,8},{8,9},{9,10},{10,1... | collective-permute-start | bytes 491528 | tf_op jit(solution)/shard_map/ppermute | solution.py:638
  7.8 10.6 %collective-permute-start.1 = (f32[40,8,128]{2,1,0:T(8,128)}, f32[40,8,128]{2,1,0:T(8,128)S(1)}, u32[]{:S(2)}, u32[]{:S(2)}) collective-permute-start(f32[40,8,128]{2,1,0:T(8,128)} %get-tuple-element.16), channel_id=1, source_target_pairs={{1,0},{2,1},{3,2},{4,3},{5,4},{6,5},{7,6},{8,7},{9,8},{10,9},{11,1... | collective-permute-start | bytes 491528 | tf_op jit(solution)/shard_map/ppermute | solution.py:639
  11.5 2.8 %collective-permute-start.2 = (f32[40,4,128]{2,1,0:T(4,128)}, f32[40,4,128]{2,1,0:T(4,128)S(1)}, u32[]{:S(2)}, u32[]{:S(2)}) collective-permute-start(f32[40,4,128]{2,1,0:T(4,128)} %get-tuple-element.17), channel_id=1, source_target_pairs={{0,16},{16,32},{32,48},{48,64},{64,80},{80,96},{96,112},{1,17},{17... | collective-permute-start | bytes 245768 | tf_op jit(solution)/shard_map/ppermute | solution.py:640
  12.9 5.4 %collective-permute-start.3 = (f32[40,4,128]{2,1,0:T(4,128)}, f32[40,4,128]{2,1,0:T(4,128)S(1)}, u32[]{:S(2)}, u32[]{:S(2)}) collective-permute-start(f32[40,4,128]{2,1,0:T(4,128)} %get-tuple-element.18), channel_id=1, source_target_pairs={{16,0},{32,16},{48,32},{64,48},{80,64},{96,80},{112,96},{17,1},{33... | collective-permute-start | bytes 245768 | tf_op jit(solution)/shard_map/ppermute | solution.py:641
  14.3 4.1 %copy-start.2 = (f32[40,4,128]{2,1,0:T(4,128)}, f32[40,4,128]{2,1,0:T(4,128)S(1)}, u32[]{:S(2)}) copy-start(f32[40,4,128]{2,1,0:T(4,128)S(1)} %collective-permute-done.2) | copy-start | bytes 245764
  18.4 0.6 copy-start.3
  18.4 0.7 copy-start
  18.4 0.8 copy-start.1
  19.1 8.3 %copy-start.6 = (s32[768]{0:T(1024)S(1)}, s32[768]{0:T(1024)}, u32[]{:S(2)}) copy-start(s32[768]{0:T(1024)} %param.17) | copy-start | bytes 9220
  23.5 20.4 %all-to-all-start.1 = ((bf16[16,2,128,128]{3,2,1,0:T(8,128)(2,1)}), bf16[16,2,128,128]{3,2,1,0:T(8,128)(2,1)S(1)}, u32[]{:S(2)}, u32[]{:S(2)}) async-start(bf16[16,2,128,128]{3,2,1,0:T(8,128)(2,1)} %bitcast.34), calls=%async_computation.1 | async-start | bytes 2097152 | tf_op jit(solution)/shard_map/all_to_all | solution.py:647
  44.0 24.6 %all-to-all-start = ((bf16[16,2,128,128]{3,2,1,0:T(8,128)(2,1)}), bf16[16,2,128,128]{3,2,1,0:T(8,128)(2,1)S(1)}, u32[]{:S(2)}, u32[]{:S(2)}) async-start(bf16[16,2,128,128]{3,2,1,0:T(8,128)(2,1)} %bitcast.33), calls=%async_computation | async-start | bytes 2097152 | tf_op jit(solution)/shard_map/all_to_all | solution.py:647
  73.8 32.6 %all-to-all-start.2 = ((bf16[128,48,128]{2,1,0:T(8,128)(2,1)}), bf16[128,48,128]{2,1,0:T(8,128)(2,1)S(1)}, u32[]{:S(2)}, u32[]{:S(2)}) async-start(bf16[128,48,128]{2,1,0:T(8,128)(2,1)} %forward.3), calls=%async_computation.2 | async-start | bytes 3145728 | tf_op jit(solution)/shard_map/all_to_all | solution.py:657
  83.4 23.1 %copy-start.5 = (s32[6]{0:T(128)}, s32[6]{0:T(128)S(1)}, u32[]{:S(2)}) copy-start(s32[6]{0:T(128)S(1)} %reshape.456.ord_ref) | copy-start | bytes 76
  84.2 4.1 %copy-start.4 = (f32[4608]{0:T(1024)}, f32[4608]{0:T(1024)S(1)}, u32[]{:S(2)}) copy-start(f32[4608]{0:T(1024)S(1)} %reshape.474.a_ref) | copy-start | bytes 55300
  151.6 33.2 %all-to-all-start.4 = ((bf16[16,4,128,128]{3,2,1,0:T(8,128)(2,1)}), bf16[16,4,128,128]{3,2,1,0:T(8,128)(2,1)S(1)}, u32[]{:S(2)}, u32[]{:S(2)}) async-start(bf16[16,4,128,128]{3,2,1,0:T(8,128)(2,1)} %bitcast.32), calls=%async_computation.4 | async-start | bytes 4194304 | tf_op jit(solution)/shard_map/all_to_all | solution.py:667

commit v5 on v4

--- a/solution.py
+++ b/solution.py
@@ -433,7 +433,7 @@
             ana_ref[o, :, 128 * jb:128 * jb + 128] = (val * w_ref[jb:jb + 1, :]).astype(BF16)
 
 
-def legendre_tables(orders):
+def legendre_inputs(orders):
     half = NLAT // 2
     colatitude = math.pi * (jnp.arange(half, dtype=F32) + 0.5) / NLAT
     sine = jnp.sin(colatitude)
@@ -454,6 +454,11 @@
     denom_b = jnp.maximum(4.0 * (deg - 1.0) * (deg - 1.0) - 1.0, 1.0)
     coef_b = coef_a * jnp.sqrt(numer_b / denom_b)
     order_rows = jnp.broadcast_to(jnp.repeat(orders, 4)[:, None], (24, 128))
+    return [coef_a.reshape(-1), coef_b.reshape(-1), order_rows, cosine, start, weight]
+
+
+def legendre_tables(inputs):
+    half = NLAT // 2
     smem = pl.BlockSpec(memory_space=pltpu.SMEM)
     full = pl.BlockSpec((24, 128), lambda g: (0, 0))
     return pl.pallas_call(
@@ -468,7 +473,7 @@
         out_shape=[pltpu.HBM((6, ORDERS, half), BF16)] * 2,
         scratch_shapes=[pltpu.VMEM((CHUNK * 24, 128), F32), pltpu.VMEM((96, 128), F32)],
         name="legendre_tables",
-    )(coef_a.reshape(-1), coef_b.reshape(-1), order_rows, cosine, start, weight)
+    )(*inputs)
 
 
 def filter_kernel(slot_ref, ord_ref, f_ref, ana_ref, syn_ref, spec_ref, back_ref):
@@ -649,11 +654,15 @@
         )
 
     first_items = exchange(tendencies(fields, halos, (fs, rc), half=0))
-    second_items = exchange(tendencies(fields, halos, (fs, rc), half=1))
+    later, *inputs = lax.optimization_barrier(
+        [tendencies(fields, halos, (fs, rc), half=1), *legendre_inputs(orders), slots]
+    )
+    slots = inputs.pop()
+    second_items = exchange(later)
     ent, pres = tendencies(fields, halos, (fs, rc), starts=[start_entropy, start_pressure])
     rows = forward(first_items, table)
     spectral = forward(second_items, table, rows)
-    analysis, synthesis = legendre_tables(orders)
+    analysis, synthesis = legendre_tables(inputs)
     spectral = lax.all_to_all(
         spectral, ("lat", "lonr"), split_axis=0, concat_axis=0, tiled=True
     )

time: 190 us -> 188 us (0.989)
  blocking collectives: 31.3 us -> 29.3 us
    all_to_all x1, waiting for transfers between devices: 2.76 us -> 8.83 us  [per_device(): lax.all_to_all(spectral, ('lat', 'lonr'), split_axis=0, concat_axis=0, ti...]
    all_to_all x2, waiting for transfers between devices: 17.9 us -> 13.4 us  [exchange(): lax.all_to_all(items.reshape(16, 2, ROWS, COLS), 'lonr', split_axis=0, co...]
    all_to_all x1, blocking collectives: 31.3 us -> 29.3 us  [per_device(): lax.all_to_all(back.reshape(128, 48, 128), ('lat', 'lonr'), split_axis=0,...]
  transfers between devices with their start and end apart: 8 -> 8, of which waited for: 5 -> 5; matrix products, arithmetic and copies ran while one was open for 7% -> 8% of each run, Pallas kernels for 18% -> 18%
where the time goes in v5:
time: 188 us
  Pallas kernels  66.9 us (36%)
  waiting for transfers between devices  46.4 us (25%)
  blocking collectives  29.3 us (16%)
  starting transfers between devices  29.1 us (15%)
  local copies, waits for them, and re-layouts  9.11 us (5%)
  other arithmetic  5.85 us (3%)
    all_to_all x1, blocking collectives, per_device(): lax.all_to_all(back.reshape(128, 48, 128), ('lat', 'lonr'), split_axis=0,...  29.3 us
    all_to_all x1, waiting for transfers between devices, per_device(): lax.all_to_all(filtered, 'lonr', split_axis=0, concat_axis=0, tiled=True)  21.6 us
    pallas_call x1, Pallas kernels, legendre_tables(): pl.pallas_call(legendre_kernel, grid=(ORDERS // CHUNK,), in_specs=[smem,...  15.5 us
    all_to_all x2, waiting for transfers between devices, exchange(): lax.all_to_all(items.reshape(16, 2, ROWS, COLS), 'lonr', split_axis=0, co...  13.4 us
    pallas_call x3, Pallas kernels, tendencies(): pl.pallas_call(tend_kernel, grid=(steps,), in_specs=in_specs, out_specs=o...  12.6 us
    pallas_call x2, Pallas kernels, forward(): pl.pallas_call(functools.partial(forward_kernel, half), grid=(2,), in_spe...  9.99 us
    all_to_all x1, waiting for transfers between devices, per_device(): lax.all_to_all(spectral, ('lat', 'lonr'), split_axis=0, concat_axis=0, ti...  8.83 us
    all_to_all x2, starting transfers between devices, exchange(): lax.all_to_all(items.reshape(16, 2, ROWS, COLS), 'lonr', split_axis=0, co...  8.79 us
  transfers between devices with their start and end apart: 8, of which 5 were waited for; matrix products, arithmetic and copies ran while one was open for 8% of the time, Pallas kernels for 18%

profile of v5, /device:TPU:0, one launch (start us, length us, event | category | flops | bytes accessed | tf_op | source)
XLA Modules:
  0.0 187.5 jit_solution(10467646231386161916)
XLA Ops:
  0.6 0.0 copy-start.6
  0.6 5.4 %edges.1 = (f32[40,8,128]{2,1,0:T(8,128)}, f32[40,4,128]{2,1,0:T(4,128)}, f32[40,4,128]{2,1,0:T(4,128)}, f32[136,128]{1,0:T(8,128)}, f32[128,128]{1,0:T(8,128)}) custom-call(s32[1]{0:T(128)} %bitcast.3.first_ref, f32[40,128,128]{2,1,0:T(8,128)} %s_any.1, f32[40,128,128]{2,1,0:T(8,128)} %u_any.1, f32[40,128,128]{2,1,0:T(8,128)} %v_ref.1), custom_call_target="tpu_custom_call" | custom-call | tf_op jit(solution)/shard_map/edges/pallas_call | solution.py:98
  6.0 1.8 collective-permute-start
  7.8 3.7 %collective-permute-start.1 = (f32[40,8,128]{2,1,0:T(8,128)}, f32[40,8,128]{2,1,0:T(8,128)S(1)}, u32[]{:S(2)}, u32[]{:S(2)}) collective-permute-start(f32[40,8,128]{2,1,0:T(8,128)} %get-tuple-element.24), channel_id=1, source_target_pairs={{1,0},{2,1},{3,2},{4,3},{5,4},{6,5},{7,6},{8,7},{9,8},{10,9},{11,1... | collective-permute-start | bytes 491528 | tf_op jit(solution)/shard_map/ppermute | solution.py:644
  11.5 1.5 collective-permute-start.2
  13.0 1.3 collective-permute-start.3
  14.3 0.2 reshape.461
  14.5 0.3 slice_reduce_fusion
  14.7 0.1 copy.19
  14.8 0.1 copy.20
  15.0 0.1 fusion.28
  15.1 0.1 copy.21
  15.2 0.1 lt.48.ord_ref
  15.2 0.1 multiply_add_fusion.1
  15.3 0.5 divide_sqrt_fusion
  15.8 0.0 collective-permute-done.2
  15.8 2.5 %collective-permute-done.3 = f32[40,4,128]{2,1,0:T(4,128)S(1)} collective-permute-done((f32[40,4,128]{2,1,0:T(4,128)}, f32[40,4,128]{2,1,0:T(4,128)S(1)}, u32[]{:S(2)}, u32[]{:S(2)}) %collective-permute-start.3) | collective-permute-done | bytes 81952 | tf_op jit(solution)/shard_map/ppermute | solution.py:646
  18.4 0.0 collective-permute-done
  18.4 0.0 collective-permute-done.1
  18.4 0.6 copy-done.3
  19.0 0.1 copy-done
  19.1 0.0 copy-done.1
  19.1 4.4 %tendencies.3 = bf16[2,8,2,128,128]{4,3,2,1,0:T(8,128)(2,1)} custom-call(f32[10,4,128,128]{3,2,1,0:T(8,128)} %bitcast.23, f32[10,4,128,128]{3,2,1,0:T(8,128)} %bitcast.26, f32[10,4,128,128]{3,2,1,0:T(8,128)} %bitcast.29, f32[10,4,8,128]{3,2,1,0:T(8,128)} %bitcast.39, f32[10,4,8,128]{3,2,1,0:T(8,128)} %bitcast.42, f32[10,4,8,128]{3,2,1,0:T(8,128)} %bitcast.36, ...), custom_call_target="tpu_custom_call" | custom-call | tf_op jit(solution)/shard_map/tendencies/pallas_call | solution.py:256
  23.5 3.9 %all-to-all-start.1 = ((bf16[16,2,128,128]{3,2,1,0:T(8,128)(2,1)}), bf16[16,2,128,128]{3,2,1,0:T(8,128)(2,1)S(1)}, u32[]{:S(2)}, u32[]{:S(2)}) async-start(bf16[16,2,128,128]{3,2,1,0:T(8,128)(2,1)} %bitcast.33), calls=%async_computation.1 | async-start | bytes 2097152 | tf_op jit(solution)/shard_map/all_to_all | solution.py:652
  27.4 0.3 reshape.471.a_ref
  27.7 0.3 sqrt.18
  28.0 0.1 broadcast_in_dim.18
  28.0 0.1 broadcast_in_dim.19
  28.1 0.1 mul.188
  28.2 0.1 mul.189
  28.3 0.1 add.167
  28.3 0.1 add.168
  28.4 0.1 add_bitcast_fusion
  28.5 0.1 copy.22
  28.6 0.6 reshape.462.slot_ref
  29.2 0.6 mul.186.b_ref
  29.9 0.1 fusion.26
  29.9 0.7 fusion.25.w_ref
  30.6 0.1 fusion.35
  30.7 0.6 pad_maximum_fusion.2.start_ref
  31.3 4.4 %tendencies.2 = bf16[2,8,2,128,128]{4,3,2,1,0:T(8,128)(2,1)} custom-call(f32[10,4,128,128]{3,2,1,0:T(8,128)} %bitcast.24, f32[10,4,128,128]{3,2,1,0:T(8,128)} %bitcast.27, f32[10,4,128,128]{3,2,1,0:T(8,128)} %bitcast.30, f32[10,4,8,128]{3,2,1,0:T(8,128)} %bitcast.40, f32[10,4,8,128]{3,2,1,0:T(8,128)} %bitcast.43, f32[10,4,8,128]{3,2,1,0:T(8,128)} %bitcast.37, ...), custom_call_target="tpu_custom_call" | custom-call | tf_op jit(solution)/shard_map/tendencies/pallas_call | solution.py:256
  35.7 0.7 broadcast_in_dim.20.m_ref
  36.3 0.6 tile.8
  36.9 7.0 %all-to-all-done.1.refs_0_ = bf16[16,2,128,128]{3,2,1,0:T(8,128)(2,1)S(1)} async-done(((bf16[16,2,128,128]{3,2,1,0:T(8,128)(2,1)}), bf16[16,2,128,128]{3,2,1,0:T(8,128)(2,1)S(1)}, u32[]{:S(2)}, u32[]{:S(2)}) %all-to-all-start.1) | async-done | bytes 1048608 | tf_op jit(solution)/shard_map/all_to_all | solution.py:652
  44.0 4.9 %all-to-all-start = ((bf16[16,2,128,128]{3,2,1,0:T(8,128)(2,1)}), bf16[16,2,128,128]{3,2,1,0:T(8,128)(2,1)S(1)}, u32[]{:S(2)}, u32[]{:S(2)}) async-start(bf16[16,2,128,128]{3,2,1,0:T(8,128)(2,1)} %bitcast.34), calls=%async_computation | async-start | bytes 2097152 | tf_op jit(solution)/shard_map/all_to_all | solution.py:652
  48.9 0.2 fusion.14
  49.1 0.9 copy.23.turn_ref
  50.0 1.6 fusion.9
  51.7 0.9 pad_maximum_fusion.base_ref
  52.6 4.9 %longitude_table.1.refs_1_.t_any = bf16[2,2,384,1024]{3,2,1,0:T(8,128)(2,1)} custom-call(f32[2,2,384,128]{3,2,1,0:T(8,128)} %pad_maximum_fusion.base_ref, f32[2,384,16]{2,1,0:T(8,128)} %copy.23.turn_ref), custom_call_target="tpu_custom_call" | custom-call | tf_op jit(solution)/shard_map/longitude_table/pallas_call | solution.py:292
  57.5 4.7 %forward.2.refs_2_ = f32[6144,128]{1,0:T(8,128)} custom-call(bf16[16,2,128,128]{3,2,1,0:T(8,128)(2,1)S(1)} %all-to-all-done.1.refs_0_, bf16[2,2,384,1024]{3,2,1,0:T(8,128)(2,1)} %longitude_table.1.refs_1_.t_any), custom_call_target="tpu_custom_call" | custom-call | tf_op jit(solution)/shard_map/forward/pallas_call | solution.py:366
  62.2 6.4 %all-to-all-done.refs_0_ = bf16[16,2,128,128]{3,2,1,0:T(8,128)(2,1)S(1)} async-done(((bf16[16,2,128,128]{3,2,1,0:T(8,128)(2,1)}), bf16[16,2,128,128]{3,2,1,0:T(8,128)(2,1)S(1)}, u32[]{:S(2)}, u32[]{:S(2)}) %all-to-all-start) | async-done | bytes 1048608 | tf_op jit(solution)/shard_map/all_to_all | solution.py:652
  68.5 5.3 %forward.3 = bf16[128,48,128]{2,1,0:T(8,128)(2,1)} custom-call(bf16[16,2,128,128]{3,2,1,0:T(8,128)(2,1)S(1)} %all-to-all-done.refs_0_, bf16[2,2,384,1024]{3,2,1,0:T(8,128)(2,1)} %longitude_table.1.refs_1_.t_any, f32[6144,128]{1,0:T(8,128)} %forward.2.refs_2_), custom_call_target="tpu_custom_call" | custom-call | tf_op jit(solution)/shard_map/forward/pallas_call | solution.py:366
  73.8 8.3 %all-to-all-start.2 = ((bf16[128,48,128]{2,1,0:T(8,128)(2,1)}), bf16[128,48,128]{2,1,0:T(8,128)(2,1)S(1)}, u32[]{:S(2)}, u32[]{:S(2)}) async-start(bf16[128,48,128]{2,1,0:T(8,128)(2,1)} %forward.3), calls=%async_computation.2 | async-start | bytes 3145728 | tf_op jit(solution)/shard_map/all_to_all | solution.py:666
  82.2 15.5 %legendre_tables.1 = (bf16[6,768,512]{2,1,0:T(8,128)(2,1)}, bf16[6,768,512]{2,1,0:T(8,128)(2,1)}) custom-call(f32[4608]{0:T(1024)} %copy-done.4, f32[4608]{0:T(1024)} %mul.186.b_ref, s32[24,128]{1,0:T(8,128)} %broadcast_in_dim.20.m_ref, f32[24,128]{1,0:T(8,128)} %bitcast.52, f32[48,128]{1,0:T(8,128)} %pad_maximum_fusion.2.start_ref, f32[4,128]{1,0:T(4,128)} %fusion.25.w_ref), custom_call_target="tpu_custom_call" | custom-call | tf_op jit(solution)/shard_map/legendre_tables/pallas_call | solution.py:464
  97.6 8.8 %all-to-all-done.2 = bf16[128,48,128]{2,1,0:T(8,128)(2,1)S(1)} async-done(((bf16[128,48,128]{2,1,0:T(8,128)(2,1)}), bf16[128,48,128]{2,1,0:T(8,128)(2,1)S(1)}, u32[]{:S(2)}, u32[]{:S(2)}) %all-to-all-start.2) | async-done | bytes 1572896 | tf_op jit(solution)/shard_map/all_to_all | solution.py:666
  106.5 8.6 %legendre_filter.1 = (f32[6,128,768]{2,1,0:T(8,128)}, bf16[8,16,6,8,128]{4,3,2,1,0:T(8,128)(2,1)}) custom-call(s32[6]{0:T(128)} %reshape.462.slot_ref, s32[6]{0:T(128)} %copy-done.5, bf16[8,16,6,8,128]{4,3,2,1,0:T(8,128)(2,1)S(1)} %bitcast.22, bf16[6,768,512]{2,1,0:T(8,128)(2,1)} %get-tuple-element.37.ana_ref, bf16[6,768,512]{2,1,0:T(8,128)(2,1)} %get-tuple-element.38.syn_ref), custom_call_target="tpu_custom_call" | custom-call | tf_op jit(solution)/shard_map/legendre_filter/pallas_call | solution.py:522
  115.0 29.3 %all_to_all.25.y_ref = bf16[128,48,128]{2,1,0:T(8,128)(2,1)S(1)} all-to-all(bf16[128,48,128]{2,1,0:T(8,128)(2,1)} %bitcast.35), channel_id=1, replica_groups=mesh['lat'=8,'lonr'=16] {'lat','lonr'}, dimensions={0} | all-to-all | bytes 3145728 | tf_op jit(solution)/shard_map/all_to_all | solution.py:672
  144.4 5.3 %inverse.1 = bf16[2,8,4,128,128]{4,3,2,1,0:T(8,128)(2,1)} custom-call(bf16[128,48,128]{2,1,0:T(8,128)(2,1)S(1)} %all_to_all.25.y_ref, bf16[2,2,384,1024]{3,2,1,0:T(8,128)(2,1)} %longitude_table.1.refs_1_.t_any), custom_call_target="tpu_custom_call" | custom-call | tf_op jit(solution)/shard_map/inverse/pallas_call | solution.py:583
  149.7 3.7 %all-to-all-start.4 = ((bf16[16,4,128,128]{3,2,1,0:T(8,128)(2,1)}), bf16[16,4,128,128]{3,2,1,0:T(8,128)(2,1)S(1)}, u32[]{:S(2)}, u32[]{:S(2)}) async-start(bf16[16,4,128,128]{3,2,1,0:T(8,128)(2,1)} %bitcast.32), calls=%async_computation.4 | async-start | bytes 4194304 | tf_op jit(solution)/shard_map/all_to_all | solution.py:676
  153.4 3.9 %tail.1 = (f32[40,128,128]{2,1,0:T(8,128)}, f32[40,128,128]{2,1,0:T(8,128)}) custom-call(f32[10,4,128,128]{3,2,1,0:T(8,128)} %bitcast.25, f32[10,4,128,128]{3,2,1,0:T(8,128)} %bitcast.28, f32[10,4,128,128]{3,2,1,0:T(8,128)} %bitcast.31, f32[10,4,8,128]{3,2,1,0:T(8,128)} %bitcast.41, f32[10,4,8,128]{3,2,1,0:T(8,128)} %bitcast.44, f32[10,4,8,128]{3,2,1,0:T(8,128)} %bitcast.38, ...), custom_call_target="tpu_custom_call" | custom-call | tf_op jit(solution)/shard_map/tail/pallas_call | solution.py:256
  157.2 4.0 %reshape.469 = f32[6,64,2,768]{3,2,1,0:T(2,128)} reshape(f32[6,128,768]{2,1,0:T(8,128)} %get-tuple-element.44) | data formatting | bytes 4718592 | tf_op jit(solution)/shard_map/reshape | solution.py:680
  161.2 21.6 %all-to-all-done.4 = bf16[16,4,128,128]{3,2,1,0:T(8,128)(2,1)S(1)} async-done(((bf16[16,4,128,128]{3,2,1,0:T(8,128)(2,1)}), bf16[16,4,128,128]{3,2,1,0:T(8,128)(2,1)S(1)}, u32[]{:S(2)}, u32[]{:S(2)}) %all-to-all-start.4) | async-done | bytes 2097184 | tf_op jit(solution)/shard_map/all_to_all | solution.py:676
  182.9 4.7 %update.1 = (f32[40,128,128]{2,1,0:T(8,128)}, f32[40,128,128]{2,1,0:T(8,128)}) custom-call(f32[40,128,128]{2,1,0:T(8,128)} %se_ref.1, f32[40,128,128]{2,1,0:T(8,128)} %sp_ref.1, bf16[2,32,128,128]{3,2,1,0:T(8,128)(2,1)S(1)} %bitcast.21, f32[40,128,128]{2,1,0:T(8,128)} %get-tuple-element.40.old_ent, ...), custom_call_target="tpu_custom_call", output_to_operand_aliasing={{0}: (3, {}), {1}: (4, {})} | custom-call | tf_op jit(solution)/shard_map/update/pallas_call | solution.py:613
  (21 shorter events, 0.1 us)
Async XLA Ops:
  0.6 13.7 %copy-start.6 = (s32[768]{0:T(1024)S(1)}, s32[768]{0:T(1024)}, u32[]{:S(2)}) copy-start(s32[768]{0:T(1024)} %param.17) | copy-start | bytes 9220
  6.0 12.4 %collective-permute-start = (f32[40,8,128]{2,1,0:T(8,128)}, f32[40,8,128]{2,1,0:T(8,128)S(1)}, u32[]{:S(2)}, u32[]{:S(2)}) collective-permute-start(f32[40,8,128]{2,1,0:T(8,128)} %get-tuple-element.24), channel_id=1, source_target_pairs={{0,1},{1,2},{2,3},{3,4},{4,5},{5,6},{6,7},{7,8},{8,9},{9,10},{10,1... | collective-permute-start | bytes 491528 | tf_op jit(solution)/shard_map/ppermute | solution.py:643
  7.8 10.6 %collective-permute-start.1 = (f32[40,8,128]{2,1,0:T(8,128)}, f32[40,8,128]{2,1,0:T(8,128)S(1)}, u32[]{:S(2)}, u32[]{:S(2)}) collective-permute-start(f32[40,8,128]{2,1,0:T(8,128)} %get-tuple-element.24), channel_id=1, source_target_pairs={{1,0},{2,1},{3,2},{4,3},{5,4},{6,5},{7,6},{8,7},{9,8},{10,9},{11,1... | collective-permute-start | bytes 491528 | tf_op jit(solution)/shard_map/ppermute | solution.py:644
  11.5 4.3 %collective-permute-start.2 = (f32[40,4,128]{2,1,0:T(4,128)}, f32[40,4,128]{2,1,0:T(4,128)S(1)}, u32[]{:S(2)}, u32[]{:S(2)}) collective-permute-start(f32[40,4,128]{2,1,0:T(4,128)} %get-tuple-element.25), channel_id=1, source_target_pairs={{0,16},{16,32},{32,48},{48,64},{64,80},{80,96},{96,112},{1,17},{17... | collective-permute-start | bytes 245768 | tf_op jit(solution)/shard_map/ppermute | solution.py:645
  13.0 5.4 %collective-permute-start.3 = (f32[40,4,128]{2,1,0:T(4,128)}, f32[40,4,128]{2,1,0:T(4,128)S(1)}, u32[]{:S(2)}, u32[]{:S(2)}) collective-permute-start(f32[40,4,128]{2,1,0:T(4,128)} %get-tuple-element.26), channel_id=1, source_target_pairs={{16,0},{32,16},{48,32},{64,48},{80,64},{96,80},{112,96},{17,1},{33... | collective-permute-start | bytes 245768 | tf_op jit(solution)/shard_map/ppermute | solution.py:646
  15.2 12.7 %copy-start.5 = (s32[6]{0:T(128)}, s32[6]{0:T(128)S(1)}, u32[]{:S(2)}) copy-start(s32[6]{0:T(128)S(1)} %lt.48.ord_ref) | copy-start | bytes 76
  15.8 2.6 %copy-start.2 = (f32[40,4,128]{2,1,0:T(4,128)}, f32[40,4,128]{2,1,0:T(4,128)S(1)}, u32[]{:S(2)}) copy-start(f32[40,4,128]{2,1,0:T(4,128)S(1)} %collective-permute-done.2) | copy-start | bytes 245764
  18.4 0.6 copy-start.3
  18.4 0.7 copy-start
  18.4 0.8 copy-start.1
  23.5 20.4 %all-to-all-start.1 = ((bf16[16,2,128,128]{3,2,1,0:T(8,128)(2,1)}), bf16[16,2,128,128]{3,2,1,0:T(8,128)(2,1)S(1)}, u32[]{:S(2)}, u32[]{:S(2)}) async-start(bf16[16,2,128,128]{3,2,1,0:T(8,128)(2,1)} %bitcast.33), calls=%async_computation.1 | async-start | bytes 2097152 | tf_op jit(solution)/shard_map/all_to_all | solution.py:652
  27.7 8.0 %copy-start.4 = (f32[4608]{0:T(1024)}, f32[4608]{0:T(1024)S(1)}, u32[]{:S(2)}) copy-start(f32[4608]{0:T(1024)S(1)} %reshape.471.a_ref) | copy-start | bytes 55300
  44.0 24.6 %all-to-all-start = ((bf16[16,2,128,128]{3,2,1,0:T(8,128)(2,1)}), bf16[16,2,128,128]{3,2,1,0:T(8,128)(2,1)S(1)}, u32[]{:S(2)}, u32[]{:S(2)}) async-start(bf16[16,2,128,128]{3,2,1,0:T(8,128)(2,1)} %bitcast.34), calls=%async_computation | async-start | bytes 2097152 | tf_op jit(solution)/shard_map/all_to_all | solution.py:652
  73.8 32.6 %all-to-all-start.2 = ((bf16[128,48,128]{2,1,0:T(8,128)(2,1)}), bf16[128,48,128]{2,1,0:T(8,128)(2,1)S(1)}, u32[]{:S(2)}, u32[]{:S(2)}) async-start(bf16[128,48,128]{2,1,0:T(8,128)(2,1)} %forward.3), calls=%async_computation.2 | async-start | bytes 3145728 | tf_op jit(solution)/shard_map/all_to_all | solution.py:666
  149.7 33.2 %all-to-all-start.4 = ((bf16[16,4,128,128]{3,2,1,0:T(8,128)(2,1)}), bf16[16,4,128,128]{3,2,1,0:T(8,128)(2,1)S(1)}, u32[]{:S(2)}, u32[]{:S(2)}) async-start(bf16[16,4,128,128]{3,2,1,0:T(8,128)(2,1)} %bitcast.32), calls=%async_computation.4 | async-start | bytes 4194304 | tf_op jit(solution)/shard_map/all_to_all | solution.py:676

commit v6 on v5

--- a/solution.py
+++ b/solution.py
@@ -476,12 +476,16 @@
     )(*inputs)
 
 
-def filter_kernel(slot_ref, ord_ref, f_ref, ana_ref, syn_ref, spec_ref, back_ref):
+def filter_kernel(
+    slot_ref, ord_ref, f_ref, ana_high, ana_full, syn_high, syn_full, spec_ref, back_ref
+):
     sub = lax.broadcasted_iota(jnp.int32, (128, 128), 0)
     flip = jnp.where(sub + lane_ids((128, 128)) == 127, 1.0, 0.0).astype(BF16)
     pair = pl.program_id(0)
     above = (ord_ref[2 * pair] < ORDERS // 2).astype(jnp.int32)
-    for k, low in ((above, ORDERS // 2), (1 - above, 0)):
+    for k, low, ana_ref, syn_ref in (
+        (above, ORDERS // 2, ana_high, syn_high), (1 - above, 0, ana_full, syn_full)
+    ):
         width = ORDERS - low
         o = 2 * pair + k
         order = ord_ref[o]
@@ -497,7 +501,7 @@
             [jnp.concatenate(plus, axis=1), jnp.concatenate(minus, axis=1)], axis=0
         )
         coef = lax.dot_general(
-            both, ana_ref[k, low:, :], (((1,), (1,)), ((), ())), preferred_element_type=F32
+            both, ana_ref[0], (((1,), (1,)), ((), ())), preferred_element_type=F32
         )
         even = ((lane_ids((128, width)) - order) & 1) == 0
         spec = jnp.where(even, coef[:128], coef[128:])
@@ -505,7 +509,7 @@
             spec_ref[slot_ref[o] & 1, :, :low] = jnp.zeros((128, low), F32)
         spec_ref[slot_ref[o] & 1, :, low:] = spec
         parts = jnp.concatenate([jnp.where(even, spec, 0.0), jnp.where(even, 0.0, spec)], axis=0)
-        grid = jnp.dot(parts.astype(BF16), syn_ref[k, low:, :], preferred_element_type=F32)
+        grid = jnp.dot(parts.astype(BF16), syn_ref[0], preferred_element_type=F32)
         factor = jnp.where(order == 0, 0.5, 1.0)
         north = (grid[:128] + grid[128:]) * factor
         south = ((grid[:128] - grid[128:]) * factor).astype(BF16)
@@ -517,14 +521,22 @@
 
 
 def legendre_filter(fourier, analysis, synthesis, orders, slots):
-    table = pl.BlockSpec((2, ORDERS, NLAT // 2), lambda p, *_: (p, 0, 0))
+    def above(p, order):
+        return (order[2 * p] < ORDERS // 2).astype(jnp.int32)
+
+    high = pl.BlockSpec(
+        (1, ORDERS // 2, NLAT // 2), lambda p, slot, order: (2 * p + above(p, order), 1, 0)
+    )
+    full = pl.BlockSpec(
+        (1, ORDERS, NLAT // 2), lambda p, slot, order: (2 * p + 1 - above(p, order), 0, 0)
+    )
     blocks = pl.BlockSpec((8, 16, 2, 8, 128), lambda p, *_: (0, 0, p, 0, 0))
     return pl.pallas_call(
         filter_kernel,
         grid_spec=pltpu.PrefetchScalarGridSpec(
             num_scalar_prefetch=2,
             grid=(3,),
-            in_specs=[IN_VMEM, table, table],
+            in_specs=[IN_VMEM, high, full, high, full],
             out_specs=[
                 pl.BlockSpec((2, 128, ORDERS), lambda p, *_: (p, 0, 0)),
                 blocks,
@@ -536,7 +548,7 @@
         ],
         compiler_params=vmem(56),
         name="legendre_filter",
-    )(slots, orders, in_vmem(fourier), analysis, synthesis)
+    )(slots, orders, in_vmem(fourier), analysis, analysis, synthesis, synthesis)
 
 
 def inverse_kernel(y_ref, t_any, o_ref, rows, cols, t_ref, sems):

time: 188 us -> 188 us (level)
  no operation moved by 1% of the time
where the time goes in v6:
time: 188 us; the launch traced here: 187 us
  Pallas kernels  66.3 us (35%)
  waiting for transfers between devices  46.4 us (25%)
  blocking collectives  29.3 us (16%)
  starting transfers between devices  29.1 us (15%)
  local copies, waits for them, and re-layouts  9.11 us (5%)
  other arithmetic  5.85 us (3%)
    all_to_all x1, blocking collectives, per_device(): lax.all_to_all(back.reshape(128, 48, 128), ('lat', 'lonr'), split_axis=0,...  29.3 us
    all_to_all x1, waiting for transfers between devices, per_device(): lax.all_to_all(filtered, 'lonr', split_axis=0, concat_axis=0, tiled=True)  21.6 us
    pallas_call x1, Pallas kernels, legendre_tables(): pl.pallas_call(legendre_kernel, grid=(ORDERS // CHUNK,), in_specs=[smem,...  15.5 us
    all_to_all x2, waiting for transfers between devices, exchange(): lax.all_to_all(items.reshape(16, 2, ROWS, COLS), 'lonr', split_axis=0, co...  13.4 us
    pallas_call x3, Pallas kernels, tendencies(): pl.pallas_call(tend_kernel, grid=(steps,), in_specs=in_specs, out_specs=o...  12.6 us
    pallas_call x2, Pallas kernels, forward(): pl.pallas_call(functools.partial(forward_kernel, half), grid=(2,), in_spe...  9.99 us
    all_to_all x1, waiting for transfers between devices, per_device(): lax.all_to_all(spectral, ('lat', 'lonr'), split_axis=0, concat_axis=0, ti...  8.83 us
    all_to_all x2, starting transfers between devices, exchange(): lax.all_to_all(items.reshape(16, 2, ROWS, COLS), 'lonr', split_axis=0, co...  8.79 us
  transfers between devices with their start and end apart: 8, of which 5 were waited for; matrix products, arithmetic and copies ran while one was open for 8% of the time, Pallas kernels for 18%

profile of v6, /device:TPU:0, one launch (start us, length us, event | category | flops | bytes accessed | tf_op | source)
XLA Modules:
  0.0 187.0 jit_solution(2093365642604101883)
XLA Ops:
  0.6 0.0 copy-start.6
  0.6 5.4 %edges.1 = (f32[40,8,128]{2,1,0:T(8,128)}, f32[40,4,128]{2,1,0:T(4,128)}, f32[40,4,128]{2,1,0:T(4,128)}, f32[136,128]{1,0:T(8,128)}, f32[128,128]{1,0:T(8,128)}) custom-call(s32[1]{0:T(128)} %bitcast.3.first_ref, f32[40,128,128]{2,1,0:T(8,128)} %s_any.1, f32[40,128,128]{2,1,0:T(8,128)} %u_any.1, f32[40,128,128]{2,1,0:T(8,128)} %v_ref.1), custom_call_target="tpu_custom_call" | custom-call | tf_op jit(solution)/shard_map/edges/pallas_call | solution.py:98
  6.0 1.8 collective-permute-start
  7.8 3.7 %collective-permute-start.1 = (f32[40,8,128]{2,1,0:T(8,128)}, f32[40,8,128]{2,1,0:T(8,128)S(1)}, u32[]{:S(2)}, u32[]{:S(2)}) collective-permute-start(f32[40,8,128]{2,1,0:T(8,128)} %get-tuple-element.24), channel_id=1, source_target_pairs={{1,0},{2,1},{3,2},{4,3},{5,4},{6,5},{7,6},{8,7},{9,8},{10,9},{11,1... | collective-permute-start | bytes 491528 | tf_op jit(solution)/shard_map/ppermute | solution.py:656
  11.5 1.5 collective-permute-start.2
  13.0 1.3 collective-permute-start.3
  14.3 0.2 reshape.461
  14.5 0.3 slice_reduce_fusion
  14.7 0.1 copy.19
  14.8 0.1 copy.20
  15.0 0.1 fusion.28
  15.1 0.1 copy.21
  15.2 0.1 lt.48.ord_ref
  15.2 0.1 multiply_add_fusion.1
  15.3 0.5 divide_sqrt_fusion
  15.8 0.0 collective-permute-done.2
  15.8 2.5 %collective-permute-done.3 = f32[40,4,128]{2,1,0:T(4,128)S(1)} collective-permute-done((f32[40,4,128]{2,1,0:T(4,128)}, f32[40,4,128]{2,1,0:T(4,128)S(1)}, u32[]{:S(2)}, u32[]{:S(2)}) %collective-permute-start.3) | collective-permute-done | bytes 81952 | tf_op jit(solution)/shard_map/ppermute | solution.py:658
  18.4 0.0 collective-permute-done
  18.4 0.0 collective-permute-done.1
  18.4 0.6 copy-done.3
  19.0 0.1 copy-done
  19.1 0.0 copy-done.1
  19.1 4.4 %tendencies.3 = bf16[2,8,2,128,128]{4,3,2,1,0:T(8,128)(2,1)} custom-call(f32[10,4,128,128]{3,2,1,0:T(8,128)} %bitcast.23, f32[10,4,128,128]{3,2,1,0:T(8,128)} %bitcast.26, f32[10,4,128,128]{3,2,1,0:T(8,128)} %bitcast.29, f32[10,4,8,128]{3,2,1,0:T(8,128)} %bitcast.39, f32[10,4,8,128]{3,2,1,0:T(8,128)} %bitcast.42, f32[10,4,8,128]{3,2,1,0:T(8,128)} %bitcast.36, ...), custom_call_target="tpu_custom_call" | custom-call | tf_op jit(solution)/shard_map/tendencies/pallas_call | solution.py:256
  23.5 3.9 %all-to-all-start.1 = ((bf16[16,2,128,128]{3,2,1,0:T(8,128)(2,1)}), bf16[16,2,128,128]{3,2,1,0:T(8,128)(2,1)S(1)}, u32[]{:S(2)}, u32[]{:S(2)}) async-start(bf16[16,2,128,128]{3,2,1,0:T(8,128)(2,1)} %bitcast.33), calls=%async_computation.1 | async-start | bytes 2097152 | tf_op jit(solution)/shard_map/all_to_all | solution.py:664
  27.4 0.3 reshape.471.a_ref
  27.7 0.3 sqrt.18
  28.0 0.1 broadcast_in_dim.18
  28.0 0.1 broadcast_in_dim.19
  28.1 0.1 mul.188
  28.2 0.1 mul.189
  28.3 0.1 add.167
  28.3 0.1 add.168
  28.4 0.1 add_bitcast_fusion
  28.5 0.1 copy.22
  28.6 0.6 reshape.462.slot_ref
  29.2 0.6 mul.186.b_ref
  29.9 0.1 fusion.26
  29.9 0.7 fusion.25.w_ref
  30.6 0.1 fusion.35
  30.7 0.6 pad_maximum_fusion.2.start_ref
  31.3 4.4 %tendencies.2 = bf16[2,8,2,128,128]{4,3,2,1,0:T(8,128)(2,1)} custom-call(f32[10,4,128,128]{3,2,1,0:T(8,128)} %bitcast.24, f32[10,4,128,128]{3,2,1,0:T(8,128)} %bitcast.27, f32[10,4,128,128]{3,2,1,0:T(8,128)} %bitcast.30, f32[10,4,8,128]{3,2,1,0:T(8,128)} %bitcast.40, f32[10,4,8,128]{3,2,1,0:T(8,128)} %bitcast.43, f32[10,4,8,128]{3,2,1,0:T(8,128)} %bitcast.37, ...), custom_call_target="tpu_custom_call" | custom-call | tf_op jit(solution)/shard_map/tendencies/pallas_call | solution.py:256
  35.7 0.7 broadcast_in_dim.20.m_ref
  36.3 0.6 tile.8
  36.9 7.0 %all-to-all-done.1.refs_0_ = bf16[16,2,128,128]{3,2,1,0:T(8,128)(2,1)S(1)} async-done(((bf16[16,2,128,128]{3,2,1,0:T(8,128)(2,1)}), bf16[16,2,128,128]{3,2,1,0:T(8,128)(2,1)S(1)}, u32[]{:S(2)}, u32[]{:S(2)}) %all-to-all-start.1) | async-done | bytes 1048608 | tf_op jit(solution)/shard_map/all_to_all | solution.py:664
  44.0 4.9 %all-to-all-start = ((bf16[16,2,128,128]{3,2,1,0:T(8,128)(2,1)}), bf16[16,2,128,128]{3,2,1,0:T(8,128)(2,1)S(1)}, u32[]{:S(2)}, u32[]{:S(2)}) async-start(bf16[16,2,128,128]{3,2,1,0:T(8,128)(2,1)} %bitcast.34), calls=%async_computation | async-start | bytes 2097152 | tf_op jit(solution)/shard_map/all_to_all | solution.py:664
  48.9 0.2 fusion.14
  49.1 0.9 copy.23.turn_ref
  50.0 1.6 fusion.9
  51.7 0.9 pad_maximum_fusion.base_ref
  52.6 4.9 %longitude_table.1.refs_1_.t_any = bf16[2,2,384,1024]{3,2,1,0:T(8,128)(2,1)} custom-call(f32[2,2,384,128]{3,2,1,0:T(8,128)} %pad_maximum_fusion.base_ref, f32[2,384,16]{2,1,0:T(8,128)} %copy.23.turn_ref), custom_call_target="tpu_custom_call" | custom-call | tf_op jit(solution)/shard_map/longitude_table/pallas_call | solution.py:292
  57.5 4.7 %forward.2.refs_2_ = f32[6144,128]{1,0:T(8,128)} custom-call(bf16[16,2,128,128]{3,2,1,0:T(8,128)(2,1)S(1)} %all-to-all-done.1.refs_0_, bf16[2,2,384,1024]{3,2,1,0:T(8,128)(2,1)} %longitude_table.1.refs_1_.t_any), custom_call_target="tpu_custom_call" | custom-call | tf_op jit(solution)/shard_map/forward/pallas_call | solution.py:366
  62.2 6.4 %all-to-all-done.refs_0_ = bf16[16,2,128,128]{3,2,1,0:T(8,128)(2,1)S(1)} async-done(((bf16[16,2,128,128]{3,2,1,0:T(8,128)(2,1)}), bf16[16,2,128,128]{3,2,1,0:T(8,128)(2,1)S(1)}, u32[]{:S(2)}, u32[]{:S(2)}) %all-to-all-start) | async-done | bytes 1048608 | tf_op jit(solution)/shard_map/all_to_all | solution.py:664
  68.5 5.3 %forward.3 = bf16[128,48,128]{2,1,0:T(8,128)(2,1)} custom-call(bf16[16,2,128,128]{3,2,1,0:T(8,128)(2,1)S(1)} %all-to-all-done.refs_0_, bf16[2,2,384,1024]{3,2,1,0:T(8,128)(2,1)} %longitude_table.1.refs_1_.t_any, f32[6144,128]{1,0:T(8,128)} %forward.2.refs_2_), custom_call_target="tpu_custom_call" | custom-call | tf_op jit(solution)/shard_map/forward/pallas_call | solution.py:366
  73.8 8.3 %all-to-all-start.2 = ((bf16[128,48,128]{2,1,0:T(8,128)(2,1)}), bf16[128,48,128]{2,1,0:T(8,128)(2,1)S(1)}, u32[]{:S(2)}, u32[]{:S(2)}) async-start(bf16[128,48,128]{2,1,0:T(8,128)(2,1)} %forward.3), calls=%async_computation.2 | async-start | bytes 3145728 | tf_op jit(solution)/shard_map/all_to_all | solution.py:678
  82.2 15.5 %legendre_tables.1 = (bf16[6,768,512]{2,1,0:T(8,128)(2,1)}, bf16[6,768,512]{2,1,0:T(8,128)(2,1)}) custom-call(f32[4608]{0:T(1024)} %copy-done.4, f32[4608]{0:T(1024)} %mul.186.b_ref, s32[24,128]{1,0:T(8,128)} %broadcast_in_dim.20.m_ref, f32[24,128]{1,0:T(8,128)} %bitcast.52, f32[48,128]{1,0:T(8,128)} %pad_maximum_fusion.2.start_ref, f32[4,128]{1,0:T(4,128)} %fusion.25.w_ref), custom_call_target="tpu_custom_call" | custom-call | tf_op jit(solution)/shard_map/legendre_tables/pallas_call | solution.py:464
  97.6 8.8 %all-to-all-done.2 = bf16[128,48,128]{2,1,0:T(8,128)(2,1)S(1)} async-done(((bf16[128,48,128]{2,1,0:T(8,128)(2,1)}), bf16[128,48,128]{2,1,0:T(8,128)(2,1)S(1)}, u32[]{:S(2)}, u32[]{:S(2)}) %all-to-all-start.2) | async-done | bytes 1572896 | tf_op jit(solution)/shard_map/all_to_all | solution.py:678
  106.5 8.0 %legendre_filter.1 = (f32[6,128,768]{2,1,0:T(8,128)}, bf16[8,16,6,8,128]{4,3,2,1,0:T(8,128)(2,1)}) custom-call(s32[6]{0:T(128)} %reshape.462.slot_ref, s32[6]{0:T(128)} %copy-done.5, bf16[8,16,6,8,128]{4,3,2,1,0:T(8,128)(2,1)S(1)} %bitcast.22, bf16[6,768,512]{2,1,0:T(8,128)(2,1)} %get-tuple-element.37.ana_high.ana_full, ...), custom_call_target="tpu_custom_call" | custom-call | tf_op jit(solution)/shard_map/legendre_filter/pallas_call | solution.py:534
  114.5 29.3 %all_to_all.25.y_ref = bf16[128,48,128]{2,1,0:T(8,128)(2,1)S(1)} all-to-all(bf16[128,48,128]{2,1,0:T(8,128)(2,1)} %bitcast.35), channel_id=1, replica_groups=mesh['lat'=8,'lonr'=16] {'lat','lonr'}, dimensions={0} | all-to-all | bytes 3145728 | tf_op jit(solution)/shard_map/all_to_all | solution.py:684
  143.8 5.3 %inverse.1 = bf16[2,8,4,128,128]{4,3,2,1,0:T(8,128)(2,1)} custom-call(bf16[128,48,128]{2,1,0:T(8,128)(2,1)S(1)} %all_to_all.25.y_ref, bf16[2,2,384,1024]{3,2,1,0:T(8,128)(2,1)} %longitude_table.1.refs_1_.t_any), custom_call_target="tpu_custom_call" | custom-call | tf_op jit(solution)/shard_map/inverse/pallas_call | solution.py:595
  149.1 3.7 %all-to-all-start.4 = ((bf16[16,4,128,128]{3,2,1,0:T(8,128)(2,1)}), bf16[16,4,128,128]{3,2,1,0:T(8,128)(2,1)S(1)}, u32[]{:S(2)}, u32[]{:S(2)}) async-start(bf16[16,4,128,128]{3,2,1,0:T(8,128)(2,1)} %bitcast.32), calls=%async_computation.4 | async-start | bytes 4194304 | tf_op jit(solution)/shard_map/all_to_all | solution.py:688
  152.9 3.9 %tail.1 = (f32[40,128,128]{2,1,0:T(8,128)}, f32[40,128,128]{2,1,0:T(8,128)}) custom-call(f32[10,4,128,128]{3,2,1,0:T(8,128)} %bitcast.25, f32[10,4,128,128]{3,2,1,0:T(8,128)} %bitcast.28, f32[10,4,128,128]{3,2,1,0:T(8,128)} %bitcast.31, f32[10,4,8,128]{3,2,1,0:T(8,128)} %bitcast.41, f32[10,4,8,128]{3,2,1,0:T(8,128)} %bitcast.44, f32[10,4,8,128]{3,2,1,0:T(8,128)} %bitcast.38, ...), custom_call_target="tpu_custom_call" | custom-call | tf_op jit(solution)/shard_map/tail/pallas_call | solution.py:256
  156.7 4.0 %reshape.469 = f32[6,64,2,768]{3,2,1,0:T(2,128)} reshape(f32[6,128,768]{2,1,0:T(8,128)} %get-tuple-element.44) | data formatting | bytes 4718592 | tf_op jit(solution)/shard_map/reshape | solution.py:692
  160.7 21.6 %all-to-all-done.4 = bf16[16,4,128,128]{3,2,1,0:T(8,128)(2,1)S(1)} async-done(((bf16[16,4,128,128]{3,2,1,0:T(8,128)(2,1)}), bf16[16,4,128,128]{3,2,1,0:T(8,128)(2,1)S(1)}, u32[]{:S(2)}, u32[]{:S(2)}) %all-to-all-start.4) | async-done | bytes 2097184 | tf_op jit(solution)/shard_map/all_to_all | solution.py:688
  182.3 4.7 %update.1 = (f32[40,128,128]{2,1,0:T(8,128)}, f32[40,128,128]{2,1,0:T(8,128)}) custom-call(f32[40,128,128]{2,1,0:T(8,128)} %se_ref.1, f32[40,128,128]{2,1,0:T(8,128)} %sp_ref.1, bf16[2,32,128,128]{3,2,1,0:T(8,128)(2,1)S(1)} %bitcast.21, f32[40,128,128]{2,1,0:T(8,128)} %get-tuple-element.40.old_ent, ...), custom_call_target="tpu_custom_call", output_to_operand_aliasing={{0}: (3, {}), {1}: (4, {})} | custom-call | tf_op jit(solution)/shard_map/update/pallas_call | solution.py:625
  (21 shorter events, 0.1 us)
Async XLA Ops:
  0.6 13.7 %copy-start.6 = (s32[768]{0:T(1024)S(1)}, s32[768]{0:T(1024)}, u32[]{:S(2)}) copy-start(s32[768]{0:T(1024)} %param.17) | copy-start | bytes 9220
  6.0 12.4 %collective-permute-start = (f32[40,8,128]{2,1,0:T(8,128)}, f32[40,8,128]{2,1,0:T(8,128)S(1)}, u32[]{:S(2)}, u32[]{:S(2)}) collective-permute-start(f32[40,8,128]{2,1,0:T(8,128)} %get-tuple-element.24), channel_id=1, source_target_pairs={{0,1},{1,2},{2,3},{3,4},{4,5},{5,6},{6,7},{7,8},{8,9},{9,10},{10,1... | collective-permute-start | bytes 491528 | tf_op jit(solution)/shard_map/ppermute | solution.py:655
  7.8 10.6 %collective-permute-start.1 = (f32[40,8,128]{2,1,0:T(8,128)}, f32[40,8,128]{2,1,0:T(8,128)S(1)}, u32[]{:S(2)}, u32[]{:S(2)}) collective-permute-start(f32[40,8,128]{2,1,0:T(8,128)} %get-tuple-element.24), channel_id=1, source_target_pairs={{1,0},{2,1},{3,2},{4,3},{5,4},{6,5},{7,6},{8,7},{9,8},{10,9},{11,1... | collective-permute-start | bytes 491528 | tf_op jit(solution)/shard_map/ppermute | solution.py:656
  11.5 4.3 %collective-permute-start.2 = (f32[40,4,128]{2,1,0:T(4,128)}, f32[40,4,128]{2,1,0:T(4,128)S(1)}, u32[]{:S(2)}, u32[]{:S(2)}) collective-permute-start(f32[40,4,128]{2,1,0:T(4,128)} %get-tuple-element.25), channel_id=1, source_target_pairs={{0,16},{16,32},{32,48},{48,64},{64,80},{80,96},{96,112},{1,17},{17... | collective-permute-start | bytes 245768 | tf_op jit(solution)/shard_map/ppermute | solution.py:657
  13.0 5.4 %collective-permute-start.3 = (f32[40,4,128]{2,1,0:T(4,128)}, f32[40,4,128]{2,1,0:T(4,128)S(1)}, u32[]{:S(2)}, u32[]{:S(2)}) collective-permute-start(f32[40,4,128]{2,1,0:T(4,128)} %get-tuple-element.26), channel_id=1, source_target_pairs={{16,0},{32,16},{48,32},{64,48},{80,64},{96,80},{112,96},{17,1},{33... | collective-permute-start | bytes 245768 | tf_op jit(solution)/shard_map/ppermute | solution.py:658
  15.2 12.7 %copy-start.5 = (s32[6]{0:T(128)}, s32[6]{0:T(128)S(1)}, u32[]{:S(2)}) copy-start(s32[6]{0:T(128)S(1)} %lt.48.ord_ref) | copy-start | bytes 76
  15.8 2.6 %copy-start.2 = (f32[40,4,128]{2,1,0:T(4,128)}, f32[40,4,128]{2,1,0:T(4,128)S(1)}, u32[]{:S(2)}) copy-start(f32[40,4,128]{2,1,0:T(4,128)S(1)} %collective-permute-done.2) | copy-start | bytes 245764
  18.4 0.6 copy-start.3
  18.4 0.7 copy-start
  18.4 0.8 copy-start.1
  23.5 20.4 %all-to-all-start.1 = ((bf16[16,2,128,128]{3,2,1,0:T(8,128)(2,1)}), bf16[16,2,128,128]{3,2,1,0:T(8,128)(2,1)S(1)}, u32[]{:S(2)}, u32[]{:S(2)}) async-start(bf16[16,2,128,128]{3,2,1,0:T(8,128)(2,1)} %bitcast.33), calls=%async_computation.1 | async-start | bytes 2097152 | tf_op jit(solution)/shard_map/all_to_all | solution.py:664
  27.7 8.0 %copy-start.4 = (f32[4608]{0:T(1024)}, f32[4608]{0:T(1024)S(1)}, u32[]{:S(2)}) copy-start(f32[4608]{0:T(1024)S(1)} %reshape.471.a_ref) | copy-start | bytes 55300
  44.0 24.6 %all-to-all-start = ((bf16[16,2,128,128]{3,2,1,0:T(8,128)(2,1)}), bf16[16,2,128,128]{3,2,1,0:T(8,128)(2,1)S(1)}, u32[]{:S(2)}, u32[]{:S(2)}) async-start(bf16[16,2,128,128]{3,2,1,0:T(8,128)(2,1)} %bitcast.34), calls=%async_computation | async-start | bytes 2097152 | tf_op jit(solution)/shard_map/all_to_all | solution.py:664
  73.8 32.6 %all-to-all-start.2 = ((bf16[128,48,128]{2,1,0:T(8,128)(2,1)}), bf16[128,48,128]{2,1,0:T(8,128)(2,1)S(1)}, u32[]{:S(2)}, u32[]{:S(2)}) async-start(bf16[128,48,128]{2,1,0:T(8,128)(2,1)} %forward.3), calls=%async_computation.2 | async-start | bytes 3145728 | tf_op jit(solution)/shard_map/all_to_all | solution.py:678
  149.1 33.2 %all-to-all-start.4 = ((bf16[16,4,128,128]{3,2,1,0:T(8,128)(2,1)}), bf16[16,4,128,128]{3,2,1,0:T(8,128)(2,1)S(1)}, u32[]{:S(2)}, u32[]{:S(2)}) async-start(bf16[16,4,128,128]{3,2,1,0:T(8,128)(2,1)} %bitcast.32), calls=%async_computation.4 | async-start | bytes 4194304 | tf_op jit(solution)/shard_map/all_to_all | solution.py:688
